TPU v7x, 32 devices: a whole 2x2x4 slice. The times are simulated.
32 devices in a mesh: row: 4 (over y, core), col: 4 (over z), feat: 2 (over x).
Axes of the slice: x: 2, y: 2, z: 4, core: 2. Of those that a mesh axis runs over, the one named last changes fastest.
Arguments:
- src_feats: bfloat16 [8192, 256], P(('row', 'col'), 'feat'), may hold values from -170 to 170
- dst_feats: bfloat16 [1024, 256], P(('row', 'col'), 'feat'), may hold values from -170 to 170
- proj: bfloat16 [256, 256], P('feat'), may hold values from -0.375 to 0.375
- att_src: float32 [256], P('feat'), may hold values from -1 to 1
- att_dst: float32 [256], P('feat'), may hold values from -1 to 1
- bias: float32 [256], P('feat'), may hold values from -3 to 3
- tile_rows: int32 [4, 4, 128], P('row', 'col'), may hold values from 0 to 1, as said below
- tile_cols: int32 [4, 4, 128], P('row', 'col'), may hold values from 0 to 15
- tile_count: int32 [4, 4], P('row', 'col'), may hold values from 16 to 128, as said below
- edge_weight: bfloat16 [4, 4, 128, 128, 128], P('row', 'col'), may hold values from 0 to 3, as said below
Outputs:
- node_out: bfloat16 [1024, 256], P(('row', 'col'), 'feat')
Inputs may be any that keep to these rules, and one draw needn't show every extreme that they name: `tile_count`: one device holds exactly 128 live slots in every draw; counts differ several times between devices. `tile_rows`: the slots of one device name distinct tiles as long as there are tiles left in its block, then name the same tiles again in the same order; slots beyond the count also hold valid tile numbers. `edge_weight`: about a third of the entries are edges.
All inputs are finite; a program needn't handle non-finite values.
Results may differ from a plain program's by a relative error of at most 0.001.
Values sent between devices are 32-bit elements; how exact they have to be, the bound alone decides.
No kernel may reach another device: no remote copies, remote signals or barrier semaphores. Data moves between devices by JAX's collectives and lax.ppermute only.
A program may use at most 64 MiB of HBM per device.

v0:
```python
import jax
import jax.numpy as jnp
from jax import lax
from jax.sharding import PartitionSpec as P

HEADS = 8
D = 256
TILE = 128
GROUP = 4


def leaky_relu(values):
    return jnp.where(values > 0, values, 0.2 * values)


def head_sum(projected, vector, dims):
    return (projected * vector).reshape(projected.shape[0], -1, dims).sum(2)


def on_device(
    src_feats,
    dst_feats,
    proj,
    att_src,
    att_dst,
    bias,
    tile_rows,
    tile_cols,
    tile_count,
    edge_weight,
):
    dims = D // HEADS
    src_rows = src_feats.shape[0]
    own_rows = dst_feats.shape[0]
    local_width = proj.shape[1] // lax.axis_size("feat")
    local_heads = local_width // dims
    both_feats = jnp.concatenate([src_feats, dst_feats], axis=0)
    projected = lax.psum_scatter(
        lax.dot_general(
            proj, both_feats, (((0,), (1,)), ((), ())), preferred_element_type=jnp.float32
        ),
        "feat",
        scatter_dimension=0,
        tiled=True,
    ).T
    zsrc = projected[:src_rows]
    zdst = projected[src_rows:]
    s_src = head_sum(zsrc, att_src, dims)
    s_dst = head_sum(zdst, att_dst, dims)
    s_self = head_sum(zdst, att_src, dims)
    z_block, s_block = (
        lax.all_gather(zsrc, "row", axis=0, tiled=True),
        lax.all_gather(s_src, "row", axis=0, tiled=True),
    )
    target = lax.all_gather(s_dst, "col", axis=0, tiled=True)
    col_tiles = z_block.shape[0] // TILE
    row_tiles = target.shape[0] // TILE
    src_tiles = s_block.reshape(col_tiles, TILE, local_heads).transpose(0, 2, 1)
    tgt_tiles = target.reshape(row_tiles, TILE, local_heads).transpose(0, 2, 1)
    z_tiles = z_block.reshape(col_tiles, TILE, local_heads, dims)
    slot_total = tile_rows.shape[2]
    alive = (jnp.arange(slot_total, dtype=jnp.int32) < tile_count[0, 0]).astype(jnp.float32)
    row_ids = tile_rows[0, 0].reshape(-1, GROUP)
    col_ids = tile_cols[0, 0].reshape(-1, GROUP)
    weights = edge_weight[0, 0].reshape(-1, GROUP, TILE, TILE)
    alive_g = alive.reshape(-1, GROUP)

    def masked_scores(row_g, col_g, weight_g, live_g):
        weight_f = weight_g.astype(jnp.float32) * live_g[:, None, None]
        scores = tgt_tiles[row_g][:, :, :, None] + src_tiles[col_g][:, :, None, :]
        return (jnp.where(weight_f[:, None] > 0, leaky_relu(scores), jnp.float32(-1e30)), weight_f)

    def max_step(running, inputs):
        row_g, col_g, weight_g, live_g = inputs
        masked, weight_f = masked_scores(row_g, col_g, weight_g, live_g)
        return (running.at[row_g].max(masked.max(-1)), None)

    start_max = jnp.full((row_tiles, local_heads, TILE), -1e30, jnp.float32)
    row_max, _ = lax.scan(max_step, start_max, (row_ids, col_ids, weights, alive_g))
    row_max = lax.pmax(row_max, "col")

    def sum_step(carry, inputs):
        total, accum = carry
        row_g, col_g, weight_g, live_g = inputs
        masked, weight_f = masked_scores(row_g, col_g, weight_g, live_g)
        probs = weight_f[:, None] * jnp.exp(masked - row_max[row_g][:, :, :, None])
        total = total.at[row_g].add(probs.sum(-1))
        contrib = jnp.einsum(
            "ghij,gjhd->gihd", probs, z_tiles[col_g], precision=lax.Precision.HIGHEST
        )
        return ((total, accum.at[row_g].add(contrib)), None)

    start_sum = (
        jnp.zeros((row_tiles, local_heads, TILE), jnp.float32),
        jnp.zeros((row_tiles, TILE, local_heads, dims), jnp.float32),
    )
    (total, accum), _ = lax.scan(sum_step, start_sum, (row_ids, col_ids, weights, alive_g))
    offset = lax.axis_index("col") * own_rows
    total_rows = total.transpose(0, 2, 1).reshape(-1, local_heads)
    accum_rows = accum.reshape(-1, local_width)
    own_total, own_accum = (
        lax.psum_scatter(total_rows, "col", scatter_dimension=0, tiled=True),
        lax.psum_scatter(accum_rows, "col", scatter_dimension=0, tiled=True),
    )
    own_max = lax.dynamic_slice_in_dim(
        row_max.transpose(0, 2, 1).reshape(-1, local_heads), offset, own_rows, 0
    )
    e_self = leaky_relu(s_dst + s_self)
    final_max = jnp.maximum(own_max, e_self)
    factor = jnp.exp(own_max - final_max)
    self_factor = jnp.exp(e_self - final_max)
    denom = own_total * factor + self_factor
    numer = (
        own_accum.reshape(own_rows, local_heads, dims) * factor[:, :, None]
        + zdst.reshape(own_rows, local_heads, dims) * self_factor[:, :, None]
    )
    mixed = (numer / denom[:, :, None]).reshape(own_rows, local_width) + bias
    return jax.nn.elu(mixed).astype(jnp.bfloat16)


def solution(mesh):
    return jax.shard_map(
        on_device,
        mesh=mesh,
        in_specs=(
            P(("row", "col"), "feat"),
            P(("row", "col"), "feat"),
            P("feat", None),
            P("feat"),
            P("feat"),
            P("feat"),
            P("row", "col", None),
            P("row", "col", None),
            P("row", "col"),
            P("row", "col", None, None, None),
        ),
        out_specs=P(("row", "col"), "feat"),
        check_vma=False,
    )
```

profile of v0, /device:TPU:0, one launch (start us, length us, event | category | flops | bytes accessed | tf_op | source)
XLA Modules:
  0.0 613.5 jit_solution(15043042324582579225)
XLA Ops:
  13.6 14.1 %reduce-scatter.6.cloned.1.call-done = f32[128,576]{0,1:T(8,128)} async-done(((f32[256,576]{0,1:T(8,128)}), f32[128,576]{0,1:T(8,128)}) %reduce-scatter.6.cloned.1.call-update) | async-done | bytes 294928 | tf_op jit(solution)/shard_map/reduce_scatter | solution.py:38
  30.3 12.0 %all-gather = f32[4,64,4]{1,2,0:T(4,128)S(1)} all-gather(f32[1,64,4]{1,2,0:T(4,128)S(1)} %bitcast.122), channel_id=1, replica_groups=mesh['row'=4,'col'=4,'feat'=2] {'col'}, dimensions={0}, use_global_device_ids=true | all-gather | bytes 5120 | tf_op jit(solution)/shard_map/all_gather | solution.py:55
  42.6 5.2 all_gather.10
  47.8 114.2 %while.22 = (s32[]{:T(128)}, f32[2,4,128]{2,1,0:T(4,128)S(1)}, s32[32,4]{1,0:T(8,128)S(1)}, bf16[32,4,128,128]{3,2,1,0:T(8,128)(2,1)}, f32[32,4]{1,0:T(8,128)S(1...) while((s32[]{:T(128)}, f32[2,4,128]{2,1,0:T(4,128)S(1)}, ...), condition=%wide.region_6.7_spmd, body=%wide.region_3.6_spmd.sunk | while | flops 1771546 | bytes 352561 | solution.py:79
  162.0 10.4 %pmax.7 = f32[2,4,128]{2,1,0:T(4,128)S(1)} all-reduce(f32[2,4,128]{2,1,0:T(4,128)S(1)} %get-tuple-element.105), channel_id=1, replica_groups=mesh['row'=4,'col'=4,'feat'=2] {'col'}, use_global_device_ids=true, to_apply=%region_7.8 | all-reduce | flops 1024 | bytes 8192 | tf_op jit(solution)/shard_map/pmax | solution.py:80
  172.5 4.3 reshape.271
  176.8 391.3 %while.23 = (s32[]{:T(128)}, f32[2,4,128]{2,1,0:T(4,128)S(1)}, f32[2,128,4,32]{1,3,2,0:T(8,128)S(1)}, s32[32,4]{1,0:T(8,128)S(1)}, bf16[32,4,128,128]{3,2,1,0:T(...) while((s32[]{:T(128)}, f32[2,4,128]{2,1,0:T(4,128)S(1)}, ...), condition=%wide.region_12.13_spmd, body=%wide.region_8.12_spmd.sunk | while | flops 104990744 | bytes 3219853 | solution.py:97
  182.3 3.4 gather_fusion.5
  194.6 3.4 gather_fusion.5
  206.8 3.4 gather_fusion.5
  219.0 3.4 gather_fusion.5
  231.2 3.4 gather_fusion.5
  243.5 3.4 gather_fusion.5
  255.7 3.4 gather_fusion.5
  267.9 3.4 gather_fusion.5
  280.1 3.4 gather_fusion.5
  292.4 3.4 gather_fusion.5
  304.6 3.4 gather_fusion.5
  316.8 3.4 gather_fusion.5
  329.0 3.4 gather_fusion.5
  341.3 3.4 gather_fusion.5
  353.5 3.4 gather_fusion.5
  365.7 3.4 gather_fusion.5
  378.0 3.4 gather_fusion.5
  390.2 3.4 gather_fusion.5
  402.4 3.4 gather_fusion.5
  414.6 3.4 gather_fusion.5
  426.9 3.4 gather_fusion.5
  463.5 3.4 gather_fusion.5
  549.1 3.4 gather_fusion.5
  569.9 15.8 %reduce-scatter.10.cloned.1.call-done = f32[64,4]{1,0:T(8,128)} async-done(((f32[256,4]{1,0:T(8,128)}), f32[64,4]{1,0:T(8,128)}) %reduce-scatter.10.cloned.1.call-update) | async-done | bytes 1040
  587.0 18.6 %reduce-scatter.8.cloned.1.call-done = f32[64,128]{1,0:T(8,128)} async-done(((f32[256,128]{1,0:T(8,128)}), f32[64,128]{1,0:T(8,128)}) %reduce-scatter.8.cloned.1.call-update) | async-done | bytes 32784 | tf_op jit(solution)/shard_map/reduce_scatter | solution.py:103
  (762 shorter events, 437.4 us)
Async XLA Ops:
  6.5 0.8 copy-start
  6.5 21.2 %reduce-scatter.6.cloned.1.call-start = ((), (), s32[]{:S(2)}) async-start(), calls=%async_computation.3 | async-start | bytes 884736 | tf_op jit(solution)/shard_map/reduce_scatter | solution.py:38
  9.4 163.1 %all-gather.3.cloned.1.call-start = ((), (), s32[]{:S(2)}) async-start(), calls=%async_computation.4 | async-start | bytes 1310720 | tf_op jit(solution)/shard_map/all_gather | solution.py:52
  42.4 543.4 %reduce-scatter.10.cloned.1.call-start = ((), (), s32[]{:S(2)}) async-start(), calls=%async_computation.6 | async-start | bytes 163840
  176.8 428.8 %copy-start.1 = (f32[128]{0:T(128)S(1)}, f32[128]{0:T(128)}, u32[]{:S(2)}) copy-start(f32[128]{0:T(128)} %param.19) | copy-start | bytes 1540
  568.9 36.7 %reduce-scatter.8.cloned.1.call-start = ((), (), s32[]{:S(2)}) async-start(), calls=%async_computation.5 | async-start | bytes 163840 | tf_op jit(solution)/shard_map/reduce_scatter | solution.py:103
Sparse Core Ops, SparseCore 0:
  9.6 18.0 reduce-scatter.5
  42.5 15.3 all-gather.2
  569.0 16.7 reduce-scatter.9
  587.9 17.6 reduce-scatter.7
where the time goes:
time: 617 us; the launch traced here: 613 us
  other arithmetic  226 us (37%)
  local copies, waits for them, and re-layouts  209 us (34%)
  matrix products  83.9 us (14%)
  waiting for transfers between devices  48.6 us (8%)
  blocking collectives  27.6 us (4%)
  between operations  13.9 us (2%)
    gather x32, local copies, waits for them, and re-layouts, sum_step(): z_tiles[col_g]  108 us
    dot_general x32, matrix products, sum_step(): jnp.einsum('ghij,gjhd->gihd', probs, z_tiles[col_g], precision=lax.Precis...  82 us
    gather x128, local copies, waits for them, and re-layouts, masked_scores(): scores = tgt_tiles[row_g][:, :, :, None] + src_tiles[col_g][:, :, None, :]  73.1 us
    gt x64, other arithmetic, masked_scores(): weight_f[:, None] > 0  65.4 us
    reduce_sum x32, other arithmetic, sum_step(): total = total.at[row_g].add(probs.sum(-1))  33.6 us
    mul x32, other arithmetic, masked_scores(): weight_f = weight_g.astype(jnp.float32) * live_g[:, None, None]  31.9 us
    scatter-add x32, other arithmetic, sum_step(): return ((total, accum.at[row_g].add(contrib)), None)  24.2 us
    reduce_max x32, other arithmetic, max_step(): return (running.at[row_g].max(masked.max(-1)), None)  21.2 us
  transfers between devices with their start and end apart: 4, of which 3 were waited for; matrix products, arithmetic and copies ran while one was open for 19% of the time, Pallas kernels for 0%

commit v1 on v0

v1 whole, which is shorter than its diff:
```python
import jax
import jax.numpy as jnp
from jax import lax
from jax.experimental import pallas as pl
from jax.experimental.pallas import tpu as pltpu
from jax.sharding import PartitionSpec as P

HEADS = 8
TILE = 128
SLOPE = 0.2
LOG2E = 1.4426950408889634
NEG = -1e30
F32 = jnp.float32
BF16 = jnp.bfloat16
HIGHEST = lax.Precision.HIGHEST
VMEM = pl.BlockSpec(memory_space=pltpu.VMEM)
SMEM = pl.BlockSpec(memory_space=pltpu.SMEM)


def is_pow2(n):
    return n & (n - 1) == 0


def goes_to(i, d, n):
    return i ^ d if is_pow2(n) else lax.rem(i + d, n)


def comes_from(i, d, n):
    return i ^ d if is_pow2(n) else lax.rem(i + n - d, n)


def hop(x, axis, d):
    n = lax.axis_size(axis)
    pairs = [(i, i ^ d if is_pow2(n) else (i + d) % n) for i in range(n)]
    return lax.ppermute(x, axis, pairs)


def call(kernel, out_shape, *args, in_specs=None, flops=0, bytes_accessed=0, **kw):
    return pl.pallas_call(
        kernel,
        out_shape=out_shape,
        in_specs=in_specs or [VMEM] * len(args),
        cost_estimate=pl.CostEstimate(
            flops=flops, bytes_accessed=bytes_accessed, transcendentals=0
        ),
        **kw,
    )(*args)


def up8(n):
    return -(-n // 8) * 8


def head_rows(vector, heads, width):
    dims = width // heads
    shape = (up8(heads), width)
    row = lax.broadcasted_iota(jnp.int32, shape, 0)
    lane = lax.broadcasted_iota(jnp.int32, shape, 1)
    return jnp.where(lane // dims == row, jnp.broadcast_to(vector, shape), 0.0)


def contract(lhs, rhs, dims, precision=HIGHEST):
    return lax.dot_general(
        lhs, rhs, (dims, ((), ())), preferred_element_type=F32, precision=precision
    )


def take_cols(proj_ref, which, width):
    if width % TILE == 0:
        return proj_ref[:, pl.ds(pl.multiple_of(which * width, width), width)]
    full = proj_ref[...]
    out = full[:, :width]
    for k in range(1, full.shape[1] // width):
        out = jnp.where(which == k, full[:, k * width : (k + 1) * width], out)
    return out


def project(x, w):
    return lax.dot_general(x, w, (((1,), (0,)), ((), ())), preferred_element_type=F32)


def leaky(x):
    return jnp.maximum(x, SLOPE * x)


def on_device(
    src_feats, dst_feats, proj, att_src, att_dst, bias, tile_rows, tile_cols, tile_count, edge_weight
):
    n_row, n_col, n_feat = (lax.axis_size(a) for a in ("row", "col", "feat"))
    width = proj.shape[1] // n_feat
    heads = HEADS // n_feat
    dims = width // heads
    lanes = -(-width // TILE) * TILE
    src_rows, own_rows = src_feats.shape[0], dst_feats.shape[0]
    slots = tile_rows.shape[2]
    row_tiles = own_rows * n_col // TILE
    piece_tiles = src_rows // TILE
    col_tiles = piece_tiles * n_row
    per_tile = TILE // own_rows
    hp = up8(heads)
    mdp = up8(2 * heads)
    att_src2, att_dst2, bias2 = (v.reshape(1, width) for v in (att_src, att_dst, bias))

    def send_kernel(dst_ref, src_ref, proj_ref, *outs):
        me = lax.axis_index("feat")
        for d in range(1, n_feat):
            w = take_cols(proj_ref, goes_to(me, d, n_feat), width)
            outs[2 * d - 2][...] = project(dst_ref[...], w)
            outs[2 * d - 1][...] = project(src_ref[...], w)

    sent = call(
        send_kernel,
        [
            jax.ShapeDtypeStruct((n, width), F32)
            for _ in range(1, n_feat)
            for n in (own_rows, src_rows)
        ],
        dst_feats,
        src_feats,
        proj,
    )
    dst_parts = [hop(sent[2 * d - 2], "feat", d) for d in range(1, n_feat)]
    src_parts = [hop(sent[2 * d - 1], "feat", d) for d in range(1, n_feat)]

    group = 16

    def weight_kernel(rows_ref, cols_ref, count_ref, w_ref, panel_ref):
        step = pl.program_id(0)

        @pl.when(step == 0)
        def _():
            @pl.loop(0, row_tiles * col_tiles)
            def _(t):
                panel_ref[t // col_tiles, t % col_tiles] = jnp.zeros((TILE, TILE), F32)

        base = step * group
        live = jnp.clip(count_ref[0, 0] - base, 0, group)

        @pl.loop(0, live)
        def _(t):
            r, c = rows_ref[0, 0, base + t], cols_ref[0, 0, base + t]
            panel_ref[r, c] = panel_ref[r, c] + w_ref[0, 0, t].astype(F32)

    panel = pl.pallas_call(
        weight_kernel,
        out_shape=jax.ShapeDtypeStruct((row_tiles, col_tiles, TILE, TILE), F32),
        grid=(slots // group,),
        in_specs=[
            SMEM,
            SMEM,
            SMEM,
            pl.BlockSpec((1, 1, group, TILE, TILE), lambda s: (0, 0, s, 0, 0)),
        ],
        out_specs=pl.BlockSpec(
            (row_tiles, col_tiles, TILE, TILE), lambda s: (0, 0, 0, 0)
        ),
        cost_estimate=pl.CostEstimate(
            flops=slots * TILE * TILE, bytes_accessed=slots * TILE * TILE * 2, transcendentals=0
        ),
    )(tile_rows, tile_cols, tile_count, edge_weight)

    def dst_kernel(dst_ref, proj_ref, att_ref, *rest):
        parts, (z_ref, s_ref) = rest[: n_feat - 1], rest[n_feat - 1 :]
        z = project(dst_ref[...], take_cols(proj_ref, lax.axis_index("feat"), width))
        for part in parts:
            z = z + part[...]
        z_ref[...] = z
        s_ref[...] = LOG2E * contract(head_rows(att_ref[...], heads, width), z, ((1,), (1,)))

    zdst, s_dst = call(
        dst_kernel,
        [
            jax.ShapeDtypeStruct((own_rows, width), F32),
            jax.ShapeDtypeStruct((hp, own_rows), F32),
        ],
        dst_feats,
        proj,
        att_dst2,
        *dst_parts,
    )
    targets = [s_dst] + [hop(s_dst, "col", d) for d in range(1, n_col)]

    pack_rows = src_rows + piece_tiles * hp

    def src_kernel(src_ref, proj_ref, att_ref, *rest):
        parts, out_ref = rest[: n_feat - 1], rest[n_feat - 1]
        z = project(src_ref[...], take_cols(proj_ref, lax.axis_index("feat"), width))
        for part in parts:
            z = z + part[...]
        if width < lanes:
            out_ref[...] = jnp.zeros_like(out_ref)
        out_ref[:src_rows, :width] = z
        s = LOG2E * contract(head_rows(att_ref[...], heads, width), z, ((1,), (1,)))
        for t in range(piece_tiles):
            at = src_rows + t * hp
            out_ref[at : at + hp, :TILE] = s[:, t * TILE : (t + 1) * TILE]

    own_piece = call(
        src_kernel,
        jax.ShapeDtypeStruct((pack_rows, lanes), F32),
        src_feats,
        proj,
        att_src2,
        *src_parts,
    )
    pieces = {0: own_piece}
    d = n_row // 2
    while d:
        for k in list(pieces):
            pieces[k ^ d] = hop(pieces[k], "row", d)
        d //= 2
    pieces = [pieces[k] for k in range(n_row)]

    block = 32
    chunk_rows = own_rows + mdp

    def att_kernel(*refs):
        tgt_refs, refs = refs[:n_col], refs[n_col:]
        piece_refs, refs = refs[:n_row], refs[n_row:]
        w_ref, refs = refs[0], refs[1:]
        out_refs, (tgt, z_cat, probs, den_s, m_s, done) = refs[:n_col], refs[n_col:]
        rt = pl.program_id(0)
        row, col = lax.axis_index("row"), lax.axis_index("col")

        @pl.when(rt == 0)
        def _():
            eye = (
                lax.broadcasted_iota(jnp.int32, (hp, TILE), 0)
                == lax.broadcasted_iota(jnp.int32, (hp, TILE), 1)
            ).astype(F32)
            for d in range(n_col):
                at = pl.multiple_of(comes_from(col, d, n_col) * own_rows, own_rows)
                tgt[pl.ds(at, own_rows), :] = contract(tgt_refs[d][...], eye, ((0,), (0,)))
            for k in range(n_row):
                z = piece_refs[k][:src_rows, :width]
                hi = z.astype(BF16)
                z_cat[k * src_rows : (k + 1) * src_rows, :width] = hi
                z_cat[k * src_rows : (k + 1) * src_rows, width:] = (z - hi.astype(F32)).astype(BF16)

        def score_row(q, h):
            k, t = divmod(q, piece_tiles)
            at = src_rows + t * hp + h
            return piece_refs[k][at : at + 1, :TILE]

        def weight(q, i0):
            k, t = divmod(q, piece_tiles)
            return w_ref[0, (row ^ k) * piece_tiles + t, pl.ds(i0, block), :]

        @pl.loop(0, TILE // block)
        def _(step):
            i0 = pl.multiple_of(step * block, block)
            best = [jnp.full((block, TILE), NEG, F32) for _ in range(heads)]
            for q in range(col_tiles):
                edge = weight(q, i0) > 0
                for h in range(heads):
                    b = jnp.broadcast_to(score_row(q, h), (block, TILE))
                    best[h] = jnp.maximum(best[h], jnp.where(edge, b, NEG))
            t_at = pl.multiple_of(rt * TILE + i0, block)
            t_all = tgt[pl.ds(t_at, block), :]
            for h in range(heads):
                a = t_all[:, h : h + 1]
                m = leaky(a + jnp.max(best[h], axis=1, keepdims=True))
                pos = jnp.broadcast_to(a - m, (block, TILE))
                neg = jnp.broadcast_to(SLOPE * a - m, (block, TILE))
                den = jnp.zeros((block, TILE), F32)
                for q in range(col_tiles):
                    b = score_row(q, h)
                    x = jnp.maximum(pos + b, neg + SLOPE * b)
                    p = weight(q, i0) * jnp.exp2(jnp.minimum(x, 0.0))
                    den = den + p
                    hi = p.astype(BF16)
                    at = 2 * h * TILE + i0
                    probs[pl.ds(pl.multiple_of(at, block), block), q * TILE : (q + 1) * TILE] = hi
                    lo = (p - hi.astype(F32)).astype(BF16)
                    probs[
                        pl.ds(pl.multiple_of(at + TILE, block), block), q * TILE : (q + 1) * TILE
                    ] = lo
                den_s[h, pl.ds(i0, block), :] = jnp.broadcast_to(
                    jnp.sum(den, axis=1, keepdims=True), (block, TILE)
                )
                m_s[h, pl.ds(i0, block), :] = jnp.broadcast_to(m, (block, TILE))

        both = lax.dot_general(
            probs[...], z_cat[...], (((1,), (0,)), ((), ())), preferred_element_type=F32
        )
        lane_w = lax.broadcasted_iota(jnp.int32, (TILE, width), 1) // dims
        lane_t = lax.broadcasted_iota(jnp.int32, (TILE, TILE), 1)
        num = jnp.zeros((TILE, width), F32)
        md = jnp.zeros((TILE, TILE), F32)
        for h in range(heads):
            hi = both[2 * h * TILE : (2 * h + 1) * TILE]
            lo = both[(2 * h + 1) * TILE : (2 * h + 2) * TILE]
            mine = hi[:, :width] + (hi[:, width:] + lo[:, :width])
            num = jnp.where(lane_w == h, mine, num)
            md = jnp.where(lane_t == h, den_s[h], md)
            md = jnp.where(lane_t == heads + h, m_s[h], md)
        md = md.T
        for k in range(per_tile):
            done[rt * per_tile + k, :own_rows, :width] = num[k * own_rows : (k + 1) * own_rows]
            done[rt * per_tile + k, own_rows:, :own_rows] = md[
                :mdp, k * own_rows : (k + 1) * own_rows
            ]

        @pl.when(rt == row_tiles - 1)
        def _():
            for d in range(n_col):
                out_refs[d][...] = done[goes_to(col, d, n_col)]

    full = lambda shape: pl.BlockSpec(shape, lambda s: (0,) * len(shape))
    chunk = jax.ShapeDtypeStruct((chunk_rows, lanes), F32)
    k_all = n_row * src_rows
    chunks = pl.pallas_call(
        att_kernel,
        out_shape=[chunk] * n_col,
        grid=(row_tiles,),
        in_specs=[full((hp, own_rows))] * n_col
        + [full((pack_rows, lanes))] * n_row
        + [pl.BlockSpec((1, col_tiles, TILE, TILE), lambda s: (s, 0, 0, 0))],
        out_specs=[full((chunk_rows, lanes))] * n_col,
        scratch_shapes=[
            pltpu.VMEM((row_tiles * TILE, TILE), F32),
            pltpu.VMEM((k_all, 2 * width), BF16),
            pltpu.VMEM((2 * heads * TILE, k_all), BF16),
            pltpu.VMEM((heads, TILE, TILE), F32),
            pltpu.VMEM((heads, TILE, TILE), F32),
            pltpu.VMEM((n_col, chunk_rows, lanes), F32),
        ],
        cost_estimate=pl.CostEstimate(
            flops=row_tiles * TILE * k_all * width * heads * 8,
            bytes_accessed=k_all * width * 4,
            transcendentals=row_tiles * TILE * k_all * heads,
        ),
    )(*targets, *pieces, panel)
    gathered = [chunks[0]] + [hop(chunks[d], "col", d) for d in range(1, n_col)]

    def out_kernel(zdst_ref, src_ref, dst_ref, bias_ref, *rest):
        parts, out_ref = rest[:n_col], rest[n_col]
        same = (
            lax.broadcasted_iota(jnp.int32, (width, width), 0) // dims
            == lax.broadcasted_iota(jnp.int32, (width, width), 1) // dims
        ).astype(F32)
        z = zdst_ref[...]
        pair = contract(z * (dst_ref[...] + src_ref[...]), same, ((1,), (0,)))
        e_self = leaky(LOG2E * pair)
        which = lax.broadcasted_iota(jnp.int32, (mdp, width), 0)
        head = lax.broadcasted_iota(jnp.int32, (mdp, width), 1) // dims
        den_of, m_of = (which == head).astype(F32), (which == head + heads).astype(F32)
        mds = [part[own_rows:, :own_rows] for part in parts]
        ms = [contract(md, m_of, ((0,), (0,))) for md in mds]
        dens = [contract(md, den_of, ((0,), (0,))) for md in mds]
        top = e_self
        for m in ms:
            top = jnp.maximum(top, m)
        den = jnp.exp2(e_self - top)
        num = den * z
        for part, m, own_den in zip(parts, ms, dens):
            factor = jnp.exp2(m - top)
            den = den + factor * own_den
            num = num + factor * part[:own_rows, :width]
        x = num / den + bias_ref[...]
        out_ref[...] = jnp.where(x > 0, x, jnp.exp(jnp.minimum(x, 0.0)) - 1.0).astype(BF16)

    return call(
        out_kernel,
        jax.ShapeDtypeStruct((own_rows, width), BF16),
        zdst,
        att_src2,
        att_dst2,
        bias2,
        *gathered,
    )


def solution(mesh):
    return jax.shard_map(
        on_device,
        mesh=mesh,
        in_specs=(
            P(("row", "col"), "feat"),
            P(("row", "col"), "feat"),
            P("feat", None),
            P("feat"),
            P("feat"),
            P("feat"),
            P("row", "col", None),
            P("row", "col", None),
            P("row", "col"),
            P("row", "col", None, None, None),
        ),
        out_specs=P(("row", "col"), "feat"),
        check_vma=False,
    )
```

time: 617 us -> 66.3 us (0.11)
  other arithmetic: 226 us -> 0 us
  local copies, waits for them, and re-layouts: 209 us -> 3.36 us
  matrix products: 83.9 us -> 0 us
  waiting for transfers between devices: 48.6 us -> 20.5 us
  blocking collectives: 27.6 us -> 0 us
  Pallas kernels: 0 us -> 26.3 us
  starting transfers between devices: 0.13 us -> 15 us
  between operations: 13.9 us -> 0.73 us
    gather x192 -> x0, local copies, waits for them, and re-layouts: 199 us -> none  [the longest x32 108 us: sum_step(): z_tiles[col_g]]
    dot_general x33 -> x0, matrix products: 83.9 us -> none  [the longest x32 82 us: sum_step(): jnp.einsum('ghij,gjhd->gihd', probs, z_tiles[col_g], precision=lax.Precis...]
    gt x64 -> x0, other arithmetic: 65.4 us -> none  [masked_scores(): weight_f[:, None] > 0]
    scatter-add x64 -> x0, other arithmetic: 44.9 us -> none  [the longest x32 24.2 us: sum_step(): return ((total, accum.at[row_g].add(contrib)), None)]
    reduce_sum x35 -> x0, other arithmetic: 33.7 us -> none  [the longest x32 33.6 us: sum_step(): total = total.at[row_g].add(probs.sum(-1))]
    reduce_scatter x2 -> x0, waiting for transfers between devices: 32.7 us -> none  [the longest x1 18.6 us: on_device(): lax.psum_scatter(accum_rows, 'col', scatter_dimension=0, tiled=True)]
    mul x33 -> x0, other arithmetic: 32.7 us -> none  [the longest x32 31.9 us: masked_scores(): weight_f = weight_g.astype(jnp.float32) * live_g[:, None, None]]
    pallas_call x0 -> x6, Pallas kernels: none -> 26.3 us  [the longest x1 11.4 us: on_device(): pl.pallas_call(att_kernel, out_shape=[chunk] * n_col, grid=(row_tiles,),...]
  transfers between devices with their start and end apart: 4 -> 11, of which waited for: 3 -> 5; matrix products, arithmetic and copies ran while one was open for 19% -> 0% of each run, Pallas kernels for 0% -> 13%
where the time goes in v1:
time: 66.3 us; the launch traced here: 65.9 us
  Pallas kernels  26.3 us (40%)
  waiting for transfers between devices  20.5 us (31%)
  starting transfers between devices  15 us (23%)
  local copies, waits for them, and re-layouts  3.36 us (5%)
  between operations  0.73 us (1%)
    ppermute x11, waiting for transfers between devices, hop(): return lax.ppermute(x, axis, pairs)  20.5 us
    ppermute x11, starting transfers between devices, hop(): return lax.ppermute(x, axis, pairs)  15 us
    pallas_call x1, Pallas kernels, on_device(): pl.pallas_call(att_kernel, out_shape=[chunk] * n_col, grid=(row_tiles,),...  11.4 us
    pallas_call x4, Pallas kernels, call(): pl.pallas_call(kernel, out_shape=out_shape, in_specs=in_specs or [VMEM] *...  7.81 us
    pallas_call x1, Pallas kernels, on_device(): pl.pallas_call(weight_kernel, out_shape=jax.ShapeDtypeStruct((row_tiles,...  7.12 us
    unnamed x22, local copies, waits for them, and re-layouts  3.36 us
  transfers between devices with their start and end apart: 11, of which 5 were waited for; matrix products, arithmetic and copies ran while one was open for 0% of the time, Pallas kernels for 13%

profile of v1, /device:TPU:0, one launch (start us, length us, event | category | flops | bytes accessed | tf_op | source)
XLA Modules:
  0.0 65.9 jit_solution(3177096087963562950)
XLA Ops:
  0.0 1.8 %shard_map.100 = (f32[64,128]{1,0:T(8,128)}, f32[512,128]{1,0:T(8,128)}) custom-call(bf16[64,128]{1,0:T(8,128)(2,1)} %dst_ref.3, bf16[512,128]{1,0:T(8,128)(2,1)} %src_ref.3, bf16[128,256]{1,0:T(8,128)(2,1)} %proj_ref.5), custom_call_target="tpu_custom_call" | custom-call | tf_op jit(solution)/shard_map/pallas_call | solution.py:39
  1.8 3.0 %collective-permute-start.4 = (f32[512,128]{1,0:T(8,128)}, f32[512,128]{1,0:T(8,128)S(1)}, u32[]{:S(2)}, u32[]{:S(2)}) collective-permute-start(f32[512,128]{1,0:T(8,128)} %get-tuple-element.16), channel_id=1, source_target_pairs={{0,1},{1,0},{2,3},{3,2},{4,5},{5,4},{6,7},{7,6},{8,9},{9,8},{10,11... | collective-permute-start | bytes 786440 | tf_op jit(solution)/shard_map/ppermute | solution.py:35
  4.8 6.5 %collective-permute-done.4.rest_0_ = f32[512,128]{1,0:T(8,128)S(1)} collective-permute-done((f32[512,128]{1,0:T(8,128)}, f32[512,128]{1,0:T(8,128)S(1)}, u32[]{:S(2)}, u32[]{:S(2)}) %collective-permute-start.4) | collective-permute-done | bytes 262176 | tf_op jit(solution)/shard_map/ppermute | solution.py:35
  11.3 0.7 %copy-done = f32[512,128]{1,0:T(8,128)} copy-done((f32[512,128]{1,0:T(8,128)}, f32[512,128]{1,0:T(8,128)S(1)}, u32[]{:S(2)}) %copy-start) | copy-done | bytes 262168
  12.0 2.3 %shard_map.102.refs_4_ = f32[544,128]{1,0:T(8,128)} custom-call(bf16[512,128]{1,0:T(8,128)(2,1)} %src_ref.3, bf16[128,256]{1,0:T(8,128)(2,1)} %proj_ref.5, f32[1,128]{1,0:T(1,128)} %bitcast.5, f32[512,128]{1,0:T(8,128)} %copy-done), custom_call_target="tpu_custom_call" | custom-call | tf_op jit(solution)/shard_map/pallas_call | solution.py:39
  14.3 1.8 %collective-permute-start.6 = (f32[544,128]{1,0:T(8,128)}, f32[544,128]{1,0:T(8,128)S(1)}, u32[]{:S(2)}, u32[]{:S(2)}) collective-permute-start(f32[544,128]{1,0:T(8,128)} %shard_map.102.refs_4_), channel_id=1, source_target_pairs={{0,16},{8,24},{16,0},{24,8},{1,17},{9,25},{17,1},{25,9},{2,18},{10... | collective-permute-start | bytes 835592 | tf_op jit(solution)/shard_map/ppermute | solution.py:35
  16.1 0.0 collective-permute-start.5
  16.1 6.3 %collective-permute-done.6.refs_6_ = f32[544,128]{1,0:T(8,128)S(1)} collective-permute-done((f32[544,128]{1,0:T(8,128)}, f32[544,128]{1,0:T(8,128)S(1)}, u32[]{:S(2)}, u32[]{:S(2)}) %collective-permute-start.6) | collective-permute-done | bytes 278560 | tf_op jit(solution)/shard_map/ppermute | solution.py:35
  22.3 0.0 collective-permute-start.7
  22.3 1.5 %collective-permute-start = (f32[64,128]{1,0:T(8,128)}, f32[64,128]{1,0:T(8,128)S(1)}, u32[]{:S(2)}, u32[]{:S(2)}) collective-permute-start(f32[64,128]{1,0:T(8,128)} %get-tuple-element.13), channel_id=1, source_target_pairs={{0,1},{1,0},{2,3},{3,2},{4,5},{5,4},{6,7},{7,6},{8,9},{9,8},{10,11... | collective-permute-start | bytes 98312 | tf_op jit(solution)/shard_map/ppermute | solution.py:35
  23.8 2.7 %collective-permute-done.rest_0_ = f32[64,128]{1,0:T(8,128)S(1)} collective-permute-done((f32[64,128]{1,0:T(8,128)}, f32[64,128]{1,0:T(8,128)S(1)}, u32[]{:S(2)}, u32[]{:S(2)}) %collective-permute-start) | collective-permute-done | bytes 32800 | tf_op jit(solution)/shard_map/ppermute | solution.py:35
  26.4 0.6 copy-done.4
  27.1 1.8 %shard_map.101 = (f32[64,128]{1,0:T(8,128)}, f32[8,64]{1,0:T(8,128)}) custom-call(bf16[64,128]{1,0:T(8,128)(2,1)} %dst_ref.3, bf16[128,256]{1,0:T(8,128)(2,1)} %proj_ref.5, f32[1,128]{1,0:T(1,128)} %bitcast.3, f32[64,128]{1,0:T(8,128)} %copy-done.4), custom_call_target="tpu_custom_call" | custom-call | tf_op jit(solution)/shard_map/pallas_call | solution.py:39
  28.8 3.6 %collective-permute-start.3 = (f32[8,64]{1,0:T(8,128)}, f32[8,64]{1,0:T(8,128)S(1)}, u32[]{:S(2)}, u32[]{:S(2)}) collective-permute-start(f32[8,64]{1,0:T(8,128)} %get-tuple-element.15.refs_0_), channel_id=1, source_target_pairs={{0,6},{2,4},{4,2},{6,0},{1,7},{3,5},{5,3},{7,1},{8,14},{10,12},{12... | collective-permute-start | bytes 6152 | tf_op jit(solution)/shard_map/ppermute | solution.py:35
  32.4 0.0 collective-permute-start.2
  32.4 0.8 %collective-permute-start.1 = (f32[8,64]{1,0:T(8,128)}, f32[8,64]{1,0:T(8,128)S(1)}, u32[]{:S(2)}, u32[]{:S(2)}) collective-permute-start(f32[8,64]{1,0:T(8,128)} %get-tuple-element.15.refs_0_), channel_id=1, source_target_pairs={{0,2},{2,0},{4,6},{6,4},{1,3},{3,1},{5,7},{7,5},{8,10},{10,8},{12,... | collective-permute-start | bytes 6152 | tf_op jit(solution)/shard_map/ppermute | solution.py:35
  33.9 7.1 %shard_map.103.refs_8_ = f32[2,16,128,128]{3,2,1,0:T(8,128)} custom-call(s32[1,1,128]{2,1,0:T(1,128)} %rows_ref.1, s32[1,1,128]{2,1,0:T(1,128)} %cols_ref.1, s32[1,1]{1,0:T(1,128)S(6)} %copy.11.count_ref, bf16[1,1,128,128,128]{4,3,2,1,0:T(8,128)(2,1)} %w_ref.1), custom_call_target="tpu_custom_call" | custom-call | flops 2097152 | bytes 4194304 | tf_op jit(solution)/shard_map/pallas_call | solution.py:144
  41.0 0.0 collective-permute-done.1.refs_1_
  41.0 0.0 collective-permute-done.7.refs_7_
  41.1 0.5 copy-done.8
  41.6 0.0 copy-done.9
  41.6 0.0 copy-done.10
  41.6 0.2 copy-done.6
  41.8 0.7 %copy-done.7 = f32[544,128]{1,0:T(8,128)} copy-done((f32[544,128]{1,0:T(8,128)}, f32[544,128]{1,0:T(8,128)S(1)}, u32[]{:S(2)}) %copy-start.7) | copy-done | bytes 278552
  42.5 11.4 %shard_map.104 = (f32[72,128]{1,0:T(8,128)}, f32[72,128]{1,0:T(8,128)}, f32[72,128]{1,0:T(8,128)}, f32[72,128]{1,0:T(8,128)}) custom-call(f32[8,64]{1,0:T(8,128)} %get-tuple-element.15.refs_0_, f32[8,64]{1,0:T(8,128)} %copy-done.10, f32[8,64]{1,0:T(8,128)} %copy-done.9, f32[8,64]{1,0:T(8,128)} %copy-done.8, f32[544,128]{1,0:T(8,128)} %shard_map.102.refs_4_, ...), custom_call_target="tpu_custom_call" | custom-call | flops 2147483648 | bytes 1048576 | tf_op jit(solution)/shard_map/pallas_call | solution.py:312
  53.8 0.6 collective-permute-start.8
  54.4 2.9 %collective-permute-start.9 = (f32[72,128]{1,0:T(8,128)}, f32[72,128]{1,0:T(8,128)S(1)}, u32[]{:S(2)}, u32[]{:S(2)}) collective-permute-start(f32[72,128]{1,0:T(8,128)} %get-tuple-element.19), channel_id=1, source_target_pairs={{0,4},{2,6},{4,0},{6,2},{1,5},{3,7},{5,1},{7,3},{8,12},{10,14},{12... | collective-permute-start | bytes 110600 | tf_op jit(solution)/shard_map/ppermute | solution.py:35
  57.4 0.9 %collective-permute-start.10 = (f32[72,128]{1,0:T(8,128)}, f32[72,128]{1,0:T(8,128)S(1)}, u32[]{:S(2)}, u32[]{:S(2)}) collective-permute-start(f32[72,128]{1,0:T(8,128)} %get-tuple-element.20), channel_id=1, source_target_pairs={{0,6},{2,4},{4,2},{6,0},{1,7},{3,5},{5,3},{7,1},{8,14},{10,12},{12... | collective-permute-start | bytes 110600 | tf_op jit(solution)/shard_map/ppermute | solution.py:35
  58.3 1.2 %collective-permute-done.9.rest_2_ = f32[72,128]{1,0:T(8,128)S(1)} collective-permute-done((f32[72,128]{1,0:T(8,128)}, f32[72,128]{1,0:T(8,128)S(1)}, u32[]{:S(2)}, u32[]{:S(2)}) %collective-permute-start.9) | collective-permute-done | bytes 36896 | tf_op jit(solution)/shard_map/ppermute | solution.py:35
  59.5 3.8 %collective-permute-done.10.rest_3_ = f32[72,128]{1,0:T(8,128)S(1)} collective-permute-done((f32[72,128]{1,0:T(8,128)}, f32[72,128]{1,0:T(8,128)S(1)}, u32[]{:S(2)}, u32[]{:S(2)}) %collective-permute-start.10) | collective-permute-done | bytes 36896 | tf_op jit(solution)/shard_map/ppermute | solution.py:35
  63.3 0.6 copy-done.3
  63.9 2.0 %shard_map.105 = bf16[64,128]{1,0:T(8,128)(2,1)} custom-call(f32[64,128]{1,0:T(8,128)} %get-tuple-element.14.zdst_ref, f32[1,128]{1,0:T(1,128)} %bitcast.6, f32[1,128]{1,0:T(1,128)} %bitcast.4, f32[1,128]{1,0:T(1,128)} %bitcast.7, f32[72,128]{1,0:T(8,128)} %get-tuple-element.17.rest_0_, f32[72,128]{1,0:T(8,128)} %copy-done.1, f32[72,128]{1,0:T(8,128)} %copy-done.2, ...), custom_call_target="tpu_custom_call" | custom-call | tf_op jit(solution)/shard_map/pallas_call | solution.py:39
  (18 shorter events, 0.0 us)
Async XLA Ops:
  1.8 9.5 %collective-permute-start.4 = (f32[512,128]{1,0:T(8,128)}, f32[512,128]{1,0:T(8,128)S(1)}, u32[]{:S(2)}, u32[]{:S(2)}) collective-permute-start(f32[512,128]{1,0:T(8,128)} %get-tuple-element.16), channel_id=1, source_target_pairs={{0,1},{1,0},{2,3},{3,2},{4,5},{5,4},{6,7},{7,6},{8,9},{9,8},{10,11... | collective-permute-start | bytes 786440 | tf_op jit(solution)/shard_map/ppermute | solution.py:35
  11.3 0.7 %copy-start = (f32[512,128]{1,0:T(8,128)}, f32[512,128]{1,0:T(8,128)S(1)}, u32[]{:S(2)}) copy-start(f32[512,128]{1,0:T(8,128)S(1)} %collective-permute-done.4.rest_0_) | copy-start | bytes 786436
  14.3 8.0 %collective-permute-start.6 = (f32[544,128]{1,0:T(8,128)}, f32[544,128]{1,0:T(8,128)S(1)}, u32[]{:S(2)}, u32[]{:S(2)}) collective-permute-start(f32[544,128]{1,0:T(8,128)} %shard_map.102.refs_4_), channel_id=1, source_target_pairs={{0,16},{8,24},{16,0},{24,8},{1,17},{9,25},{17,1},{25,9},{2,18},{10... | collective-permute-start | bytes 835592 | tf_op jit(solution)/shard_map/ppermute | solution.py:35
  16.1 25.0 %collective-permute-start.5 = (f32[544,128]{1,0:T(8,128)}, f32[544,128]{1,0:T(8,128)S(1)}, u32[]{:S(2)}, u32[]{:S(2)}) collective-permute-start(f32[544,128]{1,0:T(8,128)} %shard_map.102.refs_4_), channel_id=1, source_target_pairs={{0,8},{8,0},{16,24},{24,16},{1,9},{9,1},{17,25},{25,17},{2,10},{10... | collective-permute-start | bytes 835592 | tf_op jit(solution)/shard_map/ppermute | solution.py:35
  22.3 18.7 %copy-start.5 = (f32[544,128]{1,0:T(8,128)}, f32[544,128]{1,0:T(8,128)S(1)}, u32[]{:S(2)}) copy-start(f32[544,128]{1,0:T(8,128)S(1)} %collective-permute-done.6.refs_6_) | copy-start | bytes 835588
  22.3 18.7 %collective-permute-start.7 = (f32[544,128]{1,0:T(8,128)S(1)}, f32[544,128]{1,0:T(8,128)S(1)}, u32[]{:S(2)}, u32[]{:S(2)}) collective-permute-start(f32[544,128]{1,0:T(8,128)S(1)} %collective-permute-done.6.refs_6_), channel_id=1, source_target_pairs={{0,8},{8,0},{16,24},{24,16},{1,9},{9,1},{17,25},{25,17},{2,10},{10... | collective-permute-start | bytes 835592 | tf_op jit(solution)/shard_map/ppermute | solution.py:35
  22.3 4.1 %collective-permute-start = (f32[64,128]{1,0:T(8,128)}, f32[64,128]{1,0:T(8,128)S(1)}, u32[]{:S(2)}, u32[]{:S(2)}) collective-permute-start(f32[64,128]{1,0:T(8,128)} %get-tuple-element.13), channel_id=1, source_target_pairs={{0,1},{1,0},{2,3},{3,2},{4,5},{5,4},{6,7},{7,6},{8,9},{9,8},{10,11... | collective-permute-start | bytes 98312 | tf_op jit(solution)/shard_map/ppermute | solution.py:35
  26.4 0.6 copy-start.4
  28.8 12.2 %collective-permute-start.3 = (f32[8,64]{1,0:T(8,128)}, f32[8,64]{1,0:T(8,128)S(1)}, u32[]{:S(2)}, u32[]{:S(2)}) collective-permute-start(f32[8,64]{1,0:T(8,128)} %get-tuple-element.15.refs_0_), channel_id=1, source_target_pairs={{0,6},{2,4},{4,2},{6,0},{1,7},{3,5},{5,3},{7,1},{8,14},{10,12},{12... | collective-permute-start | bytes 6152 | tf_op jit(solution)/shard_map/ppermute | solution.py:35
  32.4 8.6 %collective-permute-start.2 = (f32[8,64]{1,0:T(8,128)}, f32[8,64]{1,0:T(8,128)S(1)}, u32[]{:S(2)}, u32[]{:S(2)}) collective-permute-start(f32[8,64]{1,0:T(8,128)} %get-tuple-element.15.refs_0_), channel_id=1, source_target_pairs={{0,4},{2,6},{4,0},{6,2},{1,5},{3,7},{5,1},{7,3},{8,12},{10,14},{12... | collective-permute-start | bytes 6152 | tf_op jit(solution)/shard_map/ppermute | solution.py:35
  32.4 8.6 %collective-permute-start.1 = (f32[8,64]{1,0:T(8,128)}, f32[8,64]{1,0:T(8,128)S(1)}, u32[]{:S(2)}, u32[]{:S(2)}) collective-permute-start(f32[8,64]{1,0:T(8,128)} %get-tuple-element.15.refs_0_), channel_id=1, source_target_pairs={{0,2},{2,0},{4,6},{6,4},{1,3},{3,1},{5,7},{7,5},{8,10},{10,8},{12,... | collective-permute-start | bytes 6152 | tf_op jit(solution)/shard_map/ppermute | solution.py:35
  41.0 0.6 copy-start.8
  41.0 0.6 copy-start.9
  41.0 0.6 copy-start.10
  41.0 0.7 %copy-start.6 = (f32[544,128]{1,0:T(8,128)}, f32[544,128]{1,0:T(8,128)S(1)}, u32[]{:S(2)}) copy-start(f32[544,128]{1,0:T(8,128)S(1)} %collective-permute-done.5.refs_5_) | copy-start | bytes 835588
  41.8 0.7 %copy-start.7 = (f32[544,128]{1,0:T(8,128)}, f32[544,128]{1,0:T(8,128)S(1)}, u32[]{:S(2)}) copy-start(f32[544,128]{1,0:T(8,128)S(1)} %collective-permute-done.7.refs_7_) | copy-start | bytes 835588
  53.8 4.4 %collective-permute-start.8 = (f32[72,128]{1,0:T(8,128)}, f32[72,128]{1,0:T(8,128)S(1)}, u32[]{:S(2)}, u32[]{:S(2)}) collective-permute-start(f32[72,128]{1,0:T(8,128)} %get-tuple-element.18), channel_id=1, source_target_pairs={{0,2},{2,0},{4,6},{6,4},{1,3},{3,1},{5,7},{7,5},{8,10},{10,8},{12,... | collective-permute-start | bytes 110600 | tf_op jit(solution)/shard_map/ppermute | solution.py:35
  54.4 5.1 %collective-permute-start.9 = (f32[72,128]{1,0:T(8,128)}, f32[72,128]{1,0:T(8,128)S(1)}, u32[]{:S(2)}, u32[]{:S(2)}) collective-permute-start(f32[72,128]{1,0:T(8,128)} %get-tuple-element.19), channel_id=1, source_target_pairs={{0,4},{2,6},{4,0},{6,2},{1,5},{3,7},{5,1},{7,3},{8,12},{10,14},{12... | collective-permute-start | bytes 110600 | tf_op jit(solution)/shard_map/ppermute | solution.py:35
  57.4 6.0 %collective-permute-start.10 = (f32[72,128]{1,0:T(8,128)}, f32[72,128]{1,0:T(8,128)S(1)}, u32[]{:S(2)}, u32[]{:S(2)}) collective-permute-start(f32[72,128]{1,0:T(8,128)} %get-tuple-element.20), channel_id=1, source_target_pairs={{0,6},{2,4},{4,2},{6,0},{1,7},{3,5},{5,3},{7,1},{8,14},{10,12},{12... | collective-permute-start | bytes 110600 | tf_op jit(solution)/shard_map/ppermute | solution.py:35
  58.3 5.1 %copy-start.1 = (f32[72,128]{1,0:T(8,128)}, f32[72,128]{1,0:T(8,128)S(1)}, u32[]{:S(2)}) copy-start(f32[72,128]{1,0:T(8,128)S(1)} %collective-permute-done.8.rest_1_) | copy-start | bytes 110596
  59.5 3.8 %copy-start.2 = (f32[72,128]{1,0:T(8,128)}, f32[72,128]{1,0:T(8,128)S(1)}, u32[]{:S(2)}) copy-start(f32[72,128]{1,0:T(8,128)S(1)} %collective-permute-done.9.rest_2_) | copy-start | bytes 110596
  63.3 0.6 copy-start.3

commit v2 on v1

v2 whole, which is shorter than its diff:
```python
import jax
import jax.numpy as jnp
from jax import lax
from jax.experimental import pallas as pl
from jax.experimental.pallas import tpu as pltpu
from jax.sharding import PartitionSpec as P

HEADS = 8
TILE = 128
SLOPE = 0.2
LOG2E = 1.4426950408889634
NEG = -1e30
F32 = jnp.float32
BF16 = jnp.bfloat16
HIGHEST = lax.Precision.HIGHEST
VMEM = pl.BlockSpec(memory_space=pltpu.VMEM)
SMEM = pl.BlockSpec(memory_space=pltpu.SMEM)


def is_pow2(n):
    return n & (n - 1) == 0


def goes_to(i, d, n):
    return i ^ d if is_pow2(n) else lax.rem(i + d, n)


def comes_from(i, d, n):
    return i ^ d if is_pow2(n) else lax.rem(i + n - d, n)


def hop(x, axis, d):
    n = lax.axis_size(axis)
    pairs = [(i, i ^ d if is_pow2(n) else (i + d) % n) for i in range(n)]
    return lax.ppermute(x, axis, pairs)


def call(kernel, out_shape, *args, in_specs=None, flops=0, bytes_accessed=0, **kw):
    return pl.pallas_call(
        kernel,
        out_shape=out_shape,
        in_specs=in_specs or [VMEM] * len(args),
        cost_estimate=pl.CostEstimate(
            flops=flops, bytes_accessed=bytes_accessed, transcendentals=0
        ),
        compiler_params=pltpu.CompilerParams(vmem_limit_bytes=limit(8, 0)),
        **kw,
    )(*args)


def limit(mib, least):
    return min(max(mib << 20, least), 60 << 20)


def up8(n):
    return -(-n // 8) * 8


def head_rows(vector, heads, width, height):
    dims = width // heads
    shape = (height, width)
    row = lax.broadcasted_iota(jnp.int32, shape, 0) % heads
    lane = lax.broadcasted_iota(jnp.int32, shape, 1)
    return jnp.where(lane // dims == row, jnp.broadcast_to(vector, shape), 0.0)


def contract(lhs, rhs, dims, precision=HIGHEST):
    return lax.dot_general(
        lhs, rhs, (dims, ((), ())), preferred_element_type=F32, precision=precision
    )


def take_cols(proj_ref, which, width):
    if width % TILE == 0:
        return proj_ref[:, pl.ds(pl.multiple_of(which * width, width), width)]
    full = proj_ref[...]
    out = full[:, :width]
    for k in range(1, full.shape[1] // width):
        out = jnp.where(which == k, full[:, k * width : (k + 1) * width], out)
    return out


def project(x, w):
    return lax.dot_general(x, w, (((1,), (0,)), ((), ())), preferred_element_type=F32)


def leaky(x):
    return jnp.maximum(x, SLOPE * x)


def on_device(
    src_feats, dst_feats, proj, att_src, att_dst, bias, tile_rows, tile_cols, tile_count, edge_weight
):
    n_row, n_col, n_feat = (lax.axis_size(a) for a in ("row", "col", "feat"))
    width = proj.shape[1] // n_feat
    heads = HEADS // n_feat
    dims = width // heads
    lanes = -(-width // TILE) * TILE
    src_rows, own_rows = src_feats.shape[0], dst_feats.shape[0]
    slots = tile_rows.shape[2]
    row_tiles = own_rows * n_col // TILE
    piece_tiles = src_rows // TILE
    col_tiles = piece_tiles * n_row
    per_tile = TILE // own_rows
    hp = up8(2 * heads)
    mdp = up8(2 * heads)
    att_src2, att_dst2, bias2 = (v.reshape(1, width) for v in (att_src, att_dst, bias))

    rows = src_rows + own_rows

    def send_kernel(src_ref, dst_ref, proj_ref, *outs):
        me = lax.axis_index("feat")
        for d in range(1, n_feat):
            w = take_cols(proj_ref, goes_to(me, d, n_feat), width)
            outs[d - 1][:src_rows] = project(src_ref[...], w)
            outs[d - 1][src_rows:] = project(dst_ref[...], w)

    sent = call(
        send_kernel,
        [jax.ShapeDtypeStruct((rows, width), F32)] * (n_feat - 1),
        src_feats,
        dst_feats,
        proj,
    )
    parts = [hop(sent[d - 1], "feat", d) for d in range(1, n_feat)]

    half = col_tiles // 2
    tiles = row_tiles * col_tiles
    period = min(slots, tiles) if slots % min(slots, tiles) == 0 else slots
    reps = slots // period
    group = 8

    def weight_kernel(rows_ref, cols_ref, count_ref, w_ref, near_ref, far_ref):
        step = pl.program_id(0)
        row = lax.axis_index("row")
        count = count_ref[0, 0]

        @pl.when(step == 0)
        def _():
            @pl.loop(0, row_tiles * half)
            def _(t):
                near_ref[t // half, t % half] = jnp.zeros((TILE, TILE), F32)
                far_ref[t // half, t % half] = jnp.zeros((TILE, TILE), F32)

        base = step * group

        @pl.loop(0, jnp.clip(count - base, 0, group))
        def _(u):
            r, c = rows_ref[0, 0, base + u], cols_ref[0, 0, base + u]
            q = ((c // piece_tiles) ^ row) * piece_tiles + c % piece_tiles
            total = w_ref[0, u].astype(F32)
            for k in range(1, reps):
                live = (base + u + k * period < count).astype(F32)
                total = total + w_ref[k, u].astype(F32) * live

            @pl.when(q < half)
            def _():
                near_ref[r, q] = near_ref[r, q] + total

            @pl.when(q >= half)
            def _():
                far_ref[r, q - half] = far_ref[r, q - half] + total

    panel_shape = (row_tiles, half, TILE, TILE)
    whole = lambda shape: pl.BlockSpec(shape, lambda s: (0,) * len(shape))
    panels = pl.pallas_call(
        weight_kernel,
        out_shape=[jax.ShapeDtypeStruct(panel_shape, F32)] * 2,
        grid=(period // group,),
        in_specs=[
            SMEM,
            SMEM,
            SMEM,
            pl.BlockSpec((reps, group, TILE, TILE), lambda s: (0, s, 0, 0)),
        ],
        out_specs=[whole(panel_shape)] * 2,
        compiler_params=pltpu.CompilerParams(vmem_limit_bytes=limit(32, 8 * tiles * TILE * TILE)),
        cost_estimate=pl.CostEstimate(
            flops=slots * TILE * TILE, bytes_accessed=slots * TILE * TILE * 2, transcendentals=0
        ),
    )(tile_rows, tile_cols, tile_count, edge_weight.reshape(reps, period, TILE, TILE))
    tied = lax.optimization_barrier((*parts, *panels))
    parts, panels = tied[: n_feat - 1], tied[n_feat - 1 :]

    pack_rows = src_rows + piece_tiles * hp

    def z_kernel(src_ref, dst_ref, proj_ref, att_src_ref, att_dst_ref, *rest):
        got, (out_ref, z_ref, s_ref) = rest[: n_feat - 1], rest[n_feat - 1 :]
        w = take_cols(proj_ref, lax.axis_index("feat"), width)
        z = project(src_ref[...], w)
        zdst = project(dst_ref[...], w)
        for part in got:
            z = z + part[:src_rows]
            zdst = zdst + part[src_rows:]
        if width < lanes:
            out_ref[...] = jnp.zeros_like(out_ref)
        out_ref[:src_rows, :width] = z
        s = LOG2E * contract(head_rows(att_src_ref[...], heads, width, hp), z, ((1,), (1,)))
        low = lax.broadcasted_iota(jnp.int32, s.shape, 0) < heads
        s = jnp.where(low, s, SLOPE * s)
        for t in range(piece_tiles):
            at = src_rows + t * hp
            out_ref[at : at + hp, :TILE] = s[:, t * TILE : (t + 1) * TILE]
        z_ref[...] = zdst
        s_ref[...] = LOG2E * contract(
            head_rows(att_dst_ref[...], heads, width, up8(heads)), zdst, ((1,), (1,))
        )

    own_piece, zdst, s_dst = call(
        z_kernel,
        [
            jax.ShapeDtypeStruct((pack_rows, lanes), F32),
            jax.ShapeDtypeStruct((own_rows, width), F32),
            jax.ShapeDtypeStruct((up8(heads), own_rows), F32),
        ],
        src_feats,
        dst_feats,
        proj,
        att_src2,
        att_dst2,
        *parts,
    )
    far0 = hop(own_piece, "row", n_row // 2)

    def spread(piece):
        pieces = {0: piece}
        d = n_row // 4
        while d:
            for k in list(pieces):
                pieces[k ^ d] = hop(pieces[k], "row", d)
            d //= 2
        return [pieces[k] for k in range(n_row // 2)]

    near_pieces = spread(own_piece)
    targets = [s_dst] + [hop(s_dst, "col", d) for d in range(1, n_col)]
    far_pieces = spread(far0)

    block = 64
    blocks = TILE // block
    unroll = 2 if row_tiles % 2 == 0 else 1
    chunk_rows = own_rows + mdp
    n_piece = n_row // 2
    k_all = n_piece * src_rows
    group_rows = unroll * TILE
    all_rows = row_tiles * TILE
    tiny = 2.0**-60

    def attend(refs, tgt, piece_refs, w_ref, z_cat, probs, num_ref, md_ref):
        step = pl.program_id(0)

        def score_rows(q, h):
            k, t = divmod(q, piece_tiles)
            at = src_rows + t * hp + h
            return piece_refs[k][at : at + 1, :TILE], piece_refs[k][at + heads : at + heads + 1, :TILE]

        tops = []
        for h in range(heads):
            top = score_rows(0, h)[0]
            for q in range(1, half):
                top = jnp.maximum(top, score_rows(q, h)[0])
            tops.append(jnp.max(top, axis=1, keepdims=True))

        lane_w = lax.broadcasted_iota(jnp.int32, (block, width), 1) // dims
        lane_t = lax.broadcasted_iota(jnp.int32, (block, TILE), 1)

        def put(at, h, q, p, slot):
            cols = slice(q * TILE, (q + 1) * TILE)
            hi = p.astype(BF16)
            lo = (p - hi.astype(F32)).astype(BF16)
            probs[slot, 2 * h * block : (2 * h + 1) * block, cols] = hi
            probs[slot, (2 * h + 1) * block : (2 * h + 2) * block, cols] = lo

        def finish(at, slot, dens, ms):
            both = lax.dot_general(
                probs[slot], z_cat[...], (((1,), (0,)), ((), ())), preferred_element_type=F32
            )
            num = jnp.zeros((block, width), F32)
            md = jnp.zeros((block, TILE), F32)
            for h in range(heads):
                hi = both[2 * h * block : (2 * h + 1) * block]
                lo = both[(2 * h + 1) * block : (2 * h + 2) * block]
                num = jnp.where(lane_w == h, hi[:, :width] + (hi[:, width:] + lo[:, :width]), num)
                md = jnp.where(lane_t == h, dens[h], md)
                md = jnp.where(lane_t == heads + h, ms[h], md)
            num_ref[pl.ds(at, block), :] = num
            md_ref[pl.ds(at, block), :] = md

        base = step * group_rows
        worst = None
        for b in range(unroll * blocks):
            at = pl.multiple_of(base + b * block, block)
            rt, i0 = divmod(b * block, TILE)
            t_all = tgt[pl.ds(at, block), :]
            dens, ms = [], []
            for h in range(heads):
                a = t_all[:, h : h + 1]
                m = leaky(a + tops[h])
                pos = jnp.broadcast_to(a - m, (block, TILE))
                neg = jnp.broadcast_to(SLOPE * a - m, (block, TILE))
                den = jnp.zeros((block, TILE), F32)
                for q in range(half):
                    s, s_low = score_rows(q, h)
                    p = w_ref[rt, q, i0 : i0 + block, :] * jnp.exp2(
                        jnp.maximum(pos + s, neg + s_low)
                    )
                    den = den + p
                    put(at, h, q, p, b % 2)
                den = jnp.sum(den, axis=1, keepdims=True)
                worst = den if worst is None else jnp.minimum(worst, den)
                dens.append(den)
                ms.append(m)
            finish(at, b % 2, dens, ms)

        @pl.when(jnp.logical_not(jnp.min(worst) >= tiny))
        def _():
            @pl.loop(0, unroll * blocks)
            def _(b):
                at = pl.multiple_of(base + b * block, block)
                rt = b // blocks
                i0 = pl.multiple_of((b % blocks) * block, block)
                t_all = tgt[pl.ds(at, block), :]
                dens, ms = [], []
                for h in range(heads):
                    best = jnp.full((block, TILE), NEG, F32)
                    for q in range(half):
                        s, _ = score_rows(q, h)
                        edge = w_ref[rt, q, pl.ds(i0, block), :] > 0
                        best = jnp.maximum(best, jnp.where(edge, s, NEG))
                    a = t_all[:, h : h + 1]
                    m = leaky(a + jnp.max(best, axis=1, keepdims=True))
                    pos, neg = a - m, SLOPE * a - m
                    den = jnp.zeros((block, TILE), F32)
                    for q in range(half):
                        s, s_low = score_rows(q, h)
                        x = jnp.maximum(pos + s, neg + s_low)
                        p = w_ref[rt, q, pl.ds(i0, block), :] * jnp.exp2(jnp.minimum(x, 0.0))
                        den = den + p
                        put(at, h, q, p, 0)
                    dens.append(jnp.sum(den, axis=1, keepdims=True))
                    ms.append(m)
                finish(at, 0, dens, ms)

    def split_z(piece_refs, z_cat):
        for k in range(n_piece):
            z = piece_refs[k][:src_rows, :width]
            hi = z.astype(BF16)
            z_cat[k * src_rows : (k + 1) * src_rows, :width] = hi
            z_cat[k * src_rows : (k + 1) * src_rows, width:] = (z - hi.astype(F32)).astype(BF16)

    def near_kernel(*refs):
        tgt_refs, refs = refs[:n_col], refs[n_col:]
        piece_refs, refs = refs[:n_piece], refs[n_piece:]
        w_ref, tgt, num_ref, md_ref, z_cat, probs = refs
        col = lax.axis_index("col")

        @pl.when(pl.program_id(0) == 0)
        def _():
            shape = (up8(heads), TILE)
            eye = (
                lax.broadcasted_iota(jnp.int32, shape, 0)
                == lax.broadcasted_iota(jnp.int32, shape, 1)
            ).astype(F32)
            for d in range(n_col):
                at = pl.multiple_of(comes_from(col, d, n_col) * own_rows, own_rows)
                tgt[pl.ds(at, own_rows), :] = contract(tgt_refs[d][...], eye, ((0,), (0,)))
            split_z(piece_refs, z_cat)

        attend(refs, tgt, piece_refs, w_ref, z_cat, probs, num_ref, md_ref)

    def far_kernel(*refs):
        tgt, near_num, near_md, refs = refs[0], refs[1], refs[2], refs[3:]
        piece_refs, refs = refs[:n_piece], refs[n_piece:]
        w_ref, refs = refs[0], refs[1:]
        out_refs, (num_ref, md_ref, z_cat, probs) = refs[:n_col], refs[n_col:]
        col = lax.axis_index("col")
        step = pl.program_id(0)

        @pl.when(step == 0)
        def _():
            split_z(piece_refs, z_cat)

        attend(refs, tgt, piece_refs, w_ref, z_cat, probs, num_ref, md_ref)

        base = step * group_rows
        lane_w = lax.broadcasted_iota(jnp.int32, (TILE, width), 1) // dims
        lane_t = lax.broadcasted_iota(jnp.int32, (TILE, TILE), 1)
        for rt in range(unroll):
            at = pl.ds(pl.multiple_of(base + rt * TILE, TILE), TILE)
            near, far = near_md[at, :], md_ref[at, :]
            md = jnp.zeros((TILE, TILE), F32)
            f_near = jnp.zeros((TILE, width), F32)
            f_far = jnp.zeros((TILE, width), F32)
            for h in range(heads):
                m0, m1 = near[:, heads + h : heads + h + 1], far[:, heads + h : heads + h + 1]
                m = jnp.maximum(m0, m1)
                f0, f1 = jnp.exp2(m0 - m), jnp.exp2(m1 - m)
                den = near[:, h : h + 1] * f0 + far[:, h : h + 1] * f1
                md = jnp.where(lane_t == h, den, md)
                md = jnp.where(lane_t == heads + h, m, md)
                f_near = jnp.where(lane_w == h, f0, f_near)
                f_far = jnp.where(lane_w == h, f1, f_far)
            num = near_num[at, :] * f_near + num_ref[at, :] * f_far
            num_ref[at, :] = num
            md_ref[at, :] = md

        @pl.when(step == row_tiles // unroll - 1)
        def _():
            for d in range(n_col):
                at = pl.multiple_of(goes_to(col, d, n_col) * own_rows, own_rows)
                if width < lanes:
                    out_refs[d][...] = jnp.zeros_like(out_refs[d])
                out_refs[d][:own_rows, :width] = num_ref[pl.ds(at, own_rows), :]
                out_refs[d][own_rows:, :own_rows] = md_ref[pl.ds(at, own_rows), :].T[:mdp]

    scratch = [
        pltpu.VMEM((k_all, 2 * width), BF16),
        pltpu.VMEM((2, 2 * heads * block, k_all), BF16),
    ]
    cost = pl.CostEstimate(
        flops=all_rows * k_all * width * heads * 8,
        bytes_accessed=k_all * width * 4,
        transcendentals=all_rows * k_all * heads,
    )
    w_spec = pl.BlockSpec((unroll, half, TILE, TILE), lambda s: (s, 0, 0, 0))
    rows_shape = [(all_rows, TILE), (all_rows, width), (all_rows, TILE)]
    params = pltpu.CompilerParams(vmem_limit_bytes=limit(32, 8 * tiles * TILE * TILE))
    tgt, near_num, near_md = pl.pallas_call(
        near_kernel,
        out_shape=[jax.ShapeDtypeStruct(s, F32) for s in rows_shape],
        grid=(row_tiles // unroll,),
        in_specs=[whole((up8(heads), own_rows))] * n_col
        + [whole((pack_rows, lanes))] * n_piece
        + [w_spec],
        out_specs=[whole(s) for s in rows_shape],
        scratch_shapes=scratch,
        cost_estimate=cost,
        compiler_params=params,
    )(*targets, *near_pieces, panels[0])
    chunk = (chunk_rows, lanes)
    chunks = pl.pallas_call(
        far_kernel,
        out_shape=[jax.ShapeDtypeStruct(chunk, F32)] * n_col,
        grid=(row_tiles // unroll,),
        in_specs=[whole(s) for s in rows_shape]
        + [whole((pack_rows, lanes))] * n_piece
        + [w_spec],
        out_specs=[whole(chunk)] * n_col,
        scratch_shapes=[pltpu.VMEM(s, F32) for s in rows_shape[1:]] + scratch,
        cost_estimate=cost,
        compiler_params=params,
    )(tgt, near_num, near_md, *far_pieces, panels[1])
    gathered = [chunks[0]] + [hop(chunks[d], "col", d) for d in range(1, n_col)]

    def out_kernel(zdst_ref, src_ref, dst_ref, bias_ref, *rest):
        parts, out_ref = rest[:n_col], rest[n_col]
        same = (
            lax.broadcasted_iota(jnp.int32, (width, width), 0) // dims
            == lax.broadcasted_iota(jnp.int32, (width, width), 1) // dims
        ).astype(F32)
        z = zdst_ref[...]
        pair = contract(z * (dst_ref[...] + src_ref[...]), same, ((1,), (0,)))
        e_self = leaky(LOG2E * pair)
        which = lax.broadcasted_iota(jnp.int32, (mdp, width), 0)
        head = lax.broadcasted_iota(jnp.int32, (mdp, width), 1) // dims
        den_of, m_of = (which == head).astype(F32), (which == head + heads).astype(F32)
        mds = [part[own_rows:, :own_rows] for part in parts]
        ms = [contract(md, m_of, ((0,), (0,))) for md in mds]
        dens = [contract(md, den_of, ((0,), (0,))) for md in mds]
        top = e_self
        for m in ms:
            top = jnp.maximum(top, m)
        den = jnp.exp2(e_self - top)
        num = den * z
        for part, m, own_den in zip(parts, ms, dens):
            factor = jnp.exp2(m - top)
            den = den + factor * own_den
            num = num + factor * part[:own_rows, :width]
        x = num / den + bias_ref[...]
        out_ref[...] = jnp.where(x > 0, x, jnp.exp(jnp.minimum(x, 0.0)) - 1.0).astype(BF16)

    return call(
        out_kernel,
        jax.ShapeDtypeStruct((own_rows, width), BF16),
        zdst,
        att_src2,
        att_dst2,
        bias2,
        *gathered,
    )


def solution(mesh):
    return jax.shard_map(
        on_device,
        mesh=mesh,
        in_specs=(
            P(("row", "col"), "feat"),
            P(("row", "col"), "feat"),
            P("feat", None),
            P("feat"),
            P("feat"),
            P("feat"),
            P("row", "col", None),
            P("row", "col", None),
            P("row", "col"),
            P("row", "col", None, None, None),
        ),
        out_specs=P(("row", "col"), "feat"),
        check_vma=False,
    )
```

time: 66.3 us -> 54.4 us (0.82)
  waiting for transfers between devices: 20.5 us -> 13.9 us
  Pallas kernels: 26.3 us -> 19.8 us
  local copies, waits for them, and re-layouts: 3.36 us -> 5.98 us
  starting transfers between devices: 15 us -> 13.6 us
    ppermute x11 -> x10, waiting for transfers between devices: 20.5 us -> 13.9 us  [hop(): return lax.ppermute(x, axis, pairs)]
    pallas_call x4 -> x3, Pallas kernels: 7.81 us -> 1.79 us  [call(): pl.pallas_call(kernel, out_shape=out_shape, in_specs=in_specs or [VMEM] *...]
    unnamed x22 -> x24, local copies, waits for them, and re-layouts: 3.36 us -> 5.98 us
    ppermute x11 -> x10, starting transfers between devices: 15 us -> 13.6 us  [hop(): return lax.ppermute(x, axis, pairs)]
    pallas_call x2 -> x3, Pallas kernels: 18.5 us -> 18 us  [the longest x1 8.19 us: on_device(): pl.pallas_call(far_kernel, out_shape=[jax.ShapeDtypeStruct(chunk, F32)] *...]
  transfers between devices with their start and end apart: 11 -> 10, of which waited for: 5 -> 6; matrix products, arithmetic and copies ran while one was open for 0% -> 0% of each run, Pallas kernels for 13% -> 18%
where the time goes in v2:
time: 54.4 us; the launch traced here: 54.1 us
  Pallas kernels  19.8 us (36%)
  waiting for transfers between devices  13.9 us (26%)
  starting transfers between devices  13.6 us (25%)
  local copies, waits for them, and re-layouts  5.98 us (11%)
  between operations  0.75 us (1%)
    ppermute x10, waiting for transfers between devices, hop(): return lax.ppermute(x, axis, pairs)  13.9 us
    ppermute x10, starting transfers between devices, hop(): return lax.ppermute(x, axis, pairs)  13.6 us
    pallas_call x1, Pallas kernels, on_device(): pl.pallas_call(far_kernel, out_shape=[jax.ShapeDtypeStruct(chunk, F32)] *...  8.19 us
    pallas_call x1, Pallas kernels, on_device(): pl.pallas_call(near_kernel, out_shape=[jax.ShapeDtypeStruct(s, F32) for s...  7.36 us
    unnamed x24, local copies, waits for them, and re-layouts  5.98 us
    pallas_call x1, Pallas kernels, on_device(): pl.pallas_call(weight_kernel, out_shape=[jax.ShapeDtypeStruct(panel_shape...  2.47 us
    pallas_call x3, Pallas kernels, call(): pl.pallas_call(kernel, out_shape=out_shape, in_specs=in_specs or [VMEM] *...  1.79 us
  transfers between devices with their start and end apart: 10, of which 6 were waited for; matrix products, arithmetic and copies ran while one was open for 0% of the time, Pallas kernels for 18%

profile of v2, /device:TPU:0, one launch (start us, length us, event | category | flops | bytes accessed | tf_op | source)
XLA Modules:
  0.0 54.1 jit_solution(8484459928486368564)
XLA Ops:
  0.0 0.9 %copy-done.1 = bf16[512,128]{1,0:T(8,128)(2,1)S(1)} copy-done((bf16[512,128]{1,0:T(8,128)(2,1)S(1)}, bf16[512,128]{1,0:T(8,128)(2,1)}, u32[]{:S(2)}) %copy-start.1) | copy-done | bytes 131096
  0.9 0.8 %copy-done.3 = bf16[128,256]{1,0:T(8,128)(2,1)S(1)} copy-done((bf16[128,256]{1,0:T(8,128)(2,1)S(1)}, bf16[128,256]{1,0:T(8,128)(2,1)}, u32[]{:S(2)}) %copy-start.3) | copy-done | bytes 65560
  1.7 0.7 %copy-done.5 = bf16[64,128]{1,0:T(8,128)(2,1)S(1)} copy-done((bf16[64,128]{1,0:T(8,128)(2,1)S(1)}, bf16[64,128]{1,0:T(8,128)(2,1)}, u32[]{:S(2)}) %copy-start.5) | copy-done | bytes 16408
  2.5 0.2 shard_map.100
  2.7 3.0 %collective-permute-start = (f32[576,128]{1,0:T(8,128)S(1)}, f32[576,128]{1,0:T(8,128)S(1)}, u32[]{:S(2)}, u32[]{:S(2)}) collective-permute-start(f32[576,128]{1,0:T(8,128)S(1)} %shard_map.100), channel_id=1, source_target_pairs={{0,1},{1,0},{2,3},{3,2},{4,5},{5,4},{6,7},{7,6},{8,9},{9,8},{10,11... | collective-permute-start | bytes 884744 | tf_op jit(solution)/shard_map/ppermute | solution.py:35
  6.4 0.0 copy-start
  6.4 2.2 %copy-done = bf16[1,1,128,128,128]{4,3,2,1,0:T(8,128)(2,1)S(1)} copy-done((bf16[1,1,128,128,128]{4,3,2,1,0:T(8,128)(2,1)S(1)}, bf16[1,1,128,128,128]{4,3,2,1,0:T(8,128)(2,1)}, u32[]{:S(2)}) %copy-start) | copy-done | bytes 4194328
  8.5 0.7 %copy-done.9 = s32[1,1,128]{2,1,0:T(1,128)S(1)} copy-done((s32[1,1,128]{2,1,0:T(1,128)S(1)}, s32[1,1,128]{2,1,0:T(1,128)}, u32[]{:S(2)}) %copy-start.9) | copy-done | bytes 536
  9.2 0.7 %copy-done.10 = s32[1,1,128]{2,1,0:T(1,128)S(1)} copy-done((s32[1,1,128]{2,1,0:T(1,128)S(1)}, s32[1,1,128]{2,1,0:T(1,128)}, u32[]{:S(2)}) %copy-start.10) | copy-done | bytes 536
  9.9 2.5 %shard_map.101 = (f32[2,8,128,128]{3,2,1,0:T(8,128)S(1)}, f32[2,8,128,128]{3,2,1,0:T(8,128)S(1)}) custom-call(s32[1,1,128]{2,1,0:T(1,128)S(1)} %copy-done.9, s32[1,1,128]{2,1,0:T(1,128)S(1)} %copy-done.10, s32[1,1]{1,0:T(1,128)S(6)} %copy.11.count_ref, bf16[4,32,128,128]{3,2,1,0:T(8,128)(2,1)S(1)} %bitcast.4), custom_call_target="tpu_custom_call" | custom-call | flops 2097152 | bytes 4194304 | tf_op jit(solution)/shard_map/pallas_call | solution.py:166
  12.3 0.4 collective-permute-done.rest_0_
  12.7 0.0 copy-start.11
  12.8 0.5 shard_map.102
  13.3 1.8 %collective-permute-start.5 = (f32[544,128]{1,0:T(8,128)S(1)}, f32[544,128]{1,0:T(8,128)S(1)}, u32[]{:S(2)}, u32[]{:S(2)}) collective-permute-start(f32[544,128]{1,0:T(8,128)S(1)} %get-tuple-element.25.refs_4_), channel_id=1, source_target_pairs={{0,16},{8,24},{16,0},{24,8},{1,17},{9,25},{17,1},{25,9},{2,18},{10... | collective-permute-start | bytes 835592 | tf_op jit(solution)/shard_map/ppermute | solution.py:35
  15.1 0.0 collective-permute-start.4
  15.1 6.0 %collective-permute-done.5.refs_3_ = f32[544,128]{1,0:T(8,128)S(1)} collective-permute-done((f32[544,128]{1,0:T(8,128)S(1)}, f32[544,128]{1,0:T(8,128)S(1)}, u32[]{:S(2)}, u32[]{:S(2)}) %collective-permute-start.5) | collective-permute-done | bytes 278560 | tf_op jit(solution)/shard_map/ppermute | solution.py:35
  21.1 0.0 collective-permute-start.6
  21.1 1.5 %collective-permute-start.1 = (f32[8,64]{1,0:T(8,128)S(1)}, f32[8,64]{1,0:T(8,128)S(1)}, u32[]{:S(2)}, u32[]{:S(2)}) collective-permute-start(f32[8,64]{1,0:T(8,128)S(1)} %get-tuple-element.24.refs_0_), channel_id=1, source_target_pairs={{0,2},{2,0},{4,6},{6,4},{1,3},{3,1},{5,7},{7,5},{8,10},{10,8},{12,... | collective-permute-start | bytes 6152 | tf_op jit(solution)/shard_map/ppermute | solution.py:35
  22.7 2.6 %collective-permute-start.2 = (f32[8,64]{1,0:T(8,128)S(1)}, f32[8,64]{1,0:T(8,128)S(1)}, u32[]{:S(2)}, u32[]{:S(2)}) collective-permute-start(f32[8,64]{1,0:T(8,128)S(1)} %get-tuple-element.24.refs_0_), channel_id=1, source_target_pairs={{0,4},{2,6},{4,0},{6,2},{1,5},{3,7},{5,1},{7,3},{8,12},{10,14},{12... | collective-permute-start | bytes 6152 | tf_op jit(solution)/shard_map/ppermute | solution.py:35
  25.3 0.3 collective-permute-start.3
  25.5 0.0 collective-permute-done.1.refs_1_
  25.5 1.7 %collective-permute-done.2.refs_2_ = f32[8,64]{1,0:T(8,128)S(1)} collective-permute-done((f32[8,64]{1,0:T(8,128)S(1)}, f32[8,64]{1,0:T(8,128)S(1)}, u32[]{:S(2)}, u32[]{:S(2)}) %collective-permute-start.2) | collective-permute-done | bytes 2080 | tf_op jit(solution)/shard_map/ppermute | solution.py:35
  27.2 3.5 %collective-permute-done.3.refs_3_ = f32[8,64]{1,0:T(8,128)S(1)} collective-permute-done((f32[8,64]{1,0:T(8,128)S(1)}, f32[8,64]{1,0:T(8,128)S(1)}, u32[]{:S(2)}, u32[]{:S(2)}) %collective-permute-start.3) | collective-permute-done | bytes 2080 | tf_op jit(solution)/shard_map/ppermute | solution.py:35
  30.7 0.0 collective-permute-done.4.refs_5_
  30.7 7.4 %shard_map.103 = (f32[256,128]{1,0:T(8,128)S(1)}, f32[256,128]{1,0:T(8,128)S(1)}, f32[256,128]{1,0:T(8,128)S(1)}) custom-call(f32[8,64]{1,0:T(8,128)S(1)} %get-tuple-element.24.refs_0_, f32[8,64]{1,0:T(8,128)S(1)} %collective-permute-done.1.refs_1_, f32[8,64]{1,0:T(8,128)S(1)} %collective-permute-done.2.refs_2_, f32[8,64]{1,0:T(8,128)S(1)} %collective-permute-done.3.refs_3_, ...), custom_call_target="tpu_custom_call" | custom-call | flops 1073741824 | bytes 524288 | tf_op jit(solution)/shard_map/pallas_call | solution.py:427
  38.1 8.2 %shard_map.104 = (f32[72,128]{1,0:T(8,128)S(1)}, f32[72,128]{1,0:T(8,128)S(1)}, f32[72,128]{1,0:T(8,128)S(1)}, f32[72,128]{1,0:T(8,128)S(1)}) custom-call(f32[256,128]{1,0:T(8,128)S(1)} %get-tuple-element.27.refs_0_, f32[256,128]{1,0:T(8,128)S(1)} %get-tuple-element.28.refs_1_, f32[256,128]{1,0:T(8,128)S(1)} %get-tuple-element.29.refs_2_, ...), custom_call_target="tpu_custom_call" | custom-call | flops 1073741824 | bytes 524288 | tf_op jit(solution)/shard_map/pallas_call | solution.py:440
  46.3 0.0 collective-permute-start.7
  46.3 0.8 %collective-permute-start.8 = (f32[72,128]{1,0:T(8,128)S(1)}, f32[72,128]{1,0:T(8,128)S(1)}, u32[]{:S(2)}, u32[]{:S(2)}) collective-permute-start(f32[72,128]{1,0:T(8,128)S(1)} %get-tuple-element.33), channel_id=1, source_target_pairs={{0,4},{2,6},{4,0},{6,2},{1,5},{3,7},{5,1},{7,3},{8,12},{10,14},{12... | collective-permute-start | bytes 110600 | tf_op jit(solution)/shard_map/ppermute | solution.py:35
  47.1 3.6 %collective-permute-start.9 = (f32[72,128]{1,0:T(8,128)S(1)}, f32[72,128]{1,0:T(8,128)S(1)}, u32[]{:S(2)}, u32[]{:S(2)}) collective-permute-start(f32[72,128]{1,0:T(8,128)S(1)} %get-tuple-element.34), channel_id=1, source_target_pairs={{0,6},{2,4},{4,2},{6,0},{1,7},{3,5},{5,3},{7,1},{8,14},{10,12},{12... | collective-permute-start | bytes 110600 | tf_op jit(solution)/shard_map/ppermute | solution.py:35
  50.7 0.5 %collective-permute-done.8.rest_2_ = f32[72,128]{1,0:T(8,128)S(1)} collective-permute-done((f32[72,128]{1,0:T(8,128)S(1)}, f32[72,128]{1,0:T(8,128)S(1)}, u32[]{:S(2)}, u32[]{:S(2)}) %collective-permute-start.8) | collective-permute-done | bytes 36896 | tf_op jit(solution)/shard_map/ppermute | solution.py:35
  51.2 1.8 %collective-permute-done.9.rest_3_ = f32[72,128]{1,0:T(8,128)S(1)} collective-permute-done((f32[72,128]{1,0:T(8,128)S(1)}, f32[72,128]{1,0:T(8,128)S(1)}, u32[]{:S(2)}, u32[]{:S(2)}) %collective-permute-start.9) | collective-permute-done | bytes 36896 | tf_op jit(solution)/shard_map/ppermute | solution.py:35
  53.0 1.1 %shard_map.105 = bf16[64,128]{1,0:T(8,128)(2,1)} custom-call(f32[64,128]{1,0:T(8,128)S(1)} %get-tuple-element.23.zdst_ref, f32[1,128]{1,0:T(1,128)S(1)} %bitcast.6, f32[1,128]{1,0:T(1,128)S(1)} %bitcast.8, f32[1,128]{1,0:T(1,128)S(1)} %bitcast.9, f32[72,128]{1,0:T(8,128)S(1)} %get-tuple-element.31.rest_0_, f32[72,128]{1,0:T(8,128)S(1)} %collective-permute-done.7.rest_1_, ...), custom_call_target="tpu_custom_call" | custom-call | tf_op jit(solution)/shard_map/pallas_call | solution.py:39
  (18 shorter events, 0.0 us)
Async XLA Ops:
  0.0 0.9 %copy-start.1 = (bf16[512,128]{1,0:T(8,128)(2,1)S(1)}, bf16[512,128]{1,0:T(8,128)(2,1)}, u32[]{:S(2)}) copy-start(bf16[512,128]{1,0:T(8,128)(2,1)} %src_ref.3) | copy-start | bytes 393220
  0.9 0.8 %copy-start.3 = (bf16[128,256]{1,0:T(8,128)(2,1)S(1)}, bf16[128,256]{1,0:T(8,128)(2,1)}, u32[]{:S(2)}) copy-start(bf16[128,256]{1,0:T(8,128)(2,1)} %proj_ref.3) | copy-start | bytes 196612
  1.7 0.7 %copy-start.5 = (bf16[64,128]{1,0:T(8,128)(2,1)S(1)}, bf16[64,128]{1,0:T(8,128)(2,1)}, u32[]{:S(2)}) copy-start(bf16[64,128]{1,0:T(8,128)(2,1)} %dst_ref.3) | copy-start | bytes 49156
  2.5 10.3 %copy-start.2 = (bf16[512,128]{1,0:T(8,128)(2,1)S(1)}, bf16[512,128]{1,0:T(8,128)(2,1)}, u32[]{:S(2)}) copy-start(bf16[512,128]{1,0:T(8,128)(2,1)} %src_ref.3) | copy-start | bytes 393220
  2.5 10.3 %copy-start.4 = (bf16[128,256]{1,0:T(8,128)(2,1)S(1)}, bf16[128,256]{1,0:T(8,128)(2,1)}, u32[]{:S(2)}) copy-start(bf16[128,256]{1,0:T(8,128)(2,1)} %proj_ref.3) | copy-start | bytes 196612
  2.5 10.3 %copy-start.6 = (bf16[64,128]{1,0:T(8,128)(2,1)S(1)}, bf16[64,128]{1,0:T(8,128)(2,1)}, u32[]{:S(2)}) copy-start(bf16[64,128]{1,0:T(8,128)(2,1)} %dst_ref.3) | copy-start | bytes 49156
  2.5 10.3 %copy-start.7 = (f32[128]{0:T(128)S(1)}, f32[128]{0:T(128)}, u32[]{:S(2)}) copy-start(f32[128]{0:T(128)} %param.13) | copy-start | bytes 1540
  2.5 10.3 %copy-start.8 = (f32[128]{0:T(128)S(1)}, f32[128]{0:T(128)}, u32[]{:S(2)}) copy-start(f32[128]{0:T(128)} %param.14) | copy-start | bytes 1540
  2.7 10.0 %collective-permute-start = (f32[576,128]{1,0:T(8,128)S(1)}, f32[576,128]{1,0:T(8,128)S(1)}, u32[]{:S(2)}, u32[]{:S(2)}) collective-permute-start(f32[576,128]{1,0:T(8,128)S(1)} %shard_map.100), channel_id=1, source_target_pairs={{0,1},{1,0},{2,3},{3,2},{4,5},{5,4},{6,7},{7,6},{8,9},{9,8},{10,11... | collective-permute-start | bytes 884744 | tf_op jit(solution)/shard_map/ppermute | solution.py:35
  6.4 2.2 %copy-start = (bf16[1,1,128,128,128]{4,3,2,1,0:T(8,128)(2,1)S(1)}, bf16[1,1,128,128,128]{4,3,2,1,0:T(8,128)(2,1)}, u32[]{:S(2)}) copy-start(bf16[1,1,128,128,128]{4,3,2,1,0:T(8,128)(2,1)} %param.19) | copy-start | bytes 12582916
  8.5 0.7 %copy-start.9 = (s32[1,1,128]{2,1,0:T(1,128)S(1)}, s32[1,1,128]{2,1,0:T(1,128)}, u32[]{:S(2)}) copy-start(s32[1,1,128]{2,1,0:T(1,128)} %rows_ref.1) | copy-start | bytes 1540
  9.2 0.7 %copy-start.10 = (s32[1,1,128]{2,1,0:T(1,128)S(1)}, s32[1,1,128]{2,1,0:T(1,128)}, u32[]{:S(2)}) copy-start(s32[1,1,128]{2,1,0:T(1,128)} %cols_ref.1) | copy-start | bytes 1540
  12.7 40.3 %copy-start.11 = (f32[128]{0:T(128)S(1)}, f32[128]{0:T(128)}, u32[]{:S(2)}) copy-start(f32[128]{0:T(128)} %param.15) | copy-start | bytes 1540
  13.3 7.8 %collective-permute-start.5 = (f32[544,128]{1,0:T(8,128)S(1)}, f32[544,128]{1,0:T(8,128)S(1)}, u32[]{:S(2)}, u32[]{:S(2)}) collective-permute-start(f32[544,128]{1,0:T(8,128)S(1)} %get-tuple-element.25.refs_4_), channel_id=1, source_target_pairs={{0,16},{8,24},{16,0},{24,8},{1,17},{9,25},{17,1},{25,9},{2,18},{10... | collective-permute-start | bytes 835592 | tf_op jit(solution)/shard_map/ppermute | solution.py:35
  15.1 15.6 %collective-permute-start.4 = (f32[544,128]{1,0:T(8,128)S(1)}, f32[544,128]{1,0:T(8,128)S(1)}, u32[]{:S(2)}, u32[]{:S(2)}) collective-permute-start(f32[544,128]{1,0:T(8,128)S(1)} %get-tuple-element.25.refs_4_), channel_id=1, source_target_pairs={{0,8},{8,0},{16,24},{24,16},{1,9},{9,1},{17,25},{25,17},{2,10},{10... | collective-permute-start | bytes 835592 | tf_op jit(solution)/shard_map/ppermute | solution.py:35
  21.1 16.9 %collective-permute-start.6 = (f32[544,128]{1,0:T(8,128)S(1)}, f32[544,128]{1,0:T(8,128)S(1)}, u32[]{:S(2)}, u32[]{:S(2)}) collective-permute-start(f32[544,128]{1,0:T(8,128)S(1)} %collective-permute-done.5.refs_3_), channel_id=1, source_target_pairs={{0,8},{8,0},{16,24},{24,16},{1,9},{9,1},{17,25},{25,17},{2,10},{10... | collective-permute-start | bytes 835592 | tf_op jit(solution)/shard_map/ppermute | solution.py:35
  21.1 4.4 %collective-permute-start.1 = (f32[8,64]{1,0:T(8,128)S(1)}, f32[8,64]{1,0:T(8,128)S(1)}, u32[]{:S(2)}, u32[]{:S(2)}) collective-permute-start(f32[8,64]{1,0:T(8,128)S(1)} %get-tuple-element.24.refs_0_), channel_id=1, source_target_pairs={{0,2},{2,0},{4,6},{6,4},{1,3},{3,1},{5,7},{7,5},{8,10},{10,8},{12,... | collective-permute-start | bytes 6152 | tf_op jit(solution)/shard_map/ppermute | solution.py:35
  22.7 4.5 %collective-permute-start.2 = (f32[8,64]{1,0:T(8,128)S(1)}, f32[8,64]{1,0:T(8,128)S(1)}, u32[]{:S(2)}, u32[]{:S(2)}) collective-permute-start(f32[8,64]{1,0:T(8,128)S(1)} %get-tuple-element.24.refs_0_), channel_id=1, source_target_pairs={{0,4},{2,6},{4,0},{6,2},{1,5},{3,7},{5,1},{7,3},{8,12},{10,14},{12... | collective-permute-start | bytes 6152 | tf_op jit(solution)/shard_map/ppermute | solution.py:35
  25.3 5.4 %collective-permute-start.3 = (f32[8,64]{1,0:T(8,128)S(1)}, f32[8,64]{1,0:T(8,128)S(1)}, u32[]{:S(2)}, u32[]{:S(2)}) collective-permute-start(f32[8,64]{1,0:T(8,128)S(1)} %get-tuple-element.24.refs_0_), channel_id=1, source_target_pairs={{0,6},{2,4},{4,2},{6,0},{1,7},{3,5},{5,3},{7,1},{8,14},{10,12},{12... | collective-permute-start | bytes 6152 | tf_op jit(solution)/shard_map/ppermute | solution.py:35
  46.3 4.4 %collective-permute-start.7 = (f32[72,128]{1,0:T(8,128)S(1)}, f32[72,128]{1,0:T(8,128)S(1)}, u32[]{:S(2)}, u32[]{:S(2)}) collective-permute-start(f32[72,128]{1,0:T(8,128)S(1)} %get-tuple-element.32), channel_id=1, source_target_pairs={{0,2},{2,0},{4,6},{6,4},{1,3},{3,1},{5,7},{7,5},{8,10},{10,8},{12,... | collective-permute-start | bytes 110600 | tf_op jit(solution)/shard_map/ppermute | solution.py:35
  46.3 4.9 %collective-permute-start.8 = (f32[72,128]{1,0:T(8,128)S(1)}, f32[72,128]{1,0:T(8,128)S(1)}, u32[]{:S(2)}, u32[]{:S(2)}) collective-permute-start(f32[72,128]{1,0:T(8,128)S(1)} %get-tuple-element.33), channel_id=1, source_target_pairs={{0,4},{2,6},{4,0},{6,2},{1,5},{3,7},{5,1},{7,3},{8,12},{10,14},{12... | collective-permute-start | bytes 110600 | tf_op jit(solution)/shard_map/ppermute | solution.py:35
  47.1 5.9 %collective-permute-start.9 = (f32[72,128]{1,0:T(8,128)S(1)}, f32[72,128]{1,0:T(8,128)S(1)}, u32[]{:S(2)}, u32[]{:S(2)}) collective-permute-start(f32[72,128]{1,0:T(8,128)S(1)} %get-tuple-element.34), channel_id=1, source_target_pairs={{0,6},{2,4},{4,2},{6,0},{1,7},{3,5},{5,3},{7,1},{8,14},{10,12},{12... | collective-permute-start | bytes 110600 | tf_op jit(solution)/shard_map/ppermute | solution.py:35

commit v3 on v2

--- a/solution.py
+++ b/solution.py
@@ -12,9 +12,11 @@
 NEG = -1e30
 F32 = jnp.float32
 BF16 = jnp.bfloat16
+ALL_VMEM = 67043328
 HIGHEST = lax.Precision.HIGHEST
 VMEM = pl.BlockSpec(memory_space=pltpu.VMEM)
 SMEM = pl.BlockSpec(memory_space=pltpu.SMEM)
+HBM = pl.BlockSpec(memory_space=pltpu.HBM)
 
 
 def is_pow2(n):
@@ -35,7 +37,7 @@
     return lax.ppermute(x, axis, pairs)
 
 
-def call(kernel, out_shape, *args, in_specs=None, flops=0, bytes_accessed=0, **kw):
+def call(kernel, out_shape, *args, in_specs=None, flops=0, bytes_accessed=0, grant=8 << 20, **kw):
     return pl.pallas_call(
         kernel,
         out_shape=out_shape,
@@ -43,7 +45,7 @@
         cost_estimate=pl.CostEstimate(
             flops=flops, bytes_accessed=bytes_accessed, transcendentals=0
         ),
-        compiler_params=pltpu.CompilerParams(vmem_limit_bytes=limit(8, 0)),
+        compiler_params=pltpu.CompilerParams(vmem_limit_bytes=grant),
         **kw,
     )(*args)
 
@@ -101,28 +103,49 @@
     row_tiles = own_rows * n_col // TILE
     piece_tiles = src_rows // TILE
     col_tiles = piece_tiles * n_row
-    per_tile = TILE // own_rows
     hp = up8(2 * heads)
     mdp = up8(2 * heads)
     att_src2, att_dst2, bias2 = (v.reshape(1, width) for v in (att_src, att_dst, bias))
 
-    rows = src_rows + own_rows
-
-    def send_kernel(src_ref, dst_ref, proj_ref, *outs):
+    def send_kernel(*refs):
+        hbm, outs, refs = refs[:4], refs[4:-5], refs[-5:]
+        sems, refs = refs[4], refs[:4]
+        copies = [pltpu.make_async_copy(h, v, sems.at[k]) for k, (h, v) in enumerate(zip(hbm, refs))]
+        for copy in copies:
+            copy.start()
+        for copy in copies:
+            copy.wait()
+        src_ref, dst_ref, proj_ref, att_ref = refs
         me = lax.axis_index("feat")
+        outs[0][...] = project(dst_ref[...], take_cols(proj_ref, me, width))
+        outs[1][...] = LOG2E * head_rows(att_ref[...], heads, width, up8(heads))
         for d in range(1, n_feat):
             w = take_cols(proj_ref, goes_to(me, d, n_feat), width)
-            outs[d - 1][:src_rows] = project(src_ref[...], w)
-            outs[d - 1][src_rows:] = project(dst_ref[...], w)
-
-    sent = call(
+            outs[2 * d][...] = project(dst_ref[...], w)
+            outs[2 * d + 1][...] = project(src_ref[...], w)
+
+    inputs = (src_feats, dst_feats, proj, att_dst2)
+    dst_own, att_rows, *sent = call(
         send_kernel,
-        [jax.ShapeDtypeStruct((rows, width), F32)] * (n_feat - 1),
-        src_feats,
-        dst_feats,
-        proj,
-    )
-    parts = [hop(sent[d - 1], "feat", d) for d in range(1, n_feat)]
+        [
+            jax.ShapeDtypeStruct((own_rows, width), F32),
+            jax.ShapeDtypeStruct((up8(heads), width), F32),
+        ]
+        + [
+            jax.ShapeDtypeStruct((n, width), F32)
+            for _ in range(1, n_feat)
+            for n in (own_rows, src_rows)
+        ],
+        *inputs,
+        in_specs=[HBM] * len(inputs),
+        scratch_shapes=[
+            *(pltpu.VMEM(v.shape, v.dtype) for v in inputs),
+            pltpu.SemaphoreType.DMA((len(inputs),)),
+        ],
+        grant=ALL_VMEM,
+    )
+    dst_parts = [hop(sent[2 * d - 2], "feat", d) for d in range(1, n_feat)]
+    src_parts = [hop(sent[2 * d - 1], "feat", d) for d in range(1, n_feat)]
 
     half = col_tiles // 2
     tiles = row_tiles * col_tiles
@@ -162,63 +185,69 @@
                 far_ref[r, q - half] = far_ref[r, q - half] + total
 
     panel_shape = (row_tiles, half, TILE, TILE)
-    whole = lambda shape: pl.BlockSpec(shape, lambda s: (0,) * len(shape))
+    whole = lambda shape: pl.BlockSpec(shape, lambda s, *_: (0,) * len(shape))
     panels = pl.pallas_call(
         weight_kernel,
         out_shape=[jax.ShapeDtypeStruct(panel_shape, F32)] * 2,
-        grid=(period // group,),
-        in_specs=[
-            SMEM,
-            SMEM,
-            SMEM,
-            pl.BlockSpec((reps, group, TILE, TILE), lambda s: (0, s, 0, 0)),
-        ],
-        out_specs=[whole(panel_shape)] * 2,
-        compiler_params=pltpu.CompilerParams(vmem_limit_bytes=limit(32, 8 * tiles * TILE * TILE)),
+        grid_spec=pltpu.PrefetchScalarGridSpec(
+            num_scalar_prefetch=3,
+            grid=(period // group,),
+            in_specs=[pl.BlockSpec((reps, group, TILE, TILE), lambda s, *_: (0, s, 0, 0))],
+            out_specs=[whole(panel_shape)] * 2,
+        ),
+        compiler_params=pltpu.CompilerParams(vmem_limit_bytes=60 << 20),
         cost_estimate=pl.CostEstimate(
             flops=slots * TILE * TILE, bytes_accessed=slots * TILE * TILE * 2, transcendentals=0
         ),
     )(tile_rows, tile_cols, tile_count, edge_weight.reshape(reps, period, TILE, TILE))
-    tied = lax.optimization_barrier((*parts, *panels))
-    parts, panels = tied[: n_feat - 1], tied[n_feat - 1 :]
+    dst_parts, panels = lax.optimization_barrier((dst_parts, panels))
+
+    def dst_kernel(own_ref, att_ref, *rest):
+        got, (z_ref, s_ref) = rest[: n_feat - 1], rest[n_feat - 1 :]
+        z = own_ref[...]
+        for part in got:
+            z = z + part[...]
+        z_ref[...] = z
+        s_ref[...] = contract(att_ref[...], z, ((1,), (1,)))
+
+    zdst, s_dst = call(
+        dst_kernel,
+        [
+            jax.ShapeDtypeStruct((own_rows, width), F32),
+            jax.ShapeDtypeStruct((up8(heads), own_rows), F32),
+        ],
+        dst_own,
+        att_rows,
+        *dst_parts,
+    )
+    targets = [hop(s_dst, "col", d) for d in range(n_col - 1, 0, -1)]
+    targets = [s_dst] + targets[::-1]
+    src_parts, targets = lax.optimization_barrier((src_parts, targets))
 
     pack_rows = src_rows + piece_tiles * hp
 
-    def z_kernel(src_ref, dst_ref, proj_ref, att_src_ref, att_dst_ref, *rest):
-        got, (out_ref, z_ref, s_ref) = rest[: n_feat - 1], rest[n_feat - 1 :]
-        w = take_cols(proj_ref, lax.axis_index("feat"), width)
-        z = project(src_ref[...], w)
-        zdst = project(dst_ref[...], w)
+    def z_kernel(src_ref, proj_ref, att_ref, *rest):
+        got, out_ref = rest[: n_feat - 1], rest[n_feat - 1]
+        z = project(src_ref[...], take_cols(proj_ref, lax.axis_index("feat"), width))
         for part in got:
-            z = z + part[:src_rows]
-            zdst = zdst + part[src_rows:]
+            z = z + part[...]
         if width < lanes:
             out_ref[...] = jnp.zeros_like(out_ref)
         out_ref[:src_rows, :width] = z
-        s = LOG2E * contract(head_rows(att_src_ref[...], heads, width, hp), z, ((1,), (1,)))
+        s = LOG2E * contract(head_rows(att_ref[...], heads, width, hp), z, ((1,), (1,)))
         low = lax.broadcasted_iota(jnp.int32, s.shape, 0) < heads
         s = jnp.where(low, s, SLOPE * s)
         for t in range(piece_tiles):
             at = src_rows + t * hp
             out_ref[at : at + hp, :TILE] = s[:, t * TILE : (t + 1) * TILE]
-        z_ref[...] = zdst
-        s_ref[...] = LOG2E * contract(
-            head_rows(att_dst_ref[...], heads, width, up8(heads)), zdst, ((1,), (1,))
-        )
-
-    own_piece, zdst, s_dst = call(
+
+    own_piece = call(
         z_kernel,
-        [
-            jax.ShapeDtypeStruct((pack_rows, lanes), F32),
-            jax.ShapeDtypeStruct((own_rows, width), F32),
-            jax.ShapeDtypeStruct((up8(heads), own_rows), F32),
-        ],
+        jax.ShapeDtypeStruct((pack_rows, lanes), F32),
         src_feats,
-        dst_feats,
         proj,
         att_src2,
-        att_dst2,
-        *parts,
+        *src_parts,
     )
     far0 = hop(own_piece, "row", n_row // 2)
 
@@ -232,8 +261,6 @@
         return [pieces[k] for k in range(n_row // 2)]
 
     near_pieces = spread(own_piece)
-    targets = [s_dst] + [hop(s_dst, "col", d) for d in range(1, n_col)]
-    far_pieces = spread(far0)
 
     block = 64
     blocks = TILE // block
@@ -245,7 +272,7 @@
     all_rows = row_tiles * TILE
     tiny = 2.0**-60
 
-    def attend(refs, tgt, piece_refs, w_ref, z_cat, probs, num_ref, md_ref):
+    def attend(tgt, piece_refs, w_ref, z_cat, probs, num_ref, md_ref):
         step = pl.program_id(0)
 
         def score_rows(q, h):
@@ -263,7 +290,7 @@
         lane_w = lax.broadcasted_iota(jnp.int32, (block, width), 1) // dims
         lane_t = lax.broadcasted_iota(jnp.int32, (block, TILE), 1)
 
-        def put(at, h, q, p, slot):
+        def put(h, q, p, slot):
             cols = slice(q * TILE, (q + 1) * TILE)
             hi = p.astype(BF16)
             lo = (p - hi.astype(F32)).astype(BF16)
@@ -304,7 +331,7 @@
                         jnp.maximum(pos + s, neg + s_low)
                     )
                     den = den + p
-                    put(at, h, q, p, b % 2)
+                    put(h, q, p, b % 2)
                 den = jnp.sum(den, axis=1, keepdims=True)
                 worst = den if worst is None else jnp.minimum(worst, den)
                 dens.append(den)
@@ -335,7 +362,7 @@
                         x = jnp.maximum(pos + s, neg + s_low)
                         p = w_ref[rt, q, pl.ds(i0, block), :] * jnp.exp2(jnp.minimum(x, 0.0))
                         den = den + p
-                        put(at, h, q, p, 0)
+                        put(h, q, p, 0)
                     dens.append(jnp.sum(den, axis=1, keepdims=True))
                     ms.append(m)
                 finish(at, 0, dens, ms)
@@ -365,7 +392,7 @@
                 tgt[pl.ds(at, own_rows), :] = contract(tgt_refs[d][...], eye, ((0,), (0,)))
             split_z(piece_refs, z_cat)
 
-        attend(refs, tgt, piece_refs, w_ref, z_cat, probs, num_ref, md_ref)
+        attend(tgt, piece_refs, w_ref, z_cat, probs, num_ref, md_ref)
 
     def far_kernel(*refs):
         tgt, near_num, near_md, refs = refs[0], refs[1], refs[2], refs[3:]
@@ -379,7 +406,7 @@
         def _():
             split_z(piece_refs, z_cat)
 
-        attend(refs, tgt, piece_refs, w_ref, z_cat, probs, num_ref, md_ref)
+        attend(tgt, piece_refs, w_ref, z_cat, probs, num_ref, md_ref)
 
         base = step * group_rows
         lane_w = lax.broadcasted_iota(jnp.int32, (TILE, width), 1) // dims
@@ -436,6 +463,8 @@
         cost_estimate=cost,
         compiler_params=params,
     )(*targets, *near_pieces, panels[0])
+    far0, tgt, near_num, near_md = lax.optimization_barrier((far0, tgt, near_num, near_md))
+    far_pieces = spread(far0)
     chunk = (chunk_rows, lanes)
     chunks = pl.pallas_call(
         far_kernel,
@@ -449,7 +478,8 @@
         cost_estimate=cost,
         compiler_params=params,
     )(tgt, near_num, near_md, *far_pieces, panels[1])
-    gathered = [chunks[0]] + [hop(chunks[d], "col", d) for d in range(1, n_col)]
+    gathered = [hop(chunks[d], "col", d) for d in range(n_col - 1, 0, -1)]
+    gathered = [chunks[0]] + gathered[::-1]
 
     def out_kernel(zdst_ref, src_ref, dst_ref, bias_ref, *rest):
         parts, out_ref = rest[:n_col], rest[n_col]

time: 54.4 us -> 50.5 us (0.928)
  Pallas kernels: 19.8 us -> 24.9 us
  local copies, waits for them, and re-layouts: 5.98 us -> 1.27 us
  waiting for transfers between devices: 13.9 us -> 9.48 us
    unnamed x24 -> x18, local copies, waits for them, and re-layouts: 5.98 us -> 1.27 us
    ppermute x10 -> x11, waiting for transfers between devices: 13.9 us -> 9.48 us  [hop(): return lax.ppermute(x, axis, pairs)]
    pallas_call x1, Pallas kernels: 2.47 us -> 5.79 us  [on_device(): pl.pallas_call(weight_kernel, out_shape=[jax.ShapeDtypeStruct(panel_shape...]
    pallas_call x3 -> x4, Pallas kernels: 1.79 us -> 3.56 us  [call(): pl.pallas_call(kernel, out_shape=out_shape, in_specs=in_specs or [VMEM] *...]
    ppermute x10 -> x11, starting transfers between devices: 13.6 us -> 13.8 us  [hop(): return lax.ppermute(x, axis, pairs)]
  transfers between devices with their start and end apart: 10 -> 11, of which waited for: 6 -> 6; matrix products, arithmetic and copies ran while one was open for 0% -> 0% of each run, Pallas kernels for 18% -> 26%
where the time goes in v3:
time: 50.5 us; the launch traced here: 50.2 us
  Pallas kernels  24.9 us (49%)
  starting transfers between devices  13.8 us (27%)
  waiting for transfers between devices  9.48 us (19%)
  local copies, waits for them, and re-layouts  1.27 us (3%)
  between operations  0.77 us (2%)
    ppermute x11, starting transfers between devices, hop(): return lax.ppermute(x, axis, pairs)  13.8 us
    ppermute x11, waiting for transfers between devices, hop(): return lax.ppermute(x, axis, pairs)  9.48 us
    pallas_call x1, Pallas kernels, on_device(): pl.pallas_call(far_kernel, out_shape=[jax.ShapeDtypeStruct(chunk, F32)] *...  8.19 us
    pallas_call x1, Pallas kernels, on_device(): pl.pallas_call(near_kernel, out_shape=[jax.ShapeDtypeStruct(s, F32) for s...  7.34 us
    pallas_call x1, Pallas kernels, on_device(): pl.pallas_call(weight_kernel, out_shape=[jax.ShapeDtypeStruct(panel_shape...  5.79 us
    pallas_call x4, Pallas kernels, call(): pl.pallas_call(kernel, out_shape=out_shape, in_specs=in_specs or [VMEM] *...  3.56 us
    unnamed x18, local copies, waits for them, and re-layouts  1.27 us
  transfers between devices with their start and end apart: 11, of which 6 were waited for; matrix products, arithmetic and copies ran while one was open for 0% of the time, Pallas kernels for 26%

profile of v3, /device:TPU:0, one launch (start us, length us, event | category | flops | bytes accessed | tf_op | source)
XLA Modules:
  0.0 50.2 jit_solution(3945978280196333486)
XLA Ops:
  0.0 1.9 %shard_map.100 = (f32[64,128]{1,0:T(8,128)}, f32[8,128]{1,0:T(8,128)}, f32[64,128]{1,0:T(8,128)}, f32[512,128]{1,0:T(8,128)}) custom-call(bf16[512,128]{1,0:T(8,128)(2,1)} %src_ref.1, bf16[64,128]{1,0:T(8,128)(2,1)} %refs_1_.1, bf16[128,256]{1,0:T(8,128)(2,1)} %proj_ref.1, f32[1,128]{1,0:T(1,128)} %bitcast.4), custom_call_target="tpu_custom_call" | custom-call | tf_op jit(solution)/shard_map/pallas_call | solution.py:41
  1.9 0.0 copy-start.3
  1.9 0.0 copy-start
  1.9 0.0 copy-start.1
  1.9 0.0 copy-start.5
  1.9 3.0 %collective-permute-start.1 = (f32[512,128]{1,0:T(8,128)}, f32[512,128]{1,0:T(8,128)S(1)}, u32[]{:S(2)}, u32[]{:S(2)}) collective-permute-start(f32[512,128]{1,0:T(8,128)} %get-tuple-element.39), channel_id=1, source_target_pairs={{0,1},{1,0},{2,3},{3,2},{4,5},{5,4},{6,7},{7,6},{8,9},{9,8},{10,11... | collective-permute-start | bytes 786440 | tf_op jit(solution)/shard_map/ppermute | solution.py:37
  5.0 0.1 collective-permute-start
  5.7 5.8 %shard_map.101 = (f32[2,8,128,128]{3,2,1,0:T(8,128)}, f32[2,8,128,128]{3,2,1,0:T(8,128)}) custom-call(s32[1,1,128]{2,1,0:T(1,128)} %rows_ref.1, s32[1,1,128]{2,1,0:T(1,128)} %cols_ref.1, s32[1,1]{1,0:T(1,128)S(6)} %copy.11.count_ref, bf16[4,32,128,128]{3,2,1,0:T(8,128)(2,1)} %bitcast.9), custom_call_target="tpu_custom_call" | custom-call | flops 2097152 | bytes 4194304 | tf_op jit(solution)/shard_map/pallas_call | solution.py:189
  11.5 0.7 %collective-permute-done.rest_0_ = f32[64,128]{1,0:T(8,128)S(1)} collective-permute-done((f32[64,128]{1,0:T(8,128)}, f32[64,128]{1,0:T(8,128)S(1)}, u32[]{:S(2)}, u32[]{:S(2)}) %collective-permute-start) | collective-permute-done | bytes 32800 | tf_op jit(solution)/shard_map/ppermute | solution.py:37
  12.2 0.1 shard_map.102
  12.3 3.9 %collective-permute-start.4 = (f32[8,64]{1,0:T(8,128)S(1)}, f32[8,64]{1,0:T(8,128)S(1)}, u32[]{:S(2)}, u32[]{:S(2)}) collective-permute-start(f32[8,64]{1,0:T(8,128)S(1)} %get-tuple-element.42.refs_0_), channel_id=1, source_target_pairs={{0,6},{2,4},{4,2},{6,0},{1,7},{3,5},{5,3},{7,1},{8,14},{10,12},{12... | collective-permute-start | bytes 6152 | tf_op jit(solution)/shard_map/ppermute | solution.py:37
  16.2 0.0 collective-permute-start.3
  16.2 0.6 %collective-permute-start.2 = (f32[8,64]{1,0:T(8,128)S(1)}, f32[8,64]{1,0:T(8,128)S(1)}, u32[]{:S(2)}, u32[]{:S(2)}) collective-permute-start(f32[8,64]{1,0:T(8,128)S(1)} %get-tuple-element.42.refs_0_), channel_id=1, source_target_pairs={{0,2},{2,0},{4,6},{6,4},{1,3},{3,1},{5,7},{7,5},{8,10},{10,8},{12,... | collective-permute-start | bytes 6152 | tf_op jit(solution)/shard_map/ppermute | solution.py:37
  16.8 1.0 %collective-permute-done.4.refs_3_ = f32[8,64]{1,0:T(8,128)S(1)} collective-permute-done((f32[8,64]{1,0:T(8,128)S(1)}, f32[8,64]{1,0:T(8,128)S(1)}, u32[]{:S(2)}, u32[]{:S(2)}) %collective-permute-start.4) | collective-permute-done | bytes 2080 | tf_op jit(solution)/shard_map/ppermute | solution.py:37
  17.8 2.9 %collective-permute-done.3.refs_2_ = f32[8,64]{1,0:T(8,128)S(1)} collective-permute-done((f32[8,64]{1,0:T(8,128)S(1)}, f32[8,64]{1,0:T(8,128)S(1)}, u32[]{:S(2)}, u32[]{:S(2)}) %collective-permute-start.3) | collective-permute-done | bytes 2080 | tf_op jit(solution)/shard_map/ppermute | solution.py:37
  20.7 0.0 collective-permute-done.2.refs_1_
  20.7 0.0 copy-start.4
  20.8 0.0 copy-start.6
  20.8 0.5 shard_map.103.refs_4_
  21.2 1.6 %collective-permute-start.5 = (f32[544,128]{1,0:T(8,128)S(1)}, f32[544,128]{1,0:T(8,128)S(1)}, u32[]{:S(2)}, u32[]{:S(2)}) collective-permute-start(f32[544,128]{1,0:T(8,128)S(1)} %shard_map.103.refs_4_), channel_id=1, source_target_pairs={{0,16},{8,24},{16,0},{24,8},{1,17},{9,25},{17,1},{25,9},{2,18},{10... | collective-permute-start | bytes 835592 | tf_op jit(solution)/shard_map/ppermute | solution.py:37
  22.8 0.0 collective-permute-done.6.refs_5_
  22.8 1.2 %copy-done.8 = f32[2,8,128,128]{3,2,1,0:T(8,128)S(1)} copy-done((f32[2,8,128,128]{3,2,1,0:T(8,128)S(1)}, f32[2,8,128,128]{3,2,1,0:T(8,128)}, u32[]{:S(2)}) %copy-start.8) | copy-done | bytes 1048600
  24.1 7.3 %shard_map.104 = (f32[256,128]{1,0:T(8,128)S(1)}, f32[256,128]{1,0:T(8,128)S(1)}, f32[256,128]{1,0:T(8,128)S(1)}) custom-call(f32[8,64]{1,0:T(8,128)S(1)} %get-tuple-element.42.refs_0_, f32[8,64]{1,0:T(8,128)S(1)} %collective-permute-done.2.refs_1_, f32[8,64]{1,0:T(8,128)S(1)} %collective-permute-done.3.refs_2_, f32[8,64]{1,0:T(8,128)S(1)} %collective-permute-done.4.refs_3_, ...), custom_call_target="tpu_custom_call" | custom-call | flops 1073741824 | bytes 524288 | tf_op jit(solution)/shard_map/pallas_call | solution.py:454
  31.4 0.3 collective-permute-start.7
  31.7 1.4 %collective-permute-done.7.refs_4_ = f32[544,128]{1,0:T(8,128)S(1)} collective-permute-done((f32[544,128]{1,0:T(8,128)S(1)}, f32[544,128]{1,0:T(8,128)S(1)}, u32[]{:S(2)}, u32[]{:S(2)}) %collective-permute-start.7) | collective-permute-done | bytes 278560 | tf_op jit(solution)/shard_map/ppermute | solution.py:37
  33.0 8.2 %shard_map.105 = (f32[72,128]{1,0:T(8,128)S(1)}, f32[72,128]{1,0:T(8,128)S(1)}, f32[72,128]{1,0:T(8,128)S(1)}, f32[72,128]{1,0:T(8,128)S(1)}) custom-call(f32[256,128]{1,0:T(8,128)S(1)} %get-tuple-element.50.refs_0_, f32[256,128]{1,0:T(8,128)S(1)} %get-tuple-element.51.refs_1_, f32[256,128]{1,0:T(8,128)S(1)} %get-tuple-element.52.refs_2_, ...), custom_call_target="tpu_custom_call" | custom-call | flops 1073741824 | bytes 524288 | tf_op jit(solution)/shard_map/pallas_call | solution.py:469
  41.2 0.0 collective-permute-start.8
  41.3 2.1 %collective-permute-start.9 = (f32[72,128]{1,0:T(8,128)S(1)}, f32[72,128]{1,0:T(8,128)S(1)}, u32[]{:S(2)}, u32[]{:S(2)}) collective-permute-start(f32[72,128]{1,0:T(8,128)S(1)} %get-tuple-element.57), channel_id=1, source_target_pairs={{0,4},{2,6},{4,0},{6,2},{1,5},{3,7},{5,1},{7,3},{8,12},{10,14},{12... | collective-permute-start | bytes 110600 | tf_op jit(solution)/shard_map/ppermute | solution.py:37
  43.4 2.3 %collective-permute-start.10 = (f32[72,128]{1,0:T(8,128)S(1)}, f32[72,128]{1,0:T(8,128)S(1)}, u32[]{:S(2)}, u32[]{:S(2)}) collective-permute-start(f32[72,128]{1,0:T(8,128)S(1)} %get-tuple-element.58), channel_id=1, source_target_pairs={{0,6},{2,4},{4,2},{6,0},{1,7},{3,5},{5,3},{7,1},{8,14},{10,12},{12... | collective-permute-start | bytes 110600 | tf_op jit(solution)/shard_map/ppermute | solution.py:37
  45.7 0.6 %collective-permute-done.9.rest_2_ = f32[72,128]{1,0:T(8,128)S(1)} collective-permute-done((f32[72,128]{1,0:T(8,128)S(1)}, f32[72,128]{1,0:T(8,128)S(1)}, u32[]{:S(2)}, u32[]{:S(2)}) %collective-permute-start.9) | collective-permute-done | bytes 36896 | tf_op jit(solution)/shard_map/ppermute | solution.py:37
  46.2 2.9 %collective-permute-done.10.rest_3_ = f32[72,128]{1,0:T(8,128)S(1)} collective-permute-done((f32[72,128]{1,0:T(8,128)S(1)}, f32[72,128]{1,0:T(8,128)S(1)}, u32[]{:S(2)}, u32[]{:S(2)}) %collective-permute-start.10) | collective-permute-done | bytes 36896 | tf_op jit(solution)/shard_map/ppermute | solution.py:37
  49.1 1.1 %shard_map.106 = bf16[64,128]{1,0:T(8,128)(2,1)} custom-call(f32[64,128]{1,0:T(8,128)S(1)} %get-tuple-element.38.zdst_ref, f32[1,128]{1,0:T(1,128)S(1)} %bitcast.7, f32[1,128]{1,0:T(1,128)S(1)} %bitcast.5, f32[1,128]{1,0:T(1,128)S(1)} %bitcast.8, f32[72,128]{1,0:T(8,128)S(1)} %get-tuple-element.55.rest_0_, f32[72,128]{1,0:T(8,128)S(1)} %collective-permute-done.8.rest_1_, ...), custom_call_target="tpu_custom_call" | custom-call | tf_op jit(solution)/shard_map/pallas_call | solution.py:41
  (15 shorter events, 0.0 us)
Async XLA Ops:
  1.9 10.3 %copy-start.2 = (f32[64,128]{1,0:T(8,128)S(1)}, f32[64,128]{1,0:T(8,128)}, u32[]{:S(2)}) copy-start(f32[64,128]{1,0:T(8,128)} %get-tuple-element.32.own_ref) | copy-start | bytes 98308
  1.9 10.3 %copy-start.3 = (f32[8,128]{1,0:T(8,128)S(1)}, f32[8,128]{1,0:T(8,128)}, u32[]{:S(2)}) copy-start(f32[8,128]{1,0:T(8,128)} %get-tuple-element.33.att_ref) | copy-start | bytes 12292
  1.9 18.8 %copy-start = (bf16[512,128]{1,0:T(8,128)(2,1)S(1)}, bf16[512,128]{1,0:T(8,128)(2,1)}, u32[]{:S(2)}) copy-start(bf16[512,128]{1,0:T(8,128)(2,1)} %src_ref.1) | copy-start | bytes 393220
  1.9 18.8 %copy-start.1 = (bf16[128,256]{1,0:T(8,128)(2,1)S(1)}, bf16[128,256]{1,0:T(8,128)(2,1)}, u32[]{:S(2)}) copy-start(bf16[128,256]{1,0:T(8,128)(2,1)} %proj_ref.1) | copy-start | bytes 196612
  1.9 18.8 %copy-start.5 = (f32[128]{0:T(128)S(1)}, f32[128]{0:T(128)}, u32[]{:S(2)}) copy-start(f32[128]{0:T(128)} %param.13) | copy-start | bytes 1540
  1.9 18.8 %collective-permute-start.1 = (f32[512,128]{1,0:T(8,128)}, f32[512,128]{1,0:T(8,128)S(1)}, u32[]{:S(2)}, u32[]{:S(2)}) collective-permute-start(f32[512,128]{1,0:T(8,128)} %get-tuple-element.39), channel_id=1, source_target_pairs={{0,1},{1,0},{2,3},{3,2},{4,5},{5,4},{6,7},{7,6},{8,9},{9,8},{10,11... | collective-permute-start | bytes 786440 | tf_op jit(solution)/shard_map/ppermute | solution.py:37
  5.0 7.2 %collective-permute-start = (f32[64,128]{1,0:T(8,128)}, f32[64,128]{1,0:T(8,128)S(1)}, u32[]{:S(2)}, u32[]{:S(2)}) collective-permute-start(f32[64,128]{1,0:T(8,128)} %get-tuple-element.34), channel_id=1, source_target_pairs={{0,1},{1,0},{2,3},{3,2},{4,5},{5,4},{6,7},{7,6},{8,9},{9,8},{10,11... | collective-permute-start | bytes 98312 | tf_op jit(solution)/shard_map/ppermute | solution.py:37
  11.5 21.6 %copy-start.7 = (f32[2,8,128,128]{3,2,1,0:T(8,128)S(1)}, f32[2,8,128,128]{3,2,1,0:T(8,128)}, u32[]{:S(2)}) copy-start(f32[2,8,128,128]{3,2,1,0:T(8,128)} %get-tuple-element.54.refs_5_) | copy-start | bytes 3145732
  12.3 5.5 %collective-permute-start.4 = (f32[8,64]{1,0:T(8,128)S(1)}, f32[8,64]{1,0:T(8,128)S(1)}, u32[]{:S(2)}, u32[]{:S(2)}) collective-permute-start(f32[8,64]{1,0:T(8,128)S(1)} %get-tuple-element.42.refs_0_), channel_id=1, source_target_pairs={{0,6},{2,4},{4,2},{6,0},{1,7},{3,5},{5,3},{7,1},{8,14},{10,12},{12... | collective-permute-start | bytes 6152 | tf_op jit(solution)/shard_map/ppermute | solution.py:37
  16.2 4.5 %collective-permute-start.3 = (f32[8,64]{1,0:T(8,128)S(1)}, f32[8,64]{1,0:T(8,128)S(1)}, u32[]{:S(2)}, u32[]{:S(2)}) collective-permute-start(f32[8,64]{1,0:T(8,128)S(1)} %get-tuple-element.42.refs_0_), channel_id=1, source_target_pairs={{0,4},{2,6},{4,0},{6,2},{1,5},{3,7},{5,1},{7,3},{8,12},{10,14},{12... | collective-permute-start | bytes 6152 | tf_op jit(solution)/shard_map/ppermute | solution.py:37
  16.2 4.5 %collective-permute-start.2 = (f32[8,64]{1,0:T(8,128)S(1)}, f32[8,64]{1,0:T(8,128)S(1)}, u32[]{:S(2)}, u32[]{:S(2)}) collective-permute-start(f32[8,64]{1,0:T(8,128)S(1)} %get-tuple-element.42.refs_0_), channel_id=1, source_target_pairs={{0,2},{2,0},{4,6},{6,4},{1,3},{3,1},{5,7},{7,5},{8,10},{10,8},{12,... | collective-permute-start | bytes 6152 | tf_op jit(solution)/shard_map/ppermute | solution.py:37
  20.7 28.4 %copy-start.4 = (f32[128]{0:T(128)S(1)}, f32[128]{0:T(128)}, u32[]{:S(2)}) copy-start(f32[128]{0:T(128)} %param.14) | copy-start | bytes 1540
  20.8 28.4 %copy-start.6 = (f32[128]{0:T(128)S(1)}, f32[128]{0:T(128)}, u32[]{:S(2)}) copy-start(f32[128]{0:T(128)} %param.15) | copy-start | bytes 1540
  21.2 1.6 %collective-permute-start.6 = (f32[544,128]{1,0:T(8,128)S(1)}, f32[544,128]{1,0:T(8,128)S(1)}, u32[]{:S(2)}, u32[]{:S(2)}) collective-permute-start(f32[544,128]{1,0:T(8,128)S(1)} %shard_map.103.refs_4_), channel_id=1, source_target_pairs={{0,8},{8,0},{16,24},{24,16},{1,9},{9,1},{17,25},{25,17},{2,10},{10... | collective-permute-start | bytes 835592 | tf_op jit(solution)/shard_map/ppermute | solution.py:37
  21.2 10.2 %collective-permute-start.5 = (f32[544,128]{1,0:T(8,128)S(1)}, f32[544,128]{1,0:T(8,128)S(1)}, u32[]{:S(2)}, u32[]{:S(2)}) collective-permute-start(f32[544,128]{1,0:T(8,128)S(1)} %shard_map.103.refs_4_), channel_id=1, source_target_pairs={{0,16},{8,24},{16,0},{24,8},{1,17},{9,25},{17,1},{25,9},{2,18},{10... | collective-permute-start | bytes 835592 | tf_op jit(solution)/shard_map/ppermute | solution.py:37
  22.8 1.2 %copy-start.8 = (f32[2,8,128,128]{3,2,1,0:T(8,128)S(1)}, f32[2,8,128,128]{3,2,1,0:T(8,128)}, u32[]{:S(2)}) copy-start(f32[2,8,128,128]{3,2,1,0:T(8,128)} %get-tuple-element.46.refs_6_) | copy-start | bytes 3145732
  31.4 1.6 %collective-permute-start.7 = (f32[544,128]{1,0:T(8,128)S(1)}, f32[544,128]{1,0:T(8,128)S(1)}, u32[]{:S(2)}, u32[]{:S(2)}) collective-permute-start(f32[544,128]{1,0:T(8,128)S(1)} %collective-permute-done.5.refs_3_), channel_id=1, source_target_pairs={{0,8},{8,0},{16,24},{24,16},{1,9},{9,1},{17,25},{25,17},{2,10},{10... | collective-permute-start | bytes 835592 | tf_op jit(solution)/shard_map/ppermute | solution.py:37
  41.2 4.4 %collective-permute-start.8 = (f32[72,128]{1,0:T(8,128)S(1)}, f32[72,128]{1,0:T(8,128)S(1)}, u32[]{:S(2)}, u32[]{:S(2)}) collective-permute-start(f32[72,128]{1,0:T(8,128)S(1)} %get-tuple-element.56), channel_id=1, source_target_pairs={{0,2},{2,0},{4,6},{6,4},{1,3},{3,1},{5,7},{7,5},{8,10},{10,8},{12,... | collective-permute-start | bytes 110600 | tf_op jit(solution)/shard_map/ppermute | solution.py:37
  41.3 4.9 %collective-permute-start.9 = (f32[72,128]{1,0:T(8,128)S(1)}, f32[72,128]{1,0:T(8,128)S(1)}, u32[]{:S(2)}, u32[]{:S(2)}) collective-permute-start(f32[72,128]{1,0:T(8,128)S(1)} %get-tuple-element.57), channel_id=1, source_target_pairs={{0,4},{2,6},{4,0},{6,2},{1,5},{3,7},{5,1},{7,3},{8,12},{10,14},{12... | collective-permute-start | bytes 110600 | tf_op jit(solution)/shard_map/ppermute | solution.py:37
  43.4 5.8 %collective-permute-start.10 = (f32[72,128]{1,0:T(8,128)S(1)}, f32[72,128]{1,0:T(8,128)S(1)}, u32[]{:S(2)}, u32[]{:S(2)}) collective-permute-start(f32[72,128]{1,0:T(8,128)S(1)} %get-tuple-element.58), channel_id=1, source_target_pairs={{0,6},{2,4},{4,2},{6,0},{1,7},{3,5},{5,3},{7,1},{8,14},{10,12},{12... | collective-permute-start | bytes 110600 | tf_op jit(solution)/shard_map/ppermute | solution.py:37

commit v4 on v3

--- a/solution.py
+++ b/solution.py
@@ -12,7 +12,6 @@
 NEG = -1e30
 F32 = jnp.float32
 BF16 = jnp.bfloat16
-ALL_VMEM = 67043328
 HIGHEST = lax.Precision.HIGHEST
 VMEM = pl.BlockSpec(memory_space=pltpu.VMEM)
 SMEM = pl.BlockSpec(memory_space=pltpu.SMEM)
@@ -52,6 +51,10 @@
 
 def limit(mib, least):
     return min(max(mib << 20, least), 60 << 20)
+
+
+def in_hbm(x):
+    return pltpu.with_memory_space_constraint(x, pltpu.HBM)
 
 
 def up8(n):
@@ -107,100 +110,73 @@
     mdp = up8(2 * heads)
     att_src2, att_dst2, bias2 = (v.reshape(1, width) for v in (att_src, att_dst, bias))
 
-    def send_kernel(*refs):
-        hbm, outs, refs = refs[:4], refs[4:-5], refs[-5:]
-        sems, refs = refs[4], refs[:4]
-        copies = [pltpu.make_async_copy(h, v, sems.at[k]) for k, (h, v) in enumerate(zip(hbm, refs))]
+    def fetch(hbm, vmem, sems):
+        copies = [pltpu.make_async_copy(h, v, sems.at[k]) for k, (h, v) in enumerate(zip(hbm, vmem))]
         for copy in copies:
             copy.start()
         for copy in copies:
             copy.wait()
-        src_ref, dst_ref, proj_ref, att_ref = refs
+
+    def fetching(kernel, outs, *args):
+        return call(
+            kernel,
+            outs,
+            *map(in_hbm, args),
+            in_specs=[HBM] * len(args),
+            scratch_shapes=[
+                *(pltpu.VMEM(v.shape, v.dtype) for v in args),
+                pltpu.SemaphoreType.DMA((len(args),)),
+            ],
+        )
+
+    def send_kernel(*refs):
+        hbm, outs, (src_ref, dst_ref, proj_ref, sems) = refs[:3], refs[3:-4], refs[-4:]
+        fetch(hbm, (src_ref, dst_ref, proj_ref), sems)
         me = lax.axis_index("feat")
-        outs[0][...] = project(dst_ref[...], take_cols(proj_ref, me, width))
-        outs[1][...] = LOG2E * head_rows(att_ref[...], heads, width, up8(heads))
         for d in range(1, n_feat):
             w = take_cols(proj_ref, goes_to(me, d, n_feat), width)
-            outs[2 * d][...] = project(dst_ref[...], w)
-            outs[2 * d + 1][...] = project(src_ref[...], w)
-
-    inputs = (src_feats, dst_feats, proj, att_dst2)
-    dst_own, att_rows, *sent = call(
+            outs[2 * d - 2][...] = project(dst_ref[...], w)
+            outs[2 * d - 1][...] = project(src_ref[...], w)
+
+    sent = fetching(
         send_kernel,
-        [
-            jax.ShapeDtypeStruct((own_rows, width), F32),
-            jax.ShapeDtypeStruct((up8(heads), width), F32),
-        ]
-        + [
-            jax.ShapeDtypeStruct((n, width), F32)
-            for _ in range(1, n_feat)
-            for n in (own_rows, src_rows)
-        ],
-        *inputs,
-        in_specs=[HBM] * len(inputs),
-        scratch_shapes=[
-            *(pltpu.VMEM(v.shape, v.dtype) for v in inputs),
-            pltpu.SemaphoreType.DMA((len(inputs),)),
-        ],
-        grant=ALL_VMEM,
+        [pltpu.VMEM((n, width), F32) for _ in range(1, n_feat) for n in (own_rows, src_rows)],
+        src_feats,
+        dst_feats,
+        proj,
     )
     dst_parts = [hop(sent[2 * d - 2], "feat", d) for d in range(1, n_feat)]
     src_parts = [hop(sent[2 * d - 1], "feat", d) for d in range(1, n_feat)]
 
+    def own_kernel(*refs):
+        hbm, outs, refs = refs[:5], refs[5:9], refs[9:]
+        fetch(hbm, refs[:5], refs[5])
+        src_ref, dst_ref, proj_ref, att_src_ref, att_dst_ref = refs[:5]
+        w = take_cols(proj_ref, lax.axis_index("feat"), width)
+        outs[0][...] = project(src_ref[...], w)
+        outs[1][...] = project(dst_ref[...], w)
+        outs[2][...] = LOG2E * head_rows(att_src_ref[...], heads, width, hp)
+        outs[3][...] = LOG2E * head_rows(att_dst_ref[...], heads, width, up8(heads))
+
+    src_own, dst_own, src_att, dst_att = fetching(
+        own_kernel,
+        [
+            pltpu.VMEM((src_rows, width), F32),
+            pltpu.VMEM((own_rows, width), F32),
+            pltpu.VMEM((hp, width), F32),
+            pltpu.VMEM((up8(heads), width), F32),
+        ],
+        src_feats,
+        dst_feats,
+        proj,
+        att_src2,
+        att_dst2,
+    )
+    dst_parts, src_own = lax.optimization_barrier((dst_parts, src_own))
+
     half = col_tiles // 2
     tiles = row_tiles * col_tiles
-    period = min(slots, tiles) if slots % min(slots, tiles) == 0 else slots
-    reps = slots // period
-    group = 8
-
-    def weight_kernel(rows_ref, cols_ref, count_ref, w_ref, near_ref, far_ref):
-        step = pl.program_id(0)
-        row = lax.axis_index("row")
-        count = count_ref[0, 0]
-
-        @pl.when(step == 0)
-        def _():
-            @pl.loop(0, row_tiles * half)
-            def _(t):
-                near_ref[t // half, t % half] = jnp.zeros((TILE, TILE), F32)
-                far_ref[t // half, t % half] = jnp.zeros((TILE, TILE), F32)
-
-        base = step * group
-
-        @pl.loop(0, jnp.clip(count - base, 0, group))
-        def _(u):
-            r, c = rows_ref[0, 0, base + u], cols_ref[0, 0, base + u]
-            q = ((c // piece_tiles) ^ row) * piece_tiles + c % piece_tiles
-            total = w_ref[0, u].astype(F32)
-            for k in range(1, reps):
-                live = (base + u + k * period < count).astype(F32)
-                total = total + w_ref[k, u].astype(F32) * live
-
-            @pl.when(q < half)
-            def _():
-                near_ref[r, q] = near_ref[r, q] + total
-
-            @pl.when(q >= half)
-            def _():
-                far_ref[r, q - half] = far_ref[r, q - half] + total
-
-    panel_shape = (row_tiles, half, TILE, TILE)
-    whole = lambda shape: pl.BlockSpec(shape, lambda s, *_: (0,) * len(shape))
-    panels = pl.pallas_call(
-        weight_kernel,
-        out_shape=[jax.ShapeDtypeStruct(panel_shape, F32)] * 2,
-        grid_spec=pltpu.PrefetchScalarGridSpec(
-            num_scalar_prefetch=3,
-            grid=(period // group,),
-            in_specs=[pl.BlockSpec((reps, group, TILE, TILE), lambda s, *_: (0, s, 0, 0))],
-            out_specs=[whole(panel_shape)] * 2,
-        ),
-        compiler_params=pltpu.CompilerParams(vmem_limit_bytes=60 << 20),
-        cost_estimate=pl.CostEstimate(
-            flops=slots * TILE * TILE, bytes_accessed=slots * TILE * TILE * 2, transcendentals=0
-        ),
-    )(tile_rows, tile_cols, tile_count, edge_weight.reshape(reps, period, TILE, TILE))
-    dst_parts, panels = lax.optimization_barrier((dst_parts, panels))
+    whole = lambda shape: pl.BlockSpec(shape, lambda s: (0,) * len(shape))
 
     def dst_kernel(own_ref, att_ref, *rest):
         got, (z_ref, s_ref) = rest[: n_feat - 1], rest[n_feat - 1 :]
@@ -217,7 +193,7 @@
             jax.ShapeDtypeStruct((up8(heads), own_rows), F32),
         ],
         dst_own,
-        att_rows,
+        dst_att,
         *dst_parts,
     )
     targets = [hop(s_dst, "col", d) for d in range(n_col - 1, 0, -1)]
@@ -226,15 +202,15 @@
 
     pack_rows = src_rows + piece_tiles * hp
 
-    def z_kernel(src_ref, proj_ref, att_ref, *rest):
+    def z_kernel(own_ref, att_ref, *rest):
         got, out_ref = rest[: n_feat - 1], rest[n_feat - 1]
-        z = project(src_ref[...], take_cols(proj_ref, lax.axis_index("feat"), width))
+        z = own_ref[...]
         for part in got:
             z = z + part[...]
         if width < lanes:
             out_ref[...] = jnp.zeros_like(out_ref)
         out_ref[:src_rows, :width] = z
-        s = LOG2E * contract(head_rows(att_ref[...], heads, width, hp), z, ((1,), (1,)))
+        s = contract(att_ref[...], z, ((1,), (1,)))
         low = lax.broadcasted_iota(jnp.int32, s.shape, 0) < heads
         s = jnp.where(low, s, SLOPE * s)
         for t in range(piece_tiles):
@@ -243,13 +219,88 @@
 
     own_piece = call(
         z_kernel,
-        jax.ShapeDtypeStruct((pack_rows, lanes), F32),
-        src_feats,
-        proj,
-        att_src2,
+        pltpu.VMEM((pack_rows, lanes), F32),
+        src_own,
+        src_att,
         *src_parts,
     )
     far0 = hop(own_piece, "row", n_row // 2)
+    own_piece, tile_count = lax.optimization_barrier((own_piece, tile_count))
+
+    period = min(slots, tiles) if slots % min(slots, tiles) == 0 else slots
+    reps = slots // period
+    group = 8
+    groups = period // group
+
+    def weight_kernel(rows_hbm, cols_hbm, count_ref, w_hbm, near_ref, far_ref, *scratch):
+        rows_ref, cols_ref, w_ref, index_sems, w_sems = scratch
+        row = lax.axis_index("row")
+        count = count_ref[0, 0]
+        indices = [
+            pltpu.make_async_copy(rows_hbm, rows_ref, index_sems.at[0]),
+            pltpu.make_async_copy(cols_hbm, cols_ref, index_sems.at[1]),
+        ]
+        blocks = [
+            pltpu.make_async_copy(
+                w_hbm.at[k, pl.ds(g * group, group)],
+                w_ref.at[k, pl.ds(g * group, group)],
+                w_sems.at[g, k],
+            )
+            for g in range(groups)
+            for k in range(reps)
+        ]
+        for copy in indices + blocks:
+            copy.start()
+
+        @pl.loop(0, row_tiles * half)
+        def _(t):
+            near_ref[t // half, t % half] = jnp.zeros((TILE, TILE), F32)
+            far_ref[t // half, t % half] = jnp.zeros((TILE, TILE), F32)
+
+        for copy in indices:
+            copy.wait()
+        for g in range(groups):
+            for copy in blocks[g * reps : (g + 1) * reps]:
+                copy.wait()
+            base = g * group
+
+            @pl.loop(base, jnp.clip(count, base, base + group))
+            def _(u):
+                r, c = rows_ref[0, 0, u], cols_ref[0, 0, u]
+                q = ((c // piece_tiles) ^ row) * piece_tiles + c % piece_tiles
+                total = w_ref[0, u].astype(F32)
+                for k in range(1, reps):
+                    live = (u + k * period < count).astype(F32)
+                    total = total + w_ref[k, u].astype(F32) * live
+
+                @pl.when(q < half)
+                def _():
+                    near_ref[r, q] = near_ref[r, q] + total
+
+                @pl.when(q >= half)
+                def _():
+                    far_ref[r, q - half] = far_ref[r, q - half] + total
+
+    panel_shape = (row_tiles, half, TILE, TILE)
+    panels = call(
+        weight_kernel,
+        [pltpu.VMEM(panel_shape, F32)] * 2,
+        in_hbm(tile_rows),
+        in_hbm(tile_cols),
+        tile_count,
+        in_hbm(edge_weight.reshape(reps, period, TILE, TILE)),
+        in_specs=[HBM, HBM, SMEM, HBM],
+        scratch_shapes=[
+            pltpu.SMEM(tile_rows.shape, jnp.int32),
+            pltpu.SMEM(tile_cols.shape, jnp.int32),
+            pltpu.VMEM((reps, period, TILE, TILE), edge_weight.dtype),
+            pltpu.SemaphoreType.DMA((2,)),
+            pltpu.SemaphoreType.DMA((groups, reps)),
+        ],
+        flops=slots * TILE * TILE,
+        bytes_accessed=slots * TILE * TILE * 2,
+        grant=12 << 20,
+    )
 
     def spread(piece):
         pieces = {0: piece}

time: 50.5 us -> 51.5 us (1.020)
  waiting for transfers between devices: 9.48 us -> 14.7 us
  Pallas kernels: 24.9 us -> 22 us
  local copies, waits for them, and re-layouts: 1.27 us -> 0.02 us
    pallas_call x1 -> x0, Pallas kernels: 5.79 us -> none  [on_device(): pl.pallas_call(weight_kernel, out_shape=[jax.ShapeDtypeStruct(panel_shape...]
    ppermute x11, waiting for transfers between devices: 9.48 us -> 14.7 us  [hop(): return lax.ppermute(x, axis, pairs)]
    pallas_call x4 -> x6, Pallas kernels: 3.56 us -> 6.45 us  [call(): pl.pallas_call(kernel, out_shape=out_shape, in_specs=in_specs or [VMEM] *...]
    unnamed x18 -> x6, local copies, waits for them, and re-layouts: 1.27 us -> 0.02 us
  transfers between devices with their start and end apart: 11 -> 11, of which waited for: 6 -> 6; matrix products, arithmetic and copies ran while one was open for 0% -> 0% of each run, Pallas kernels for 26% -> 22%
where the time goes in v4:
time: 51.5 us; the launch traced here: 51.3 us
  Pallas kernels  22 us (43%)
  waiting for transfers between devices  14.7 us (29%)
  starting transfers between devices  13.8 us (27%)
  between operations  0.74 us (1%)
    ppermute x11, waiting for transfers between devices, hop(): return lax.ppermute(x, axis, pairs)  14.7 us
    ppermute x11, starting transfers between devices, hop(): return lax.ppermute(x, axis, pairs)  13.8 us
    pallas_call x1, Pallas kernels, on_device(): pl.pallas_call(far_kernel, out_shape=[jax.ShapeDtypeStruct(chunk, F32)] *...  8.21 us
    pallas_call x1, Pallas kernels, on_device(): pl.pallas_call(near_kernel, out_shape=[jax.ShapeDtypeStruct(s, F32) for s...  7.35 us
    pallas_call x6, Pallas kernels, call(): pl.pallas_call(kernel, out_shape=out_shape, in_specs=in_specs or [VMEM] *...  6.45 us
  transfers between devices with their start and end apart: 11, of which 6 were waited for; matrix products, arithmetic and copies ran while one was open for 0% of the time, Pallas kernels for 22%

profile of v4, /device:TPU:0, one launch (start us, length us, event | category | flops | bytes accessed | tf_op | source)
XLA Modules:
  0.0 51.3 jit_solution(8080507044295832398)
XLA Ops:
  0.0 1.1 %shard_map.101 = (f32[64,128]{1,0:T(8,128)S(1)}, f32[512,128]{1,0:T(8,128)S(1)}) custom-call(bf16[512,128]{1,0:T(8,128)(2,1)} %refs_0_.3, bf16[64,128]{1,0:T(8,128)(2,1)} %refs_1_.3, bf16[128,256]{1,0:T(8,128)(2,1)} %refs_2_.3), custom_call_target="tpu_custom_call" | custom-call | tf_op jit(solution)/shard_map/pallas_call | solution.py:40
  1.1 3.0 %collective-permute-start.1 = (f32[512,128]{1,0:T(8,128)S(1)}, f32[512,128]{1,0:T(8,128)S(1)}, u32[]{:S(2)}, u32[]{:S(2)}) collective-permute-start(f32[512,128]{1,0:T(8,128)S(1)} %get-tuple-element.43), channel_id=1, source_target_pairs={{0,1},{1,0},{2,3},{3,2},{4,5},{5,4},{6,7},{7,6},{8,9},{9,8},{10,11... | collective-permute-start | bytes 786440 | tf_op jit(solution)/shard_map/ppermute | solution.py:36
  4.2 0.1 collective-permute-start
  4.3 1.2 %shard_map.100 = (f32[512,128]{1,0:T(8,128)S(1)}, f32[64,128]{1,0:T(8,128)S(1)}, f32[8,128]{1,0:T(8,128)S(1)}, f32[8,128]{1,0:T(8,128)S(1)}) custom-call(bf16[512,128]{1,0:T(8,128)(2,1)} %refs_0_.3, bf16[64,128]{1,0:T(8,128)(2,1)} %refs_1_.3, bf16[128,256]{1,0:T(8,128)(2,1)} %refs_2_.3, f32[1,128]{1,0:T(1,128)} %bitcast.4, f32[1,128]{1,0:T(1,128)} %bitcast.6), custom_call_target="tpu_custom_call" | custom-call | tf_op jit(solution)/shard_map/pallas_call | solution.py:40
  5.4 5.8 %collective-permute-done.rest_0_ = f32[64,128]{1,0:T(8,128)S(1)} collective-permute-done((f32[64,128]{1,0:T(8,128)S(1)}, f32[64,128]{1,0:T(8,128)S(1)}, u32[]{:S(2)}, u32[]{:S(2)}) %collective-permute-start) | collective-permute-done | bytes 32800 | tf_op jit(solution)/shard_map/ppermute | solution.py:36
  11.2 0.1 shard_map.102
  11.3 1.9 %collective-permute-start.2 = (f32[8,64]{1,0:T(8,128)S(1)}, f32[8,64]{1,0:T(8,128)S(1)}, u32[]{:S(2)}, u32[]{:S(2)}) collective-permute-start(f32[8,64]{1,0:T(8,128)S(1)} %get-tuple-element.46.refs_0_), channel_id=1, source_target_pairs={{0,2},{2,0},{4,6},{6,4},{1,3},{3,1},{5,7},{7,5},{8,10},{10,8},{12,... | collective-permute-start | bytes 6152 | tf_op jit(solution)/shard_map/ppermute | solution.py:36
  13.2 2.6 %collective-permute-start.3 = (f32[8,64]{1,0:T(8,128)S(1)}, f32[8,64]{1,0:T(8,128)S(1)}, u32[]{:S(2)}, u32[]{:S(2)}) collective-permute-start(f32[8,64]{1,0:T(8,128)S(1)} %get-tuple-element.46.refs_0_), channel_id=1, source_target_pairs={{0,4},{2,6},{4,0},{6,2},{1,5},{3,7},{5,1},{7,3},{8,12},{10,14},{12... | collective-permute-start | bytes 6152 | tf_op jit(solution)/shard_map/ppermute | solution.py:36
  15.8 0.0 collective-permute-start.4
  15.8 0.0 collective-permute-done.2.refs_1_
  15.8 1.9 %collective-permute-done.3.refs_2_ = f32[8,64]{1,0:T(8,128)S(1)} collective-permute-done((f32[8,64]{1,0:T(8,128)S(1)}, f32[8,64]{1,0:T(8,128)S(1)}, u32[]{:S(2)}, u32[]{:S(2)}) %collective-permute-start.3) | collective-permute-done | bytes 2080 | tf_op jit(solution)/shard_map/ppermute | solution.py:36
  17.7 3.5 %collective-permute-done.4.refs_3_ = f32[8,64]{1,0:T(8,128)S(1)} collective-permute-done((f32[8,64]{1,0:T(8,128)S(1)}, f32[8,64]{1,0:T(8,128)S(1)}, u32[]{:S(2)}, u32[]{:S(2)}) %collective-permute-start.4) | collective-permute-done | bytes 2080 | tf_op jit(solution)/shard_map/ppermute | solution.py:36
  21.2 0.0 collective-permute-done.1.rest_0_
  21.2 0.3 shard_map.103.refs_4_
  21.5 0.0 collective-permute-start.6
  21.5 1.6 %collective-permute-start.5 = (f32[544,128]{1,0:T(8,128)S(1)}, f32[544,128]{1,0:T(8,128)S(1)}, u32[]{:S(2)}, u32[]{:S(2)}) collective-permute-start(f32[544,128]{1,0:T(8,128)S(1)} %shard_map.103.refs_4_), channel_id=1, source_target_pairs={{0,16},{8,24},{16,0},{24,8},{1,17},{9,25},{17,1},{25,9},{2,18},{10... | collective-permute-start | bytes 835592 | tf_op jit(solution)/shard_map/ppermute | solution.py:36
  23.7 2.6 %shard_map.104 = (f32[2,8,128,128]{3,2,1,0:T(8,128)S(1)}, f32[2,8,128,128]{3,2,1,0:T(8,128)S(1)}) custom-call(s32[1,1,128]{2,1,0:T(1,128)} %rows_hbm.1, s32[1,1,128]{2,1,0:T(1,128)} %cols_hbm.1, s32[1,1]{1,0:T(1,128)S(6)} %copy.11.count_ref, bf16[4,32,128,128]{3,2,1,0:T(8,128)(2,1)} %bitcast.9), custom_call_target="tpu_custom_call" | custom-call | flops 2097152 | bytes 4194304 | tf_op jit(solution)/shard_map/pallas_call | solution.py:40
  26.4 0.0 copy-start
  26.4 0.0 copy-start.1
  26.4 0.0 copy-start.2
  26.4 0.0 collective-permute-done.6.refs_5_
  26.4 7.4 %shard_map.105 = (f32[256,128]{1,0:T(8,128)S(1)}, f32[256,128]{1,0:T(8,128)S(1)}, f32[256,128]{1,0:T(8,128)S(1)}) custom-call(f32[8,64]{1,0:T(8,128)S(1)} %get-tuple-element.46.refs_0_, f32[8,64]{1,0:T(8,128)S(1)} %collective-permute-done.2.refs_1_, f32[8,64]{1,0:T(8,128)S(1)} %collective-permute-done.3.refs_2_, f32[8,64]{1,0:T(8,128)S(1)} %collective-permute-done.4.refs_3_, ...), custom_call_target="tpu_custom_call" | custom-call | flops 1073741824 | bytes 524288 | tf_op jit(solution)/shard_map/pallas_call | solution.py:505
  33.8 0.0 collective-permute-done.5.refs_3_
  33.8 0.2 collective-permute-start.7
  34.0 1.4 %collective-permute-done.7.refs_4_ = f32[544,128]{1,0:T(8,128)S(1)} collective-permute-done((f32[544,128]{1,0:T(8,128)S(1)}, f32[544,128]{1,0:T(8,128)S(1)}, u32[]{:S(2)}, u32[]{:S(2)}) %collective-permute-start.7) | collective-permute-done | bytes 278560 | tf_op jit(solution)/shard_map/ppermute | solution.py:36
  35.4 8.2 %shard_map.106 = (f32[72,128]{1,0:T(8,128)S(1)}, f32[72,128]{1,0:T(8,128)S(1)}, f32[72,128]{1,0:T(8,128)S(1)}, f32[72,128]{1,0:T(8,128)S(1)}) custom-call(f32[256,128]{1,0:T(8,128)S(1)} %get-tuple-element.56.refs_0_, f32[256,128]{1,0:T(8,128)S(1)} %get-tuple-element.57.refs_1_, f32[256,128]{1,0:T(8,128)S(1)} %get-tuple-element.58.refs_2_, ...), custom_call_target="tpu_custom_call" | custom-call | flops 1073741824 | bytes 524288 | tf_op jit(solution)/shard_map/pallas_call | solution.py:520
  43.6 0.3 collective-permute-start.10
  43.9 0.0 collective-permute-start.8
  43.9 4.2 %collective-permute-start.9 = (f32[72,128]{1,0:T(8,128)S(1)}, f32[72,128]{1,0:T(8,128)S(1)}, u32[]{:S(2)}, u32[]{:S(2)}) collective-permute-start(f32[72,128]{1,0:T(8,128)S(1)} %get-tuple-element.63), channel_id=1, source_target_pairs={{0,4},{2,6},{4,0},{6,2},{1,5},{3,7},{5,1},{7,3},{8,12},{10,14},{12... | collective-permute-start | bytes 110600 | tf_op jit(solution)/shard_map/ppermute | solution.py:36
  48.0 1.8 %collective-permute-done.10.rest_3_ = f32[72,128]{1,0:T(8,128)S(1)} collective-permute-done((f32[72,128]{1,0:T(8,128)S(1)}, f32[72,128]{1,0:T(8,128)S(1)}, u32[]{:S(2)}, u32[]{:S(2)}) %collective-permute-start.10) | collective-permute-done | bytes 36896 | tf_op jit(solution)/shard_map/ppermute | solution.py:36
  49.8 0.4 collective-permute-done.9.rest_2_
  50.2 1.1 %shard_map.107 = bf16[64,128]{1,0:T(8,128)(2,1)} custom-call(f32[64,128]{1,0:T(8,128)S(1)} %get-tuple-element.40.zdst_ref, f32[1,128]{1,0:T(1,128)S(1)} %bitcast.5, f32[1,128]{1,0:T(1,128)S(1)} %bitcast.7, f32[1,128]{1,0:T(1,128)S(1)} %bitcast.8, f32[72,128]{1,0:T(8,128)S(1)} %get-tuple-element.61.rest_0_, f32[72,128]{1,0:T(8,128)S(1)} %collective-permute-done.8.rest_1_, ...), custom_call_target="tpu_custom_call" | custom-call | tf_op jit(solution)/shard_map/pallas_call | solution.py:40
  (4 shorter events, 0.0 us)
Async XLA Ops:
  1.1 20.0 %collective-permute-start.1 = (f32[512,128]{1,0:T(8,128)S(1)}, f32[512,128]{1,0:T(8,128)S(1)}, u32[]{:S(2)}, u32[]{:S(2)}) collective-permute-start(f32[512,128]{1,0:T(8,128)S(1)} %get-tuple-element.43), channel_id=1, source_target_pairs={{0,1},{1,0},{2,3},{3,2},{4,5},{5,4},{6,7},{7,6},{8,9},{9,8},{10,11... | collective-permute-start | bytes 786440 | tf_op jit(solution)/shard_map/ppermute | solution.py:36
  4.2 7.0 %collective-permute-start = (f32[64,128]{1,0:T(8,128)S(1)}, f32[64,128]{1,0:T(8,128)S(1)}, u32[]{:S(2)}, u32[]{:S(2)}) collective-permute-start(f32[64,128]{1,0:T(8,128)S(1)} %get-tuple-element.37), channel_id=1, source_target_pairs={{0,1},{1,0},{2,3},{3,2},{4,5},{5,4},{6,7},{7,6},{8,9},{9,8},{10,11... | collective-permute-start | bytes 98312 | tf_op jit(solution)/shard_map/ppermute | solution.py:36
  11.3 4.5 %collective-permute-start.2 = (f32[8,64]{1,0:T(8,128)S(1)}, f32[8,64]{1,0:T(8,128)S(1)}, u32[]{:S(2)}, u32[]{:S(2)}) collective-permute-start(f32[8,64]{1,0:T(8,128)S(1)} %get-tuple-element.46.refs_0_), channel_id=1, source_target_pairs={{0,2},{2,0},{4,6},{6,4},{1,3},{3,1},{5,7},{7,5},{8,10},{10,8},{12,... | collective-permute-start | bytes 6152 | tf_op jit(solution)/shard_map/ppermute | solution.py:36
  13.2 4.5 %collective-permute-start.3 = (f32[8,64]{1,0:T(8,128)S(1)}, f32[8,64]{1,0:T(8,128)S(1)}, u32[]{:S(2)}, u32[]{:S(2)}) collective-permute-start(f32[8,64]{1,0:T(8,128)S(1)} %get-tuple-element.46.refs_0_), channel_id=1, source_target_pairs={{0,4},{2,6},{4,0},{6,2},{1,5},{3,7},{5,1},{7,3},{8,12},{10,14},{12... | collective-permute-start | bytes 6152 | tf_op jit(solution)/shard_map/ppermute | solution.py:36
  15.8 5.4 %collective-permute-start.4 = (f32[8,64]{1,0:T(8,128)S(1)}, f32[8,64]{1,0:T(8,128)S(1)}, u32[]{:S(2)}, u32[]{:S(2)}) collective-permute-start(f32[8,64]{1,0:T(8,128)S(1)} %get-tuple-element.46.refs_0_), channel_id=1, source_target_pairs={{0,6},{2,4},{4,2},{6,0},{1,7},{3,5},{5,3},{7,1},{8,14},{10,12},{12... | collective-permute-start | bytes 6152 | tf_op jit(solution)/shard_map/ppermute | solution.py:36
  21.5 4.9 %collective-permute-start.6 = (f32[544,128]{1,0:T(8,128)S(1)}, f32[544,128]{1,0:T(8,128)S(1)}, u32[]{:S(2)}, u32[]{:S(2)}) collective-permute-start(f32[544,128]{1,0:T(8,128)S(1)} %shard_map.103.refs_4_), channel_id=1, source_target_pairs={{0,8},{8,0},{16,24},{24,16},{1,9},{9,1},{17,25},{25,17},{2,10},{10... | collective-permute-start | bytes 835592 | tf_op jit(solution)/shard_map/ppermute | solution.py:36
  21.5 12.3 %collective-permute-start.5 = (f32[544,128]{1,0:T(8,128)S(1)}, f32[544,128]{1,0:T(8,128)S(1)}, u32[]{:S(2)}, u32[]{:S(2)}) collective-permute-start(f32[544,128]{1,0:T(8,128)S(1)} %shard_map.103.refs_4_), channel_id=1, source_target_pairs={{0,16},{8,24},{16,0},{24,8},{1,17},{9,25},{17,1},{25,9},{2,18},{10... | collective-permute-start | bytes 835592 | tf_op jit(solution)/shard_map/ppermute | solution.py:36
  26.4 23.8 %copy-start = (f32[128]{0:T(128)S(1)}, f32[128]{0:T(128)}, u32[]{:S(2)}) copy-start(f32[128]{0:T(128)} %param.13) | copy-start | bytes 1540
  26.4 23.8 %copy-start.1 = (f32[128]{0:T(128)S(1)}, f32[128]{0:T(128)}, u32[]{:S(2)}) copy-start(f32[128]{0:T(128)} %param.14) | copy-start | bytes 1540
  26.4 23.8 %copy-start.2 = (f32[128]{0:T(128)S(1)}, f32[128]{0:T(128)}, u32[]{:S(2)}) copy-start(f32[128]{0:T(128)} %param.15) | copy-start | bytes 1540
  33.8 1.6 %collective-permute-start.7 = (f32[544,128]{1,0:T(8,128)S(1)}, f32[544,128]{1,0:T(8,128)S(1)}, u32[]{:S(2)}, u32[]{:S(2)}) collective-permute-start(f32[544,128]{1,0:T(8,128)S(1)} %collective-permute-done.5.refs_3_), channel_id=1, source_target_pairs={{0,8},{8,0},{16,24},{24,16},{1,9},{9,1},{17,25},{25,17},{2,10},{10... | collective-permute-start | bytes 835592 | tf_op jit(solution)/shard_map/ppermute | solution.py:36
  43.6 6.2 %collective-permute-start.10 = (f32[72,128]{1,0:T(8,128)S(1)}, f32[72,128]{1,0:T(8,128)S(1)}, u32[]{:S(2)}, u32[]{:S(2)}) collective-permute-start(f32[72,128]{1,0:T(8,128)S(1)} %get-tuple-element.64), channel_id=1, source_target_pairs={{0,6},{2,4},{4,2},{6,0},{1,7},{3,5},{5,3},{7,1},{8,14},{10,12},{12... | collective-permute-start | bytes 110600 | tf_op jit(solution)/shard_map/ppermute | solution.py:36
  43.9 5.9 %collective-permute-start.8 = (f32[72,128]{1,0:T(8,128)S(1)}, f32[72,128]{1,0:T(8,128)S(1)}, u32[]{:S(2)}, u32[]{:S(2)}) collective-permute-start(f32[72,128]{1,0:T(8,128)S(1)} %get-tuple-element.62), channel_id=1, source_target_pairs={{0,2},{2,0},{4,6},{6,4},{1,3},{3,1},{5,7},{7,5},{8,10},{10,8},{12,... | collective-permute-start | bytes 110600 | tf_op jit(solution)/shard_map/ppermute | solution.py:36
  43.9 6.3 %collective-permute-start.9 = (f32[72,128]{1,0:T(8,128)S(1)}, f32[72,128]{1,0:T(8,128)S(1)}, u32[]{:S(2)}, u32[]{:S(2)}) collective-permute-start(f32[72,128]{1,0:T(8,128)S(1)} %get-tuple-element.63), channel_id=1, source_target_pairs={{0,4},{2,6},{4,0},{6,2},{1,5},{3,7},{5,1},{7,3},{8,12},{10,14},{12... | collective-permute-start | bytes 110600 | tf_op jit(solution)/shard_map/ppermute | solution.py:36

commit v5 on v4

v5 whole, which is shorter than its diff:
```python
import jax
import jax.numpy as jnp
from jax import lax
from jax.experimental import pallas as pl
from jax.experimental.pallas import tpu as pltpu
from jax.sharding import PartitionSpec as P

HEADS = 8
TILE = 128
SLOPE = 0.2
LOG2E = 1.4426950408889634
NEG = -1e30
F32 = jnp.float32
BF16 = jnp.bfloat16
HIGHEST = lax.Precision.HIGHEST
VMEM = pl.BlockSpec(memory_space=pltpu.VMEM)
SMEM = pl.BlockSpec(memory_space=pltpu.SMEM)
HBM = pl.BlockSpec(memory_space=pltpu.HBM)


def is_pow2(n):
    return n & (n - 1) == 0


def goes_to(i, d, n):
    return i ^ d if is_pow2(n) else lax.rem(i + d, n)


def comes_from(i, d, n):
    return i ^ d if is_pow2(n) else lax.rem(i + n - d, n)


def hop(x, axis, d):
    n = lax.axis_size(axis)
    pairs = [(i, i ^ d if is_pow2(n) else (i + d) % n) for i in range(n)]
    return lax.ppermute(x, axis, pairs)


def call(kernel, out_shape, *args, in_specs=None, flops=0, bytes_accessed=0, grant=8 << 20, **kw):
    return pl.pallas_call(
        kernel,
        out_shape=out_shape,
        in_specs=in_specs or [VMEM] * len(args),
        cost_estimate=pl.CostEstimate(
            flops=flops, bytes_accessed=bytes_accessed, transcendentals=0
        ),
        compiler_params=pltpu.CompilerParams(vmem_limit_bytes=grant),
        **kw,
    )(*args)


def limit(mib, least):
    return min(max(mib << 20, least), 60 << 20)


def in_hbm(x):
    return pltpu.with_memory_space_constraint(x, pltpu.HBM)


def up8(n):
    return -(-n // 8) * 8


def head_rows(vector, heads, width, height):
    dims = width // heads
    shape = (height, width)
    row = lax.broadcasted_iota(jnp.int32, shape, 0) % heads
    lane = lax.broadcasted_iota(jnp.int32, shape, 1)
    return jnp.where(lane // dims == row, jnp.broadcast_to(vector, shape), 0.0)


def contract(lhs, rhs, dims, precision=HIGHEST):
    return lax.dot_general(
        lhs, rhs, (dims, ((), ())), preferred_element_type=F32, precision=precision
    )


def take_cols(proj_ref, which, width):
    if width % TILE == 0:
        return proj_ref[:, pl.ds(pl.multiple_of(which * width, width), width)]
    full = proj_ref[...]
    out = full[:, :width]
    for k in range(1, full.shape[1] // width):
        out = jnp.where(which == k, full[:, k * width : (k + 1) * width], out)
    return out


def project(x, w):
    return lax.dot_general(x, w, (((1,), (0,)), ((), ())), preferred_element_type=F32)


def leaky(x):
    return jnp.maximum(x, SLOPE * x)


def on_device(
    src_feats, dst_feats, proj, att_src, att_dst, bias, tile_rows, tile_cols, tile_count, edge_weight
):
    n_row, n_col, n_feat = (lax.axis_size(a) for a in ("row", "col", "feat"))
    width = proj.shape[1] // n_feat
    heads = HEADS // n_feat
    dims = width // heads
    lanes = -(-width // TILE) * TILE
    src_rows, own_rows = src_feats.shape[0], dst_feats.shape[0]
    slots = tile_rows.shape[2]
    row_tiles = own_rows * n_col // TILE
    piece_tiles = src_rows // TILE
    n_chunk = 2 if piece_tiles % 2 == 0 else 1
    chunk_tiles = piece_tiles // n_chunk
    part_rows = src_rows // n_chunk
    col_tiles = piece_tiles * n_row
    hp = up8(2 * heads)
    mdp = up8(2 * heads)
    att_src2, att_dst2, bias2 = (v.reshape(1, width) for v in (att_src, att_dst, bias))

    def fetch(hbm, vmem, sems):
        copies = [pltpu.make_async_copy(h, v, sems.at[k]) for k, (h, v) in enumerate(zip(hbm, vmem))]
        for copy in copies:
            copy.start()
        for copy in copies:
            copy.wait()

    def fetching(kernel, outs, *args):
        return call(
            kernel,
            outs,
            *map(in_hbm, args),
            in_specs=[HBM] * len(args),
            scratch_shapes=[
                *(pltpu.VMEM(v.shape, v.dtype) for v in args),
                pltpu.SemaphoreType.DMA((len(args),)),
            ],
        )

    def send_kernel(*refs):
        hbm, outs, (src_ref, dst_ref, proj_ref, sems) = refs[:3], refs[3:-4], refs[-4:]
        fetch(hbm, (src_ref, dst_ref, proj_ref), sems)
        me = lax.axis_index("feat")
        for d in range(1, n_feat):
            w = take_cols(proj_ref, goes_to(me, d, n_feat), width)
            own_outs = outs[(d - 1) * (n_chunk + 1) : d * (n_chunk + 1)]
            own_outs[0][...] = project(dst_ref[...], w)
            for ch in range(n_chunk):
                own_outs[ch + 1][...] = project(src_ref[ch * part_rows : (ch + 1) * part_rows], w)

    sent = fetching(
        send_kernel,
        [
            pltpu.VMEM((n, width), F32)
            for _ in range(1, n_feat)
            for n in [own_rows] + [part_rows] * n_chunk
        ],
        src_feats,
        dst_feats,
        proj,
    )
    sent = [sent[k :: n_chunk + 1] for k in range(n_chunk + 1)]
    dst_parts = [hop(sent[0][d - 1], "feat", d) for d in range(1, n_feat)]
    src_parts = [[hop(part[d - 1], "feat", d) for d in range(1, n_feat)] for part in sent[1:]]

    def own_kernel(*refs):
        hbm, outs, refs = refs[:5], refs[5 : 8 + n_chunk], refs[8 + n_chunk :]
        fetch(hbm, refs[:5], refs[5])
        src_ref, dst_ref, proj_ref, att_src_ref, att_dst_ref = refs[:5]
        w = take_cols(proj_ref, lax.axis_index("feat"), width)
        outs[0][...] = project(dst_ref[...], w)
        outs[1][...] = LOG2E * head_rows(att_dst_ref[...], heads, width, up8(heads))
        outs[2][...] = LOG2E * head_rows(att_src_ref[...], heads, width, hp)
        for ch in range(n_chunk):
            outs[3 + ch][...] = project(src_ref[ch * part_rows : (ch + 1) * part_rows], w)

    dst_own, dst_att, src_att, *src_own = fetching(
        own_kernel,
        [
            pltpu.VMEM((own_rows, width), F32),
            pltpu.VMEM((up8(heads), width), F32),
            pltpu.VMEM((hp, width), F32),
        ]
        + [pltpu.VMEM((part_rows, width), F32)] * n_chunk,
        src_feats,
        dst_feats,
        proj,
        att_src2,
        att_dst2,
    )
    dst_parts, src_own = lax.optimization_barrier((dst_parts, src_own))

    tiles = row_tiles * col_tiles
    whole = lambda shape: pl.BlockSpec(shape, lambda s: (0,) * len(shape))

    def dst_kernel(own_ref, att_ref, *rest):
        got, (z_ref, s_ref) = rest[: n_feat - 1], rest[n_feat - 1 :]
        z = own_ref[...]
        for part in got:
            z = z + part[...]
        z_ref[...] = z
        s_ref[...] = contract(att_ref[...], z, ((1,), (1,)))

    zdst, s_dst = call(
        dst_kernel,
        [
            jax.ShapeDtypeStruct((own_rows, width), F32),
            jax.ShapeDtypeStruct((up8(heads), own_rows), F32),
        ],
        dst_own,
        dst_att,
        *dst_parts,
    )
    targets = [hop(s_dst, "col", d) for d in range(n_col - 1, 0, -1)]
    targets = [s_dst] + targets[::-1]


    pack_rows = part_rows + chunk_tiles * hp

    def z_kernel(own_ref, att_ref, *rest):
        got, out_ref = rest[: n_feat - 1], rest[n_feat - 1]
        z = own_ref[...]
        for part in got:
            z = z + part[...]
        if width < lanes:
            out_ref[...] = jnp.zeros_like(out_ref)
        out_ref[:part_rows, :width] = z
        s = contract(att_ref[...], z, ((1,), (1,)))
        low = lax.broadcasted_iota(jnp.int32, s.shape, 0) < heads
        s = jnp.where(low, s, SLOPE * s)
        for t in range(chunk_tiles):
            at = part_rows + t * hp
            out_ref[at : at + hp, :TILE] = s[:, t * TILE : (t + 1) * TILE]

    parts, far_first = {}, n_row // 2
    for ch in range(n_chunk):
        own = call(z_kernel, pltpu.VMEM((pack_rows, lanes), F32), src_own[ch], src_att, *src_parts[ch])
        parts[far_first, ch] = hop(own, "row", far_first)
        parts[0, ch] = own
    last = n_chunk - 1
    parts[0, last], tile_rows = lax.optimization_barrier((parts[0, last], tile_rows))

    def spread(first, ch):
        d = n_row // 4
        while d:
            for k in [k for k, c in parts if c == ch and k ^ first < far_first]:
                parts[k ^ d, ch] = hop(parts[k, ch], "row", d)
            d //= 2

    for ch in range(n_chunk):
        spread(0, ch)

    units = n_row * n_chunk
    period = min(slots, tiles) if slots % min(slots, tiles) == 0 else slots
    reps = slots // period
    group = 8
    groups = period // group

    def weight_kernel(rows_hbm, cols_hbm, count_ref, w_hbm, panel_ref, *scratch):
        rows_ref, cols_ref, w_ref, index_sems, w_sems = scratch
        row = lax.axis_index("row")
        indices = [
            pltpu.make_async_copy(rows_hbm, rows_ref, index_sems.at[0]),
            pltpu.make_async_copy(cols_hbm, cols_ref, index_sems.at[1]),
        ]
        blocks = [
            pltpu.make_async_copy(
                w_hbm.at[k, pl.ds(g * group, group)],
                w_ref.at[k, pl.ds(g * group, group)],
                w_sems.at[g, k],
            )
            for g in range(groups)
            for k in range(reps)
        ]
        for copy in indices + blocks:
            copy.start()

        @pl.loop(0, units)
        def _(u):
            @pl.loop(0, row_tiles)
            def _(r):
                panel_ref[u, r] = jnp.zeros((chunk_tiles, TILE, TILE), F32)

        for copy in indices:
            copy.wait()
        count = count_ref[0, 0]
        for g in range(groups):
            for copy in blocks[g * reps : (g + 1) * reps]:
                copy.wait()
            base = g * group

            @pl.loop(base, jnp.clip(count, base, base + group))
            def _(u):
                r, c = rows_ref[0, 0, u], cols_ref[0, 0, u]
                unit = ((c // piece_tiles) ^ row) * n_chunk + c % piece_tiles // chunk_tiles
                t = c % chunk_tiles
                total = w_ref[0, u].astype(F32)
                for k in range(1, reps):
                    live = (u + k * period < count).astype(F32)
                    total = total + w_ref[k, u].astype(F32) * live
                panel_ref[unit, r, t] = panel_ref[unit, r, t] + total

    panel = call(
        weight_kernel,
        pltpu.VMEM((units, row_tiles, chunk_tiles, TILE, TILE), F32),
        in_hbm(tile_rows),
        in_hbm(tile_cols),
        tile_count,
        in_hbm(edge_weight.reshape(reps, period, TILE, TILE)),
        in_specs=[HBM, HBM, SMEM, HBM],
        scratch_shapes=[
            pltpu.SMEM(tile_rows.shape, jnp.int32),
            pltpu.SMEM(tile_cols.shape, jnp.int32),
            pltpu.VMEM((reps, period, TILE, TILE), edge_weight.dtype),
            pltpu.SemaphoreType.DMA((2,)),
            pltpu.SemaphoreType.DMA((groups, reps)),
        ],
        flops=slots * TILE * TILE,
        bytes_accessed=slots * TILE * TILE * 2,
        grant=12 << 20,
    )

    block = 64
    blocks = TILE // block
    unroll = 2 if row_tiles % 2 == 0 else 1
    steps = row_tiles // unroll
    chunk_rows = own_rows + mdp
    group_rows = unroll * TILE
    all_rows = row_tiles * TILE
    tiny, huge = 2.0**-60, 2.0**60
    lane_w = lambda: lax.broadcasted_iota(jnp.int32, (block, width), 1) // dims
    lane_t = lambda: lax.broadcasted_iota(jnp.int32, (block, TILE), 1)

    def score_rows(part_ref, t, h):
        at = part_rows + t * hp + h
        return part_ref[at : at + 1, :TILE], part_ref[at + heads : at + heads + 1, :TILE]

    def split_z(part_ref, z_cat, k):
        z = part_ref[:part_rows, :width]
        hi = z.astype(BF16)
        z_cat[k * part_rows : (k + 1) * part_rows, :width] = hi
        z_cat[k * part_rows : (k + 1) * part_rows, width:] = (z - hi.astype(F32)).astype(BF16)

    def put(probs, slot, h, q, p):
        cols = slice(q * TILE, (q + 1) * TILE)
        hi = p.astype(BF16)
        probs[slot, 2 * h * block : (2 * h + 1) * block, cols] = hi
        probs[slot, (2 * h + 1) * block : (2 * h + 2) * block, cols] = (
            p - hi.astype(F32)
        ).astype(BF16)

    def weighted(probs, z):
        both = lax.dot_general(probs, z, (((1,), (0,)), ((), ())), preferred_element_type=F32)
        num = jnp.zeros((block, width), F32)
        for h in range(heads):
            hi = both[2 * h * block : (2 * h + 1) * block]
            lo = both[(2 * h + 1) * block : (2 * h + 2) * block]
            num = jnp.where(lane_w() == h, hi[:, :width] + (hi[:, width:] + lo[:, :width]), num)
        return num

    def attend(part_refs, w_refs, posneg, den_in, num_in, den_out, num_out, z_cat, probs):
        base = pl.program_id(0) * group_rows
        for b in range(unroll * blocks):
            at = pl.ds(pl.multiple_of(base + b * block, block), block)
            rt, i0 = divmod(b * block, TILE)
            for h in range(heads):
                pn = posneg[at, :]
                pos = jnp.broadcast_to(pn[:, h : h + 1], (block, TILE))
                neg = jnp.broadcast_to(pn[:, heads + h : heads + h + 1], (block, TILE))
                den = jnp.zeros((block, TILE), F32) if den_in is None else den_in[h, at, :]
                for k, part_ref in enumerate(part_refs):
                    for t in range(chunk_tiles):
                        s, s_low = score_rows(part_ref, t, h)
                        x = jnp.maximum(pos + s, neg + s_low)
                        p = w_refs[k][0, rt, t, i0 : i0 + block, :] * jnp.exp2(x)
                        den = den + p
                        put(probs, b % 2, h, k * chunk_tiles + t, p)
                den_out[h, at, :] = den
            num = weighted(probs[b % 2], z_cat[...])
            num_out[at, :] = num if num_in is None else num_in[at, :] + num

    shape_t, shape_w, shape_d = (all_rows, TILE), (all_rows, width), (heads, all_rows, TILE)
    part_spec = whole((pack_rows, lanes))

    def unit_spec(k, ch):
        return pl.BlockSpec(
            (1, unroll, chunk_tiles, TILE, TILE), lambda s: (k * n_chunk + ch, s, 0, 0, 0)
        )

    def stage(kernel, keys, before, before_shapes, outs, extra=(), scratch=()):
        n = len(keys)
        return pl.pallas_call(
            kernel,
            out_shape=[pltpu.VMEM(s, F32) for s in outs],
            grid=(steps,),
            in_specs=[whole(s) for s in before_shapes]
            + [part_spec] * (n + len(extra))
            + [unit_spec(*key) for key in (*keys, *extra)],
            out_specs=[whole(s) for s in outs],
            scratch_shapes=[
                pltpu.VMEM((n * part_rows, 2 * width), BF16),
                pltpu.VMEM((2, 2 * heads * block, n * part_rows), BF16),
                *scratch,
            ],
            cost_estimate=pl.CostEstimate(
                flops=all_rows * n * part_rows * width * heads * 8,
                bytes_accessed=n * part_rows * width * 4,
                transcendentals=all_rows * n * part_rows * heads,
            ),
            compiler_params=pltpu.CompilerParams(vmem_limit_bytes=limit(16, 4 * tiles * TILE * TILE)),
        )(*before, *(parts[key] for key in (*keys, *extra)), *[panel] * (n + len(extra)))

    near_keys = [(k, ch) for ch in range(n_chunk) for k in range(far_first)]

    def near_kernel(*refs):
        n = len(near_keys)
        tgt_refs, part_refs, w_refs = refs[:n_col], refs[n_col : n_col + n], refs[n_col + n :][:n]
        posneg, tgt_m, den_out, num_out, z_cat, probs, tgt = refs[n_col + 2 * n :]
        col = lax.axis_index("col")

        @pl.when(pl.program_id(0) == 0)
        def _():
            shape = (up8(heads), TILE)
            eye = (
                lax.broadcasted_iota(jnp.int32, shape, 0)
                == lax.broadcasted_iota(jnp.int32, shape, 1) % heads
            ).astype(F32)
            lane = lax.broadcasted_iota(jnp.int32, (1, TILE), 1)
            bound = jnp.zeros((1, TILE), F32)
            for h in range(heads):
                rows = [score_rows(r, t, h)[0] for r in part_refs for t in range(chunk_tiles)]
                top = rows[0]
                for other in rows[1:]:
                    top = jnp.maximum(top, other)
                top = jnp.max(top, axis=1, keepdims=True)
                bound = jnp.where(lane % heads == h, top, bound)
            for d in range(n_col):
                at = pl.ds(
                    pl.multiple_of(comes_from(col, d, n_col) * own_rows, own_rows), own_rows
                )
                a = contract(tgt_refs[d][...], eye, ((0,), (0,)))
                m = leaky(a + bound)
                tgt[at, :] = a
                tgt_m[at, :] = jnp.where(lane < heads, a, m)
                posneg[at, :] = jnp.where(lane < heads, a, SLOPE * a) - m
            for k, part_ref in enumerate(part_refs):
                split_z(part_ref, z_cat, k)

        attend(part_refs, w_refs, posneg, None, None, den_out, num_out, z_cat, probs)

    def middle_kernel(*refs):
        n = len(middle_keys)
        (posneg, den_in, num_in), refs = refs[:3], refs[3:]
        part_refs, w_refs, (den_out, num_out, z_cat, probs) = refs[:n], refs[n : 2 * n], refs[2 * n :]

        @pl.when(pl.program_id(0) == 0)
        def _():
            for k, part_ref in enumerate(part_refs):
                split_z(part_ref, z_cat, k)

        attend(part_refs, w_refs, posneg, den_in, num_in, den_out, num_out, z_cat, probs)

    def last_kernel(*refs):
        n, n_all = len(last_keys), len(last_keys) + len(other_keys)
        (posneg, den_in, num_in, tgt_m), refs = refs[:4], refs[4:]
        part_refs, w_refs, refs = refs[:n_all], refs[n_all : 2 * n_all], refs[2 * n_all :]
        out_refs, (z_cat, probs, den_s, num_s, md_s, z_one) = refs[:n_col], refs[n_col:]
        col = lax.axis_index("col")
        step = pl.program_id(0)

        @pl.when(step == 0)
        def _():
            for k in range(n):
                split_z(part_refs[k], z_cat, k)

        attend(part_refs[:n], w_refs[:n], posneg, den_in, num_in, den_s, num_s, z_cat, probs)
        base = step * group_rows
        low = high = None
        for b in range(unroll * blocks):
            at = pl.ds(pl.multiple_of(base + b * block, block), block)
            md = tgt_m[at, :]
            for h in range(heads):
                den = jnp.sum(den_s[h, at, :], axis=1, keepdims=True)
                low = den if low is None else jnp.minimum(low, den)
                high = den if high is None else jnp.maximum(high, den)
                md = jnp.where(lane_t() == h, den, md)
            md_s[at, :] = md
        fine = jnp.logical_and(jnp.min(low) >= tiny, jnp.max(high) <= huge)

        @pl.when(jnp.logical_not(fine))
        def _():
            @pl.loop(0, unroll * blocks)
            def _(b):
                at = pl.ds(pl.multiple_of(base + b * block, block), block)
                rt = b // blocks
                rows = pl.ds(pl.multiple_of((b % blocks) * block, block), block)
                md = tgt_m[at, :]
                posnegs, dens = [], []
                for h in range(heads):
                    best = jnp.full((block, TILE), NEG, F32)
                    for part_ref, w_ref in zip(part_refs, w_refs):
                        for t in range(chunk_tiles):
                            edge = w_ref[0, rt, t, rows, :] > 0
                            s = score_rows(part_ref, t, h)[0]
                            best = jnp.maximum(best, jnp.where(edge, s, NEG))
                    a = tgt_m[at, :][:, h : h + 1]
                    m = leaky(a + jnp.max(best, axis=1, keepdims=True))
                    md = jnp.where(lane_t() == heads + h, m, md)
                    posnegs.append((a - m, SLOPE * a - m))
                    dens.append(jnp.zeros((block, TILE), F32))
                num_s[at, :] = jnp.zeros((block, width), F32)
                for part_ref, w_ref in zip(part_refs, w_refs):
                    for h in range(heads):
                        pos, neg = posnegs[h]
                        for t in range(chunk_tiles):
                            s, s_low = score_rows(part_ref, t, h)
                            x = jnp.minimum(jnp.maximum(pos + s, neg + s_low), 0.0)
                            p = w_ref[0, rt, t, rows, :] * jnp.exp2(x)
                            dens[h] = dens[h] + p
                            put(probs, 0, h, t, p)
                    split_z(part_ref, z_one, 0)
                    num_s[at, :] = num_s[at, :] + weighted(probs[0, :, :part_rows], z_one[...])
                for h in range(heads):
                    md = jnp.where(lane_t() == h, jnp.sum(dens[h], axis=1, keepdims=True), md)
                md_s[at, :] = md

        @pl.when(step == steps - 1)
        def _():
            for d in range(n_col):
                at = pl.ds(
                    pl.multiple_of(goes_to(col, d, n_col) * own_rows, own_rows), own_rows
                )
                if width < lanes:
                    out_refs[d][...] = jnp.zeros_like(out_refs[d])
                out_refs[d][:own_rows, :width] = num_s[at, :]
                out_refs[d][own_rows:, :own_rows] = md_s[at, :].T[:mdp]

    if n_chunk > 1:
        parts[far_first, 0], targets = lax.optimization_barrier((parts[far_first, 0], targets))
        spread(far_first, 0)
    posneg, tgt_m, den, num = stage(
        near_kernel,
        near_keys,
        targets,
        [(up8(heads), own_rows)] * n_col,
        [shape_t, shape_t, shape_d, shape_w],
        scratch=[pltpu.VMEM(shape_t, F32)],
    )
    parts[far_first, last], den = lax.optimization_barrier((parts[far_first, last], den))
    spread(far_first, last)
    middle_keys = [(k, ch) for ch in range(last) for k in range(far_first, n_row)]
    if middle_keys:
        den, num = stage(
            middle_kernel,
            middle_keys,
            (posneg, den, num),
            [shape_t, shape_d, shape_w],
            [shape_d, shape_w],
        )
    last_keys = [(k, last) for k in range(far_first, n_row)]
    other_keys = near_keys + middle_keys
    chunks = stage(
        last_kernel,
        last_keys,
        (posneg, den, num, tgt_m),
        [shape_t, shape_d, shape_w, shape_t],
        [(chunk_rows, lanes)] * n_col,
        extra=other_keys,
        scratch=[
            pltpu.VMEM(shape_d, F32),
            pltpu.VMEM(shape_w, F32),
            pltpu.VMEM(shape_t, F32),
            pltpu.VMEM((part_rows, 2 * width), BF16),
        ],
    )
    gathered = [hop(chunks[d], "col", d) for d in range(n_col - 1, 0, -1)]
    gathered = [chunks[0]] + gathered[::-1]

    def out_kernel(zdst_ref, src_ref, dst_ref, bias_ref, *rest):
        parts, out_ref = rest[:n_col], rest[n_col]
        same = (
            lax.broadcasted_iota(jnp.int32, (width, width), 0) // dims
            == lax.broadcasted_iota(jnp.int32, (width, width), 1) // dims
        ).astype(F32)
        z = zdst_ref[...]
        pair = contract(z * (dst_ref[...] + src_ref[...]), same, ((1,), (0,)))
        e_self = leaky(LOG2E * pair)
        which = lax.broadcasted_iota(jnp.int32, (mdp, width), 0)
        head = lax.broadcasted_iota(jnp.int32, (mdp, width), 1) // dims
        den_of, m_of = (which == head).astype(F32), (which == head + heads).astype(F32)
        mds = [part[own_rows:, :own_rows] for part in parts]
        ms = [contract(md, m_of, ((0,), (0,))) for md in mds]
        dens = [contract(md, den_of, ((0,), (0,))) for md in mds]
        top = e_self
        for m in ms:
            top = jnp.maximum(top, m)
        den = jnp.exp2(e_self - top)
        num = den * z
        for part, m, own_den in zip(parts, ms, dens):
            factor = jnp.exp2(m - top)
            den = den + factor * own_den
            num = num + factor * part[:own_rows, :width]
        x = num / den + bias_ref[...]
        out_ref[...] = jnp.where(x > 0, x, jnp.exp(jnp.minimum(x, 0.0)) - 1.0).astype(BF16)

    return call(
        out_kernel,
        jax.ShapeDtypeStruct((own_rows, width), BF16),
        zdst,
        att_src2,
        att_dst2,
        bias2,
        *gathered,
    )


def solution(mesh):
    return jax.shard_map(
        on_device,
        mesh=mesh,
        in_specs=(
            P(("row", "col"), "feat"),
            P(("row", "col"), "feat"),
            P("feat", None),
            P("feat"),
            P("feat"),
            P("feat"),
            P("row", "col", None),
            P("row", "col", None),
            P("row", "col"),
            P("row", "col", None, None, None),
        ),
        out_specs=P(("row", "col"), "feat"),
        check_vma=False,
    )
```

time: 51.5 us -> 54.6 us (1.060)
  starting transfers between devices: 13.8 us -> 19 us
  waiting for transfers between devices: 14.7 us -> 13.6 us
  Pallas kernels: 22 us -> 21.1 us
    ppermute x11 -> x15, starting transfers between devices: 13.8 us -> 19 us  [hop(): return lax.ppermute(x, axis, pairs)]
    ppermute x11 -> x15, waiting for transfers between devices: 14.7 us -> 13.6 us  [hop(): return lax.ppermute(x, axis, pairs)]
    pallas_call x2 -> x3, Pallas kernels: 15.6 us -> 14.6 us  [stage(): pl.pallas_call(kernel, out_shape=[pltpu.VMEM(s, F32) for s in outs], grid...]
    pallas_call x6 -> x7, Pallas kernels: 6.45 us -> 6.43 us  [call(): pl.pallas_call(kernel, out_shape=out_shape, in_specs=in_specs or [VMEM] *...]
  transfers between devices with their start and end apart: 11 -> 15, of which waited for: 6 -> 5; matrix products, arithmetic and copies ran while one was open for 0% -> 0% of each run, Pallas kernels for 22% -> 16%
where the time goes in v5:
time: 54.6 us; the launch traced here: 54.5 us
  Pallas kernels  21.1 us (39%)
  starting transfers between devices  19 us (35%)
  waiting for transfers between devices  13.6 us (25%)
  between operations  0.79 us (1%)
    ppermute x15, starting transfers between devices, hop(): return lax.ppermute(x, axis, pairs)  19 us
    pallas_call x3, Pallas kernels, stage(): pl.pallas_call(kernel, out_shape=[pltpu.VMEM(s, F32) for s in outs], grid...  14.6 us
    ppermute x15, waiting for transfers between devices, hop(): return lax.ppermute(x, axis, pairs)  13.6 us
    pallas_call x7, Pallas kernels, call(): pl.pallas_call(kernel, out_shape=out_shape, in_specs=in_specs or [VMEM] *...  6.43 us
  transfers between devices with their start and end apart: 15, of which 5 were waited for; matrix products, arithmetic and copies ran while one was open for 0% of the time, Pallas kernels for 16%

profile of v5, /device:TPU:0, one launch (start us, length us, event | category | flops | bytes accessed | tf_op | source)
XLA Modules:
  0.0 54.5 jit_solution(9716008393250030113)
XLA Ops:
  0.0 1.1 %shard_map.101 = (f32[64,128]{1,0:T(8,128)S(1)}, f32[256,128]{1,0:T(8,128)S(1)}, f32[256,128]{1,0:T(8,128)S(1)}) custom-call(bf16[512,128]{1,0:T(8,128)(2,1)} %refs_0_.3, bf16[64,128]{1,0:T(8,128)(2,1)} %refs_1_.3, bf16[128,256]{1,0:T(8,128)(2,1)} %refs_2_.3), custom_call_target="tpu_custom_call" | custom-call | tf_op jit(solution)/shard_map/pallas_call | solution.py:40
  1.1 3.0 %collective-permute-start.1 = (f32[256,128]{1,0:T(8,128)S(1)}, f32[256,128]{1,0:T(8,128)S(1)}, u32[]{:S(2)}, u32[]{:S(2)}) collective-permute-start(f32[256,128]{1,0:T(8,128)S(1)} %get-tuple-element.46), channel_id=1, source_target_pairs={{0,1},{1,0},{2,3},{3,2},{4,5},{5,4},{6,7},{7,6},{8,9},{9,8},{10,11... | collective-permute-start | bytes 393224 | tf_op jit(solution)/shard_map/ppermute | solution.py:36
  4.2 0.1 collective-permute-start.7
  4.3 1.9 %collective-permute-start = (f32[64,128]{1,0:T(8,128)S(1)}, f32[64,128]{1,0:T(8,128)S(1)}, u32[]{:S(2)}, u32[]{:S(2)}) collective-permute-start(f32[64,128]{1,0:T(8,128)S(1)} %get-tuple-element.39), channel_id=1, source_target_pairs={{0,1},{1,0},{2,3},{3,2},{4,5},{5,4},{6,7},{7,6},{8,9},{9,8},{10,11... | collective-permute-start | bytes 98312 | tf_op jit(solution)/shard_map/ppermute | solution.py:36
  6.2 1.2 %shard_map.100 = (f32[64,128]{1,0:T(8,128)S(1)}, f32[8,128]{1,0:T(8,128)S(1)}, f32[8,128]{1,0:T(8,128)S(1)}, f32[256,128]{1,0:T(8,128)S(1)}, f32[256,128]{1,0:T(8,128)S(1)}) custom-call(bf16[512,128]{1,0:T(8,128)(2,1)} %refs_0_.3, bf16[64,128]{1,0:T(8,128)(2,1)} %refs_1_.3, bf16[128,256]{1,0:T(8,128)(2,1)} %refs_2_.3, f32[1,128]{1,0:T(1,128)} %bitcast.4, ...), custom_call_target="tpu_custom_call" | custom-call | tf_op jit(solution)/shard_map/pallas_call | solution.py:40
  7.4 3.8 %collective-permute-done.rest_0_ = f32[64,128]{1,0:T(8,128)S(1)} collective-permute-done((f32[64,128]{1,0:T(8,128)S(1)}, f32[64,128]{1,0:T(8,128)S(1)}, u32[]{:S(2)}, u32[]{:S(2)}) %collective-permute-start) | collective-permute-done | bytes 32800 | tf_op jit(solution)/shard_map/ppermute | solution.py:36
  11.2 0.2 shard_map.103.refs_4_.refs_6_
  11.4 1.8 %collective-permute-start.2 = (f32[272,128]{1,0:T(8,128)S(1)}, f32[272,128]{1,0:T(8,128)S(1)}, u32[]{:S(2)}, u32[]{:S(2)}) collective-permute-start(f32[272,128]{1,0:T(8,128)S(1)} %shard_map.103.refs_4_.refs_6_), channel_id=1, source_target_pairs={{0,16},{8,24},{16,0},{24,8},{1,17},{9,25},{17,1},{25,9},{2,18},{10... | collective-permute-start | bytes 417800 | tf_op jit(solution)/shard_map/ppermute | solution.py:36
  13.2 0.2 shard_map.104.refs_6_.refs_8_
  13.4 0.5 collective-permute-start.6
  13.9 0.3 collective-permute-start.9
  14.2 0.1 shard_map.102
  14.3 3.9 %collective-permute-start.5 = (f32[8,64]{1,0:T(8,128)S(1)}, f32[8,64]{1,0:T(8,128)S(1)}, u32[]{:S(2)}, u32[]{:S(2)}) collective-permute-start(f32[8,64]{1,0:T(8,128)S(1)} %get-tuple-element.48.refs_0_), channel_id=1, source_target_pairs={{0,6},{2,4},{4,2},{6,0},{1,7},{3,5},{5,3},{7,1},{8,14},{10,12},{12... | collective-permute-start | bytes 6152 | tf_op jit(solution)/shard_map/ppermute | solution.py:36
  18.2 1.6 %collective-permute-done.5.refs_3_ = f32[8,64]{1,0:T(8,128)S(1)} collective-permute-done((f32[8,64]{1,0:T(8,128)S(1)}, f32[8,64]{1,0:T(8,128)S(1)}, u32[]{:S(2)}, u32[]{:S(2)}) %collective-permute-start.5) | collective-permute-done | bytes 2080 | tf_op jit(solution)/shard_map/ppermute | solution.py:36
  19.8 1.0 %collective-permute-start.4 = (f32[8,64]{1,0:T(8,128)S(1)}, f32[8,64]{1,0:T(8,128)S(1)}, u32[]{:S(2)}, u32[]{:S(2)}) collective-permute-start(f32[8,64]{1,0:T(8,128)S(1)} %get-tuple-element.48.refs_0_), channel_id=1, source_target_pairs={{0,4},{2,6},{4,0},{6,2},{1,5},{3,7},{5,1},{7,3},{8,12},{10,14},{12... | collective-permute-start | bytes 6152 | tf_op jit(solution)/shard_map/ppermute | solution.py:36
  20.8 3.5 %collective-permute-done.4.refs_2_ = f32[8,64]{1,0:T(8,128)S(1)} collective-permute-done((f32[8,64]{1,0:T(8,128)S(1)}, f32[8,64]{1,0:T(8,128)S(1)}, u32[]{:S(2)}, u32[]{:S(2)}) %collective-permute-start.4) | collective-permute-done | bytes 2080 | tf_op jit(solution)/shard_map/ppermute | solution.py:36
  24.3 1.5 %collective-permute-start.3 = (f32[8,64]{1,0:T(8,128)S(1)}, f32[8,64]{1,0:T(8,128)S(1)}, u32[]{:S(2)}, u32[]{:S(2)}) collective-permute-start(f32[8,64]{1,0:T(8,128)S(1)} %get-tuple-element.48.refs_0_), channel_id=1, source_target_pairs={{0,2},{2,0},{4,6},{6,4},{1,3},{3,1},{5,7},{7,5},{8,10},{10,8},{12,... | collective-permute-start | bytes 6152 | tf_op jit(solution)/shard_map/ppermute | solution.py:36
  26.4 2.5 %shard_map.105.refs_8_.refs_9_.refs_10_.refs_11_.refs_5_.refs_6_.refs_12_.refs_13_.refs_14_.refs_15_.refs_16_.refs_17_.refs_18_.refs_19_ = f32[8,2,2,128,128]{4,3,2,1,0:T(8,128)S(1)} custom-call(s32[1,1,128]{2,1,0:T(1,128)} %rows_hbm, s32[1,1,128]{2,1,0:T(1,128)} %cols_hbm.1, s32[1,1]{1,0:T(1,128)S(6)} %copy.11.count_ref, bf16[4,32,128,128]{3,2,1,0:T(8,128)(2,1)} %bitcast.9), custom_call_target="tpu_custom_call" | custom-call | flops 2097152 | bytes 4194304 | tf_op jit(solution)/shard_map/pallas_call | solution.py:40
  29.0 0.1 collective-permute-start.10
  29.1 3.3 %shard_map.106 = (f32[256,128]{1,0:T(8,128)S(1)}, f32[256,128]{1,0:T(8,128)S(1)}, f32[4,256,128]{2,1,0:T(8,128)S(1)}, f32[256,128]{1,0:T(8,128)S(1)}) custom-call(f32[8,64]{1,0:T(8,128)S(1)} %get-tuple-element.48.refs_0_, f32[8,64]{1,0:T(8,128)S(1)} %collective-permute-done.3.refs_1_, f32[8,64]{1,0:T(8,128)S(1)} %collective-permute-done.4.refs_2_, ...), custom_call_target="tpu_custom_call" | custom-call | flops 1073741824 | bytes 524288 | tf_op jit(solution)/shard_map/pallas_call | solution.py:387
  32.4 0.5 %collective-permute-start.11 = (f32[272,128]{1,0:T(8,128)S(1)}, f32[272,128]{1,0:T(8,128)S(1)}, u32[]{:S(2)}, u32[]{:S(2)}) collective-permute-start(f32[272,128]{1,0:T(8,128)S(1)} %collective-permute-done.9.refs_4_), channel_id=1, source_target_pairs={{0,8},{8,0},{16,24},{24,16},{1,9},{9,1},{17,25},{25,17},{2,10},{10... | collective-permute-start | bytes 417800 | tf_op jit(solution)/shard_map/ppermute | solution.py:36
  32.9 1.3 %shard_map.107 = (f32[4,256,128]{2,1,0:T(8,128)S(1)}, f32[256,128]{1,0:T(8,128)S(1)}) custom-call(f32[256,128]{1,0:T(8,128)S(1)} %get-tuple-element.56.refs_0_, f32[4,256,128]{2,1,0:T(8,128)S(1)} %get-tuple-element.58.refs_1_, f32[256,128]{1,0:T(8,128)S(1)} %get-tuple-element.59.refs_2_, f32[272,128]{1,0:T(8,128)S(1)} %collective-permute-done.2.refs_3_.refs_10_, ...), custom_call_target="tpu_custom_call" | custom-call | flops 536870912 | bytes 262144 | tf_op jit(solution)/shard_map/pallas_call | solution.py:387
  34.3 0.0 copy-start
  34.3 0.0 copy-start.1
  34.3 0.0 copy-start.2
  34.3 10.0 %shard_map.108 = (f32[72,128]{1,0:T(8,128)S(1)}, f32[72,128]{1,0:T(8,128)S(1)}, f32[72,128]{1,0:T(8,128)S(1)}, f32[72,128]{1,0:T(8,128)S(1)}) custom-call(f32[256,128]{1,0:T(8,128)S(1)} %get-tuple-element.56.refs_0_, f32[4,256,128]{2,1,0:T(8,128)S(1)} %get-tuple-element.61.refs_1_, f32[256,128]{1,0:T(8,128)S(1)} %get-tuple-element.62.refs_2_, ...), custom_call_target="tpu_custom_call" | custom-call | flops 536870912 | bytes 262144 | tf_op jit(solution)/shard_map/pallas_call | solution.py:387
  44.3 0.6 %collective-permute-start.12 = (f32[72,128]{1,0:T(8,128)S(1)}, f32[72,128]{1,0:T(8,128)S(1)}, u32[]{:S(2)}, u32[]{:S(2)}) collective-permute-start(f32[72,128]{1,0:T(8,128)S(1)} %get-tuple-element.66), channel_id=1, source_target_pairs={{0,2},{2,0},{4,6},{6,4},{1,3},{3,1},{5,7},{7,5},{8,10},{10,8},{12,... | collective-permute-start | bytes 110600 | tf_op jit(solution)/shard_map/ppermute | solution.py:36
  44.9 2.7 %collective-permute-start.13 = (f32[72,128]{1,0:T(8,128)S(1)}, f32[72,128]{1,0:T(8,128)S(1)}, u32[]{:S(2)}, u32[]{:S(2)}) collective-permute-start(f32[72,128]{1,0:T(8,128)S(1)} %get-tuple-element.67), channel_id=1, source_target_pairs={{0,4},{2,6},{4,0},{6,2},{1,5},{3,7},{5,1},{7,3},{8,12},{10,14},{12... | collective-permute-start | bytes 110600 | tf_op jit(solution)/shard_map/ppermute | solution.py:36
  47.6 1.1 %collective-permute-start.14 = (f32[72,128]{1,0:T(8,128)S(1)}, f32[72,128]{1,0:T(8,128)S(1)}, u32[]{:S(2)}, u32[]{:S(2)}) collective-permute-start(f32[72,128]{1,0:T(8,128)S(1)} %get-tuple-element.68), channel_id=1, source_target_pairs={{0,6},{2,4},{4,2},{6,0},{1,7},{3,5},{5,3},{7,1},{8,14},{10,12},{12... | collective-permute-start | bytes 110600 | tf_op jit(solution)/shard_map/ppermute | solution.py:36
  48.7 1.0 %collective-permute-done.13.rest_2_ = f32[72,128]{1,0:T(8,128)S(1)} collective-permute-done((f32[72,128]{1,0:T(8,128)S(1)}, f32[72,128]{1,0:T(8,128)S(1)}, u32[]{:S(2)}, u32[]{:S(2)}) %collective-permute-start.13) | collective-permute-done | bytes 36896 | tf_op jit(solution)/shard_map/ppermute | solution.py:36
  49.8 3.6 %collective-permute-done.14.rest_3_ = f32[72,128]{1,0:T(8,128)S(1)} collective-permute-done((f32[72,128]{1,0:T(8,128)S(1)}, f32[72,128]{1,0:T(8,128)S(1)}, u32[]{:S(2)}, u32[]{:S(2)}) %collective-permute-start.14) | collective-permute-done | bytes 36896 | tf_op jit(solution)/shard_map/ppermute | solution.py:36
  53.4 1.1 %shard_map.109 = bf16[64,128]{1,0:T(8,128)(2,1)} custom-call(f32[64,128]{1,0:T(8,128)S(1)} %get-tuple-element.43.zdst_ref, f32[1,128]{1,0:T(1,128)S(1)} %bitcast.5, f32[1,128]{1,0:T(1,128)S(1)} %bitcast.7, f32[1,128]{1,0:T(1,128)S(1)} %bitcast.8, f32[72,128]{1,0:T(8,128)S(1)} %get-tuple-element.65.rest_0_, f32[72,128]{1,0:T(8,128)S(1)} %collective-permute-done.12.rest_1_, ...), custom_call_target="tpu_custom_call" | custom-call | tf_op jit(solution)/shard_map/pallas_call | solution.py:40
  (14 shorter events, 0.0 us)
Async XLA Ops:
  1.1 10.0 %collective-permute-start.1 = (f32[256,128]{1,0:T(8,128)S(1)}, f32[256,128]{1,0:T(8,128)S(1)}, u32[]{:S(2)}, u32[]{:S(2)}) collective-permute-start(f32[256,128]{1,0:T(8,128)S(1)} %get-tuple-element.46), channel_id=1, source_target_pairs={{0,1},{1,0},{2,3},{3,2},{4,5},{5,4},{6,7},{7,6},{8,9},{9,8},{10,11... | collective-permute-start | bytes 393224 | tf_op jit(solution)/shard_map/ppermute | solution.py:36
  4.2 9.0 %collective-permute-start.7 = (f32[256,128]{1,0:T(8,128)S(1)}, f32[256,128]{1,0:T(8,128)S(1)}, u32[]{:S(2)}, u32[]{:S(2)}) collective-permute-start(f32[256,128]{1,0:T(8,128)S(1)} %get-tuple-element.53), channel_id=1, source_target_pairs={{0,1},{1,0},{2,3},{3,2},{4,5},{5,4},{6,7},{7,6},{8,9},{9,8},{10,11... | collective-permute-start | bytes 393224 | tf_op jit(solution)/shard_map/ppermute | solution.py:36
  4.3 6.9 %collective-permute-start = (f32[64,128]{1,0:T(8,128)S(1)}, f32[64,128]{1,0:T(8,128)S(1)}, u32[]{:S(2)}, u32[]{:S(2)}) collective-permute-start(f32[64,128]{1,0:T(8,128)S(1)} %get-tuple-element.39), channel_id=1, source_target_pairs={{0,1},{1,0},{2,3},{3,2},{4,5},{5,4},{6,7},{7,6},{8,9},{9,8},{10,11... | collective-permute-start | bytes 98312 | tf_op jit(solution)/shard_map/ppermute | solution.py:36
  11.4 17.6 %collective-permute-start.2 = (f32[272,128]{1,0:T(8,128)S(1)}, f32[272,128]{1,0:T(8,128)S(1)}, u32[]{:S(2)}, u32[]{:S(2)}) collective-permute-start(f32[272,128]{1,0:T(8,128)S(1)} %shard_map.103.refs_4_.refs_6_), channel_id=1, source_target_pairs={{0,16},{8,24},{16,0},{24,8},{1,17},{9,25},{17,1},{25,9},{2,18},{10... | collective-permute-start | bytes 417800 | tf_op jit(solution)/shard_map/ppermute | solution.py:36
  13.4 15.7 %collective-permute-start.8 = (f32[272,128]{1,0:T(8,128)S(1)}, f32[272,128]{1,0:T(8,128)S(1)}, u32[]{:S(2)}, u32[]{:S(2)}) collective-permute-start(f32[272,128]{1,0:T(8,128)S(1)} %shard_map.104.refs_6_.refs_8_), channel_id=1, source_target_pairs={{0,8},{8,0},{16,24},{24,16},{1,9},{9,1},{17,25},{25,17},{2,10},{10... | collective-permute-start | bytes 417800 | tf_op jit(solution)/shard_map/ppermute | solution.py:36
  13.4 15.7 %collective-permute-start.6 = (f32[272,128]{1,0:T(8,128)S(1)}, f32[272,128]{1,0:T(8,128)S(1)}, u32[]{:S(2)}, u32[]{:S(2)}) collective-permute-start(f32[272,128]{1,0:T(8,128)S(1)} %shard_map.103.refs_4_.refs_6_), channel_id=1, source_target_pairs={{0,8},{8,0},{16,24},{24,16},{1,9},{9,1},{17,25},{25,17},{2,10},{10... | collective-permute-start | bytes 417800 | tf_op jit(solution)/shard_map/ppermute | solution.py:36
  13.9 18.4 %collective-permute-start.9 = (f32[272,128]{1,0:T(8,128)S(1)}, f32[272,128]{1,0:T(8,128)S(1)}, u32[]{:S(2)}, u32[]{:S(2)}) collective-permute-start(f32[272,128]{1,0:T(8,128)S(1)} %shard_map.104.refs_6_.refs_8_), channel_id=1, source_target_pairs={{0,16},{8,24},{16,0},{24,8},{1,17},{9,25},{17,1},{25,9},{2,18},{10... | collective-permute-start | bytes 417800 | tf_op jit(solution)/shard_map/ppermute | solution.py:36
  14.3 5.5 %collective-permute-start.5 = (f32[8,64]{1,0:T(8,128)S(1)}, f32[8,64]{1,0:T(8,128)S(1)}, u32[]{:S(2)}, u32[]{:S(2)}) collective-permute-start(f32[8,64]{1,0:T(8,128)S(1)} %get-tuple-element.48.refs_0_), channel_id=1, source_target_pairs={{0,6},{2,4},{4,2},{6,0},{1,7},{3,5},{5,3},{7,1},{8,14},{10,12},{12... | collective-permute-start | bytes 6152 | tf_op jit(solution)/shard_map/ppermute | solution.py:36
  19.8 4.5 %collective-permute-start.4 = (f32[8,64]{1,0:T(8,128)S(1)}, f32[8,64]{1,0:T(8,128)S(1)}, u32[]{:S(2)}, u32[]{:S(2)}) collective-permute-start(f32[8,64]{1,0:T(8,128)S(1)} %get-tuple-element.48.refs_0_), channel_id=1, source_target_pairs={{0,4},{2,6},{4,0},{6,2},{1,5},{3,7},{5,1},{7,3},{8,12},{10,14},{12... | collective-permute-start | bytes 6152 | tf_op jit(solution)/shard_map/ppermute | solution.py:36
  24.3 4.6 %collective-permute-start.3 = (f32[8,64]{1,0:T(8,128)S(1)}, f32[8,64]{1,0:T(8,128)S(1)}, u32[]{:S(2)}, u32[]{:S(2)}) collective-permute-start(f32[8,64]{1,0:T(8,128)S(1)} %get-tuple-element.48.refs_0_), channel_id=1, source_target_pairs={{0,2},{2,0},{4,6},{6,4},{1,3},{3,1},{5,7},{7,5},{8,10},{10,8},{12,... | collective-permute-start | bytes 6152 | tf_op jit(solution)/shard_map/ppermute | solution.py:36
  29.0 4.0 %collective-permute-start.10 = (f32[272,128]{1,0:T(8,128)S(1)}, f32[272,128]{1,0:T(8,128)S(1)}, u32[]{:S(2)}, u32[]{:S(2)}) collective-permute-start(f32[272,128]{1,0:T(8,128)S(1)} %collective-permute-done.2.refs_3_.refs_10_), channel_id=1, source_target_pairs={{0,8},{8,0},{16,24},{24,16},{1,9},{9,1},{17,25},{25,17},{2,10},{10... | collective-permute-start | bytes 417800 | tf_op jit(solution)/shard_map/ppermute | solution.py:36
  32.4 1.9 %collective-permute-start.11 = (f32[272,128]{1,0:T(8,128)S(1)}, f32[272,128]{1,0:T(8,128)S(1)}, u32[]{:S(2)}, u32[]{:S(2)}) collective-permute-start(f32[272,128]{1,0:T(8,128)S(1)} %collective-permute-done.9.refs_4_), channel_id=1, source_target_pairs={{0,8},{8,0},{16,24},{24,16},{1,9},{9,1},{17,25},{25,17},{2,10},{10... | collective-permute-start | bytes 417800 | tf_op jit(solution)/shard_map/ppermute | solution.py:36
  34.3 19.1 %copy-start = (f32[128]{0:T(128)S(1)}, f32[128]{0:T(128)}, u32[]{:S(2)}) copy-start(f32[128]{0:T(128)} %param.13) | copy-start | bytes 1540
  34.3 19.1 %copy-start.1 = (f32[128]{0:T(128)S(1)}, f32[128]{0:T(128)}, u32[]{:S(2)}) copy-start(f32[128]{0:T(128)} %param.14) | copy-start | bytes 1540
  34.3 19.1 %copy-start.2 = (f32[128]{0:T(128)S(1)}, f32[128]{0:T(128)}, u32[]{:S(2)}) copy-start(f32[128]{0:T(128)} %param.15) | copy-start | bytes 1540
  44.3 4.4 %collective-permute-start.12 = (f32[72,128]{1,0:T(8,128)S(1)}, f32[72,128]{1,0:T(8,128)S(1)}, u32[]{:S(2)}, u32[]{:S(2)}) collective-permute-start(f32[72,128]{1,0:T(8,128)S(1)} %get-tuple-element.66), channel_id=1, source_target_pairs={{0,2},{2,0},{4,6},{6,4},{1,3},{3,1},{5,7},{7,5},{8,10},{10,8},{12,... | collective-permute-start | bytes 110600 | tf_op jit(solution)/shard_map/ppermute | solution.py:36
  44.9 4.9 %collective-permute-start.13 = (f32[72,128]{1,0:T(8,128)S(1)}, f32[72,128]{1,0:T(8,128)S(1)}, u32[]{:S(2)}, u32[]{:S(2)}) collective-permute-start(f32[72,128]{1,0:T(8,128)S(1)} %get-tuple-element.67), channel_id=1, source_target_pairs={{0,4},{2,6},{4,0},{6,2},{1,5},{3,7},{5,1},{7,3},{8,12},{10,14},{12... | collective-permute-start | bytes 110600 | tf_op jit(solution)/shard_map/ppermute | solution.py:36
  47.6 5.8 %collective-permute-start.14 = (f32[72,128]{1,0:T(8,128)S(1)}, f32[72,128]{1,0:T(8,128)S(1)}, u32[]{:S(2)}, u32[]{:S(2)}) collective-permute-start(f32[72,128]{1,0:T(8,128)S(1)} %get-tuple-element.68), channel_id=1, source_target_pairs={{0,6},{2,4},{4,2},{6,0},{1,7},{3,5},{5,3},{7,1},{8,14},{10,12},{12... | collective-permute-start | bytes 110600 | tf_op jit(solution)/shard_map/ppermute | solution.py:36

commit v6 on v5

--- a/solution.py
+++ b/solution.py
@@ -158,10 +158,41 @@
     dst_parts = [hop(sent[0][d - 1], "feat", d) for d in range(1, n_feat)]
     src_parts = [[hop(part[d - 1], "feat", d) for d in range(1, n_feat)] for part in sent[1:]]
 
-    def own_kernel(*refs):
-        hbm, outs, refs = refs[:5], refs[5 : 8 + n_chunk], refs[8 + n_chunk :]
-        fetch(hbm, refs[:5], refs[5])
-        src_ref, dst_ref, proj_ref, att_src_ref, att_dst_ref = refs[:5]
+    units = n_row * n_chunk
+    tiles = row_tiles * col_tiles
+    period = min(slots, tiles) if slots % min(slots, tiles) == 0 else slots
+    reps = slots // period
+    group = 8
+    groups = period // group
+
+    def local_kernel(*refs):
+        hbm, count_ref, refs = refs[:8], refs[8], refs[9:]
+        outs, panel_ref, refs = refs[: 3 + n_chunk], refs[3 + n_chunk], refs[4 + n_chunk :]
+        src_ref, dst_ref, proj_ref, att_src_ref, att_dst_ref, rows_ref, cols_ref, w_ref = refs[:8]
+        sems, w_sems = refs[8:]
+        small = [
+            pltpu.make_async_copy(h, v, sems.at[k]) for k, (h, v) in enumerate(zip(hbm[:7], refs[:7]))
+        ]
+        large = [
+            pltpu.make_async_copy(
+                hbm[7].at[k, pl.ds(g * group, group)],
+                w_ref.at[k, pl.ds(g * group, group)],
+                w_sems.at[g, k],
+            )
+            for g in range(groups)
+            for k in range(reps)
+        ]
+        for copy in small + large:
+            copy.start()
+
+        @pl.loop(0, units)
+        def _(u):
+            @pl.loop(0, row_tiles)
+            def _(r):
+                panel_ref[u, r] = jnp.zeros((chunk_tiles, TILE, TILE), F32)
+
+        for copy in small:
+            copy.wait()
         w = take_cols(proj_ref, lax.axis_index("feat"), width)
         outs[0][...] = project(dst_ref[...], w)
         outs[1][...] = LOG2E * head_rows(att_dst_ref[...], heads, width, up8(heads))
@@ -169,23 +200,50 @@
         for ch in range(n_chunk):
             outs[3 + ch][...] = project(src_ref[ch * part_rows : (ch + 1) * part_rows], w)
 
-    dst_own, dst_att, src_att, *src_own = fetching(
-        own_kernel,
+        row = lax.axis_index("row")
+        count = count_ref[0, 0]
+        for g in range(groups):
+            for copy in large[g * reps : (g + 1) * reps]:
+                copy.wait()
+            base = g * group
+
+            @pl.loop(base, jnp.clip(count, base, base + group))
+            def _(u):
+                r, c = rows_ref[0, 0, u], cols_ref[0, 0, u]
+                unit = ((c // piece_tiles) ^ row) * n_chunk + c % piece_tiles // chunk_tiles
+                t = c % chunk_tiles
+                total = w_ref[0, u].astype(F32)
+                for k in range(1, reps):
+                    live = (u + k * period < count).astype(F32)
+                    total = total + w_ref[k, u].astype(F32) * live
+                panel_ref[unit, r, t] = panel_ref[unit, r, t] + total
+
+    slot_weights = edge_weight.reshape(reps, period, TILE, TILE)
+    inputs = (src_feats, dst_feats, proj, att_src2, att_dst2, tile_rows, tile_cols, slot_weights)
+    dst_own, dst_att, src_att, *src_own, panel = call(
+        local_kernel,
         [
             pltpu.VMEM((own_rows, width), F32),
             pltpu.VMEM((up8(heads), width), F32),
             pltpu.VMEM((hp, width), F32),
         ]
-        + [pltpu.VMEM((part_rows, width), F32)] * n_chunk,
-        src_feats,
-        dst_feats,
-        proj,
-        att_src2,
-        att_dst2,
+        + [pltpu.VMEM((part_rows, width), F32)] * n_chunk
+        + [pltpu.VMEM((units, row_tiles, chunk_tiles, TILE, TILE), F32)],
+        *map(in_hbm, inputs),
+        tile_count,
+        in_specs=[HBM] * len(inputs) + [SMEM],
+        scratch_shapes=[
+            *(
+                (pltpu.SMEM if v.dtype == jnp.int32 else pltpu.VMEM)(v.shape, v.dtype)
+                for v in inputs
+            ),
+            pltpu.SemaphoreType.DMA((7,)),
+            pltpu.SemaphoreType.DMA((groups, reps)),
+        ],
+        grant=12 << 20,
     )
     dst_parts, src_own = lax.optimization_barrier((dst_parts, src_own))
 
-    tiles = row_tiles * col_tiles
     whole = lambda shape: pl.BlockSpec(shape, lambda s: (0,) * len(shape))
 
     def dst_kernel(own_ref, att_ref, *rest):
@@ -233,7 +291,6 @@
         parts[far_first, ch] = hop(own, "row", far_first)
         parts[0, ch] = own
     last = n_chunk - 1
-    parts[0, last], tile_rows = lax.optimization_barrier((parts[0, last], tile_rows))
 
     def spread(first, ch):
         d = n_row // 4
@@ -244,76 +301,6 @@
 
     for ch in range(n_chunk):
         spread(0, ch)
-
-    units = n_row * n_chunk
-    period = min(slots, tiles) if slots % min(slots, tiles) == 0 else slots
-    reps = slots // period
-    group = 8
-    groups = period // group
-
-    def weight_kernel(rows_hbm, cols_hbm, count_ref, w_hbm, panel_ref, *scratch):
-        rows_ref, cols_ref, w_ref, index_sems, w_sems = scratch
-        row = lax.axis_index("row")
-        indices = [
-            pltpu.make_async_copy(rows_hbm, rows_ref, index_sems.at[0]),
-            pltpu.make_async_copy(cols_hbm, cols_ref, index_sems.at[1]),
-        ]
-        blocks = [
-            pltpu.make_async_copy(
-                w_hbm.at[k, pl.ds(g * group, group)],
-                w_ref.at[k, pl.ds(g * group, group)],
-                w_sems.at[g, k],
-            )
-            for g in range(groups)
-            for k in range(reps)
-        ]
-        for copy in indices + blocks:
-            copy.start()
-
-        @pl.loop(0, units)
-        def _(u):
-            @pl.loop(0, row_tiles)
-            def _(r):
-                panel_ref[u, r] = jnp.zeros((chunk_tiles, TILE, TILE), F32)
-
-        for copy in indices:
-            copy.wait()
-        count = count_ref[0, 0]
-        for g in range(groups):
-            for copy in blocks[g * reps : (g + 1) * reps]:
-                copy.wait()
-            base = g * group
-
-            @pl.loop(base, jnp.clip(count, base, base + group))
-            def _(u):
-                r, c = rows_ref[0, 0, u], cols_ref[0, 0, u]
-                unit = ((c // piece_tiles) ^ row) * n_chunk + c % piece_tiles // chunk_tiles
-                t = c % chunk_tiles
-                total = w_ref[0, u].astype(F32)
-                for k in range(1, reps):
-                    live = (u + k * period < count).astype(F32)
-                    total = total + w_ref[k, u].astype(F32) * live
-                panel_ref[unit, r, t] = panel_ref[unit, r, t] + total
-
-    panel = call(
-        weight_kernel,
-        pltpu.VMEM((units, row_tiles, chunk_tiles, TILE, TILE), F32),
-        in_hbm(tile_rows),
-        in_hbm(tile_cols),
-        tile_count,
-        in_hbm(edge_weight.reshape(reps, period, TILE, TILE)),
-        in_specs=[HBM, HBM, SMEM, HBM],
-        scratch_shapes=[
-            pltpu.SMEM(tile_rows.shape, jnp.int32),
-            pltpu.SMEM(tile_cols.shape, jnp.int32),
-            pltpu.VMEM((reps, period, TILE, TILE), edge_weight.dtype),
-            pltpu.SemaphoreType.DMA((2,)),
-            pltpu.SemaphoreType.DMA((groups, reps)),
-        ],
-        flops=slots * TILE * TILE,
-        bytes_accessed=slots * TILE * TILE * 2,
-        grant=12 << 20,
-    )
 
     block = 64
     blocks = TILE // block
@@ -330,19 +317,19 @@
         at = part_rows + t * hp + h
         return part_ref[at : at + 1, :TILE], part_ref[at + heads : at + heads + 1, :TILE]
 
-    def split_z(part_ref, z_cat, k):
-        z = part_ref[:part_rows, :width]
-        hi = z.astype(BF16)
-        z_cat[k * part_rows : (k + 1) * part_rows, :width] = hi
-        z_cat[k * part_rows : (k + 1) * part_rows, width:] = (z - hi.astype(F32)).astype(BF16)
-
-    def put(probs, slot, h, q, p):
-        cols = slice(q * TILE, (q + 1) * TILE)
-        hi = p.astype(BF16)
-        probs[slot, 2 * h * block : (2 * h + 1) * block, cols] = hi
-        probs[slot, (2 * h + 1) * block : (2 * h + 2) * block, cols] = (
-            p - hi.astype(F32)
-        ).astype(BF16)
+    def split(x):
+        hi = x.astype(BF16)
+        return hi, (x - hi.astype(F32)).astype(BF16)
+
+    def split_z(part_refs):
+        return jnp.concatenate(
+            [jnp.concatenate(split(p[:part_rows, :width]), axis=1) for p in part_refs], axis=0
+        )
+
+    def stack(pairs):
+        return jnp.concatenate(
+            [jnp.concatenate([p[k] for p in row], axis=1) for row in pairs for k in range(2)], axis=0
+        )
 
     def weighted(probs, z):
         both = lax.dot_general(probs, z, (((1,), (0,)), ((), ())), preferred_element_type=F32)
@@ -353,12 +340,15 @@
             num = jnp.where(lane_w() == h, hi[:, :width] + (hi[:, width:] + lo[:, :width]), num)
         return num
 
-    def attend(part_refs, w_refs, posneg, den_in, num_in, den_out, num_out, z_cat, probs):
+    def attend(part_refs, w_refs, posneg, den_in, num_in, den_out, num_out):
         base = pl.program_id(0) * group_rows
+        z_cat = split_z(part_refs)
         for b in range(unroll * blocks):
             at = pl.ds(pl.multiple_of(base + b * block, block), block)
             rt, i0 = divmod(b * block, TILE)
+            pairs = []
             for h in range(heads):
+                pairs.append([])
                 pn = posneg[at, :]
                 pos = jnp.broadcast_to(pn[:, h : h + 1], (block, TILE))
                 neg = jnp.broadcast_to(pn[:, heads + h : heads + h + 1], (block, TILE))
@@ -369,9 +359,9 @@
                         x = jnp.maximum(pos + s, neg + s_low)
                         p = w_refs[k][0, rt, t, i0 : i0 + block, :] * jnp.exp2(x)
                         den = den + p
-                        put(probs, b % 2, h, k * chunk_tiles + t, p)
+                        pairs[h].append(split(p))
                 den_out[h, at, :] = den
-            num = weighted(probs[b % 2], z_cat[...])
+            num = weighted(stack(pairs), z_cat)
             num_out[at, :] = num if num_in is None else num_in[at, :] + num
 
     shape_t, shape_w, shape_d = (all_rows, TILE), (all_rows, width), (heads, all_rows, TILE)
@@ -392,11 +382,7 @@
             + [part_spec] * (n + len(extra))
             + [unit_spec(*key) for key in (*keys, *extra)],
             out_specs=[whole(s) for s in outs],
-            scratch_shapes=[
-                pltpu.VMEM((n * part_rows, 2 * width), BF16),
-                pltpu.VMEM((2, 2 * heads * block, n * part_rows), BF16),
-                *scratch,
-            ],
+            scratch_shapes=scratch,
             cost_estimate=pl.CostEstimate(
                 flops=all_rows * n * part_rows * width * heads * 8,
                 bytes_accessed=n * part_rows * width * 4,
@@ -410,7 +396,7 @@
     def near_kernel(*refs):
         n = len(near_keys)
         tgt_refs, part_refs, w_refs = refs[:n_col], refs[n_col : n_col + n], refs[n_col + n :][:n]
-        posneg, tgt_m, den_out, num_out, z_cat, probs, tgt = refs[n_col + 2 * n :]
+        posneg, tgt_m, den_out, num_out = refs[n_col + 2 * n :]
         col = lax.axis_index("col")
 
         @pl.when(pl.program_id(0) == 0)
@@ -435,40 +421,26 @@
                 )
                 a = contract(tgt_refs[d][...], eye, ((0,), (0,)))
                 m = leaky(a + bound)
-                tgt[at, :] = a
                 tgt_m[at, :] = jnp.where(lane < heads, a, m)
                 posneg[at, :] = jnp.where(lane < heads, a, SLOPE * a) - m
-            for k, part_ref in enumerate(part_refs):
-                split_z(part_ref, z_cat, k)
-
-        attend(part_refs, w_refs, posneg, None, None, den_out, num_out, z_cat, probs)
+
+        attend(part_refs, w_refs, posneg, None, None, den_out, num_out)
 
     def middle_kernel(*refs):
         n = len(middle_keys)
         (posneg, den_in, num_in), refs = refs[:3], refs[3:]
-        part_refs, w_refs, (den_out, num_out, z_cat, probs) = refs[:n], refs[n : 2 * n], refs[2 * n :]
-
-        @pl.when(pl.program_id(0) == 0)
-        def _():
-            for k, part_ref in enumerate(part_refs):
-                split_z(part_ref, z_cat, k)
-
-        attend(part_refs, w_refs, posneg, den_in, num_in, den_out, num_out, z_cat, probs)
+        part_refs, w_refs, (den_out, num_out) = refs[:n], refs[n : 2 * n], refs[2 * n :]
+        attend(part_refs, w_refs, posneg, den_in, num_in, den_out, num_out)
 
     def last_kernel(*refs):
         n, n_all = len(last_keys), len(last_keys) + len(other_keys)
         (posneg, den_in, num_in, tgt_m), refs = refs[:4], refs[4:]
         part_refs, w_refs, refs = refs[:n_all], refs[n_all : 2 * n_all], refs[2 * n_all :]
-        out_refs, (z_cat, probs, den_s, num_s, md_s, z_one) = refs[:n_col], refs[n_col:]
+        out_refs, (den_s, num_s, md_s) = refs[:n_col], refs[n_col:]
         col = lax.axis_index("col")
         step = pl.program_id(0)
 
-        @pl.when(step == 0)
-        def _():
-            for k in range(n):
-                split_z(part_refs[k], z_cat, k)
-
-        attend(part_refs[:n], w_refs[:n], posneg, den_in, num_in, den_s, num_s, z_cat, probs)
+        attend(part_refs[:n], w_refs[:n], posneg, den_in, num_in, den_s, num_s)
         base = step * group_rows
         low = high = None
         for b in range(unroll * blocks):
@@ -505,16 +477,17 @@
                     dens.append(jnp.zeros((block, TILE), F32))
                 num_s[at, :] = jnp.zeros((block, width), F32)
                 for part_ref, w_ref in zip(part_refs, w_refs):
+                    pairs = []
                     for h in range(heads):
+                        pairs.append([])
                         pos, neg = posnegs[h]
                         for t in range(chunk_tiles):
                             s, s_low = score_rows(part_ref, t, h)
                             x = jnp.minimum(jnp.maximum(pos + s, neg + s_low), 0.0)
                             p = w_ref[0, rt, t, rows, :] * jnp.exp2(x)
                             dens[h] = dens[h] + p
-                            put(probs, 0, h, t, p)
-                    split_z(part_ref, z_one, 0)
-                    num_s[at, :] = num_s[at, :] + weighted(probs[0, :, :part_rows], z_one[...])
+                            pairs[h].append(split(p))
+                    num_s[at, :] = num_s[at, :] + weighted(stack(pairs), split_z([part_ref]))
                 for h in range(heads):
                     md = jnp.where(lane_t() == h, jnp.sum(dens[h], axis=1, keepdims=True), md)
                 md_s[at, :] = md
@@ -539,7 +512,6 @@
         targets,
         [(up8(heads), own_rows)] * n_col,
         [shape_t, shape_t, shape_d, shape_w],
-        scratch=[pltpu.VMEM(shape_t, F32)],
     )
     parts[far_first, last], den = lax.optimization_barrier((parts[far_first, last], den))
     spread(far_first, last)
@@ -565,7 +537,6 @@
             pltpu.VMEM(shape_d, F32),
             pltpu.VMEM(shape_w, F32),
             pltpu.VMEM(shape_t, F32),
-            pltpu.VMEM((part_rows, 2 * width), BF16),
         ],
     )
     gathered = [hop(chunks[d], "col", d) for d in range(n_col - 1, 0, -1)]

time: 54.6 us -> 50.1 us (0.918)
  Pallas kernels: 21.1 us -> 16.1 us
  waiting for transfers between devices: 13.6 us -> 14.2 us
    pallas_call x3, Pallas kernels: 14.6 us -> 10.2 us  [stage(): pl.pallas_call(kernel, out_shape=[pltpu.VMEM(s, F32) for s in outs], grid...]
    ppermute x15, waiting for transfers between devices: 13.6 us -> 14.2 us  [hop(): return lax.ppermute(x, axis, pairs)]
    pallas_call x7 -> x6, Pallas kernels: 6.43 us -> 5.89 us  [call(): pl.pallas_call(kernel, out_shape=out_shape, in_specs=in_specs or [VMEM] *...]
  transfers between devices with their start and end apart: 15 -> 15, of which waited for: 5 -> 6; matrix products, arithmetic and copies ran while one was open for 0% -> 0% of each run, Pallas kernels for 16% -> 13%
where the time goes in v6:
time: 50.1 us; the launch traced here: 50 us
  starting transfers between devices  19 us (38%)
  Pallas kernels  16.1 us (32%)
  waiting for transfers between devices  14.2 us (28%)
  between operations  0.75 us (1%)
    ppermute x15, starting transfers between devices, hop(): return lax.ppermute(x, axis, pairs)  19 us
    ppermute x15, waiting for transfers between devices, hop(): return lax.ppermute(x, axis, pairs)  14.2 us
    pallas_call x3, Pallas kernels, stage(): pl.pallas_call(kernel, out_shape=[pltpu.VMEM(s, F32) for s in outs], grid...  10.2 us
    pallas_call x6, Pallas kernels, call(): pl.pallas_call(kernel, out_shape=out_shape, in_specs=in_specs or [VMEM] *...  5.89 us
  transfers between devices with their start and end apart: 15, of which 6 were waited for; matrix products, arithmetic and copies ran while one was open for 0% of the time, Pallas kernels for 13%

profile of v6, /device:TPU:0, one launch (start us, length us, event | category | flops | bytes accessed | tf_op | source)
XLA Modules:
  0.0 50.0 jit_solution(8306683446215727536)
XLA Ops:
  0.0 1.1 %shard_map.101 = (f32[64,128]{1,0:T(8,128)S(1)}, f32[256,128]{1,0:T(8,128)S(1)}, f32[256,128]{1,0:T(8,128)S(1)}) custom-call(bf16[512,128]{1,0:T(8,128)(2,1)} %refs_0_.3, bf16[64,128]{1,0:T(8,128)(2,1)} %refs_1_.3, bf16[128,256]{1,0:T(8,128)(2,1)} %refs_2_.3), custom_call_target="tpu_custom_call" | custom-call | tf_op jit(solution)/shard_map/pallas_call | solution.py:40
  1.1 3.0 %collective-permute-start.1 = (f32[256,128]{1,0:T(8,128)S(1)}, f32[256,128]{1,0:T(8,128)S(1)}, u32[]{:S(2)}, u32[]{:S(2)}) collective-permute-start(f32[256,128]{1,0:T(8,128)S(1)} %get-tuple-element.45), channel_id=1, source_target_pairs={{0,1},{1,0},{2,3},{3,2},{4,5},{5,4},{6,7},{7,6},{8,9},{9,8},{10,11... | collective-permute-start | bytes 393224 | tf_op jit(solution)/shard_map/ppermute | solution.py:36
  4.2 0.1 collective-permute-start.7
  4.3 1.9 %collective-permute-start = (f32[64,128]{1,0:T(8,128)S(1)}, f32[64,128]{1,0:T(8,128)S(1)}, u32[]{:S(2)}, u32[]{:S(2)}) collective-permute-start(f32[64,128]{1,0:T(8,128)S(1)} %get-tuple-element.38), channel_id=1, source_target_pairs={{0,1},{1,0},{2,3},{3,2},{4,5},{5,4},{6,7},{7,6},{8,9},{9,8},{10,11... | collective-permute-start | bytes 98312 | tf_op jit(solution)/shard_map/ppermute | solution.py:36
  6.9 3.1 %shard_map.100 = (f32[64,128]{1,0:T(8,128)S(1)}, f32[8,128]{1,0:T(8,128)S(1)}, f32[8,128]{1,0:T(8,128)S(1)}, f32[256,128]{1,0:T(8,128)S(1)}, f32[256,128]{1,0:T(8,128)S(1)}, /*index=5*/f32[8,2,2,128,128]{4,3,2,1,0:T(8,128)S(1)}) custom-call(bf16[512,128]{1,0:T(8,128)(2,1)} %refs_0_.3, bf16[64,128]{1,0:T(8,128)(2,1)} %refs_1_.3, bf16[128,256]{1,0:T(8,128)(2,1)} %refs_2_.3, ...), custom_call_target="tpu_custom_call" | custom-call | tf_op jit(solution)/shard_map/pallas_call | solution.py:40
  10.0 1.2 %collective-permute-done.rest_0_ = f32[64,128]{1,0:T(8,128)S(1)} collective-permute-done((f32[64,128]{1,0:T(8,128)S(1)}, f32[64,128]{1,0:T(8,128)S(1)}, u32[]{:S(2)}, u32[]{:S(2)}) %collective-permute-start) | collective-permute-done | bytes 32800 | tf_op jit(solution)/shard_map/ppermute | solution.py:36
  11.2 0.0 collective-permute-done.1.rest_0_
  11.2 0.2 shard_map.103.refs_4_.refs_6_
  11.4 1.8 %collective-permute-start.2 = (f32[272,128]{1,0:T(8,128)S(1)}, f32[272,128]{1,0:T(8,128)S(1)}, u32[]{:S(2)}, u32[]{:S(2)}) collective-permute-start(f32[272,128]{1,0:T(8,128)S(1)} %shard_map.103.refs_4_.refs_6_), channel_id=1, source_target_pairs={{0,16},{8,24},{16,0},{24,8},{1,17},{9,25},{17,1},{25,9},{2,18},{10... | collective-permute-start | bytes 417800 | tf_op jit(solution)/shard_map/ppermute | solution.py:36
  13.2 0.2 shard_map.104.refs_6_.refs_8_
  13.4 0.5 %collective-permute-start.6 = (f32[272,128]{1,0:T(8,128)S(1)}, f32[272,128]{1,0:T(8,128)S(1)}, u32[]{:S(2)}, u32[]{:S(2)}) collective-permute-start(f32[272,128]{1,0:T(8,128)S(1)} %shard_map.103.refs_4_.refs_6_), channel_id=1, source_target_pairs={{0,8},{8,0},{16,24},{24,16},{1,9},{9,1},{17,25},{25,17},{2,10},{10... | collective-permute-start | bytes 417800 | tf_op jit(solution)/shard_map/ppermute | solution.py:36
  13.9 0.3 collective-permute-start.9
  14.2 0.1 shard_map.102
  14.3 3.9 %collective-permute-start.5 = (f32[8,64]{1,0:T(8,128)S(1)}, f32[8,64]{1,0:T(8,128)S(1)}, u32[]{:S(2)}, u32[]{:S(2)}) collective-permute-start(f32[8,64]{1,0:T(8,128)S(1)} %get-tuple-element.47.refs_0_), channel_id=1, source_target_pairs={{0,6},{2,4},{4,2},{6,0},{1,7},{3,5},{5,3},{7,1},{8,14},{10,12},{12... | collective-permute-start | bytes 6152 | tf_op jit(solution)/shard_map/ppermute | solution.py:36
  18.2 1.6 %collective-permute-done.5.refs_3_ = f32[8,64]{1,0:T(8,128)S(1)} collective-permute-done((f32[8,64]{1,0:T(8,128)S(1)}, f32[8,64]{1,0:T(8,128)S(1)}, u32[]{:S(2)}, u32[]{:S(2)}) %collective-permute-start.5) | collective-permute-done | bytes 2080 | tf_op jit(solution)/shard_map/ppermute | solution.py:36
  19.8 1.0 %collective-permute-start.4 = (f32[8,64]{1,0:T(8,128)S(1)}, f32[8,64]{1,0:T(8,128)S(1)}, u32[]{:S(2)}, u32[]{:S(2)}) collective-permute-start(f32[8,64]{1,0:T(8,128)S(1)} %get-tuple-element.47.refs_0_), channel_id=1, source_target_pairs={{0,4},{2,6},{4,0},{6,2},{1,5},{3,7},{5,1},{7,3},{8,12},{10,14},{12... | collective-permute-start | bytes 6152 | tf_op jit(solution)/shard_map/ppermute | solution.py:36
  20.8 3.5 %collective-permute-done.4.refs_2_ = f32[8,64]{1,0:T(8,128)S(1)} collective-permute-done((f32[8,64]{1,0:T(8,128)S(1)}, f32[8,64]{1,0:T(8,128)S(1)}, u32[]{:S(2)}, u32[]{:S(2)}) %collective-permute-start.4) | collective-permute-done | bytes 2080 | tf_op jit(solution)/shard_map/ppermute | solution.py:36
  24.3 1.5 %collective-permute-start.3 = (f32[8,64]{1,0:T(8,128)S(1)}, f32[8,64]{1,0:T(8,128)S(1)}, u32[]{:S(2)}, u32[]{:S(2)}) collective-permute-start(f32[8,64]{1,0:T(8,128)S(1)} %get-tuple-element.47.refs_0_), channel_id=1, source_target_pairs={{0,2},{2,0},{4,6},{6,4},{1,3},{3,1},{5,7},{7,5},{8,10},{10,8},{12,... | collective-permute-start | bytes 6152 | tf_op jit(solution)/shard_map/ppermute | solution.py:36
  25.8 2.1 %collective-permute-done.3.refs_1_ = f32[8,64]{1,0:T(8,128)S(1)} collective-permute-done((f32[8,64]{1,0:T(8,128)S(1)}, f32[8,64]{1,0:T(8,128)S(1)}, u32[]{:S(2)}, u32[]{:S(2)}) %collective-permute-start.3) | collective-permute-done | bytes 2080 | tf_op jit(solution)/shard_map/ppermute | solution.py:36
  27.9 2.0 %shard_map.105 = (f32[256,128]{1,0:T(8,128)S(1)}, f32[256,128]{1,0:T(8,128)S(1)}, f32[4,256,128]{2,1,0:T(8,128)S(1)}, f32[256,128]{1,0:T(8,128)S(1)}) custom-call(f32[8,64]{1,0:T(8,128)S(1)} %get-tuple-element.47.refs_0_, f32[8,64]{1,0:T(8,128)S(1)} %collective-permute-done.3.refs_1_, f32[8,64]{1,0:T(8,128)S(1)} %collective-permute-done.4.refs_2_, ...), custom_call_target="tpu_custom_call" | custom-call | flops 1073741824 | bytes 524288 | tf_op jit(solution)/shard_map/pallas_call | solution.py:377
  30.0 0.6 %collective-permute-start.11 = (f32[272,128]{1,0:T(8,128)S(1)}, f32[272,128]{1,0:T(8,128)S(1)}, u32[]{:S(2)}, u32[]{:S(2)}) collective-permute-start(f32[272,128]{1,0:T(8,128)S(1)} %collective-permute-done.9.refs_4_), channel_id=1, source_target_pairs={{0,8},{8,0},{16,24},{24,16},{1,9},{9,1},{17,25},{25,17},{2,10},{10... | collective-permute-start | bytes 417800 | tf_op jit(solution)/shard_map/ppermute | solution.py:36
  30.5 1.0 %shard_map.106 = (f32[4,256,128]{2,1,0:T(8,128)S(1)}, f32[256,128]{1,0:T(8,128)S(1)}) custom-call(f32[256,128]{1,0:T(8,128)S(1)} %get-tuple-element.54.refs_0_, f32[4,256,128]{2,1,0:T(8,128)S(1)} %get-tuple-element.56.refs_1_, f32[256,128]{1,0:T(8,128)S(1)} %get-tuple-element.57.refs_2_, f32[272,128]{1,0:T(8,128)S(1)} %collective-permute-done.2.refs_3_.refs_10_, ...), custom_call_target="tpu_custom_call" | custom-call | flops 536870912 | bytes 262144 | tf_op jit(solution)/shard_map/pallas_call | solution.py:377
  31.6 0.0 copy-start
  31.6 0.0 copy-start.1
  31.6 0.0 copy-start.2
  31.6 7.1 %shard_map.107 = (f32[72,128]{1,0:T(8,128)S(1)}, f32[72,128]{1,0:T(8,128)S(1)}, f32[72,128]{1,0:T(8,128)S(1)}, f32[72,128]{1,0:T(8,128)S(1)}) custom-call(f32[256,128]{1,0:T(8,128)S(1)} %get-tuple-element.54.refs_0_, f32[4,256,128]{2,1,0:T(8,128)S(1)} %get-tuple-element.59.refs_1_, f32[256,128]{1,0:T(8,128)S(1)} %get-tuple-element.60.refs_2_, ...), custom_call_target="tpu_custom_call" | custom-call | flops 536870912 | bytes 262144 | tf_op jit(solution)/shard_map/pallas_call | solution.py:377
  38.7 1.5 %collective-permute-start.12 = (f32[72,128]{1,0:T(8,128)S(1)}, f32[72,128]{1,0:T(8,128)S(1)}, u32[]{:S(2)}, u32[]{:S(2)}) collective-permute-start(f32[72,128]{1,0:T(8,128)S(1)} %get-tuple-element.64), channel_id=1, source_target_pairs={{0,2},{2,0},{4,6},{6,4},{1,3},{3,1},{5,7},{7,5},{8,10},{10,8},{12,... | collective-permute-start | bytes 110600 | tf_op jit(solution)/shard_map/ppermute | solution.py:36
  40.2 2.9 %collective-permute-start.13 = (f32[72,128]{1,0:T(8,128)S(1)}, f32[72,128]{1,0:T(8,128)S(1)}, u32[]{:S(2)}, u32[]{:S(2)}) collective-permute-start(f32[72,128]{1,0:T(8,128)S(1)} %get-tuple-element.65), channel_id=1, source_target_pairs={{0,4},{2,6},{4,0},{6,2},{1,5},{3,7},{5,1},{7,3},{8,12},{10,14},{12... | collective-permute-start | bytes 110600 | tf_op jit(solution)/shard_map/ppermute | solution.py:36
  43.1 0.0 collective-permute-start.14
  43.1 2.7 %collective-permute-done.13.rest_2_ = f32[72,128]{1,0:T(8,128)S(1)} collective-permute-done((f32[72,128]{1,0:T(8,128)S(1)}, f32[72,128]{1,0:T(8,128)S(1)}, u32[]{:S(2)}, u32[]{:S(2)}) %collective-permute-start.13) | collective-permute-done | bytes 36896 | tf_op jit(solution)/shard_map/ppermute | solution.py:36
  45.8 3.0 %collective-permute-done.14.rest_3_ = f32[72,128]{1,0:T(8,128)S(1)} collective-permute-done((f32[72,128]{1,0:T(8,128)S(1)}, f32[72,128]{1,0:T(8,128)S(1)}, u32[]{:S(2)}, u32[]{:S(2)}) %collective-permute-start.14) | collective-permute-done | bytes 36896 | tf_op jit(solution)/shard_map/ppermute | solution.py:36
  48.9 1.1 %shard_map.108 = bf16[64,128]{1,0:T(8,128)(2,1)} custom-call(f32[64,128]{1,0:T(8,128)S(1)} %get-tuple-element.42.zdst_ref, f32[1,128]{1,0:T(1,128)S(1)} %bitcast.5, f32[1,128]{1,0:T(1,128)S(1)} %bitcast.7, f32[1,128]{1,0:T(1,128)S(1)} %bitcast.8, f32[72,128]{1,0:T(8,128)S(1)} %get-tuple-element.63.rest_0_, f32[72,128]{1,0:T(8,128)S(1)} %collective-permute-done.12.rest_1_, ...), custom_call_target="tpu_custom_call" | custom-call | tf_op jit(solution)/shard_map/pallas_call | solution.py:40
  (13 shorter events, 0.0 us)
Async XLA Ops:
  1.1 10.0 %collective-permute-start.1 = (f32[256,128]{1,0:T(8,128)S(1)}, f32[256,128]{1,0:T(8,128)S(1)}, u32[]{:S(2)}, u32[]{:S(2)}) collective-permute-start(f32[256,128]{1,0:T(8,128)S(1)} %get-tuple-element.45), channel_id=1, source_target_pairs={{0,1},{1,0},{2,3},{3,2},{4,5},{5,4},{6,7},{7,6},{8,9},{9,8},{10,11... | collective-permute-start | bytes 393224 | tf_op jit(solution)/shard_map/ppermute | solution.py:36
  4.2 9.0 %collective-permute-start.7 = (f32[256,128]{1,0:T(8,128)S(1)}, f32[256,128]{1,0:T(8,128)S(1)}, u32[]{:S(2)}, u32[]{:S(2)}) collective-permute-start(f32[256,128]{1,0:T(8,128)S(1)} %get-tuple-element.52), channel_id=1, source_target_pairs={{0,1},{1,0},{2,3},{3,2},{4,5},{5,4},{6,7},{7,6},{8,9},{9,8},{10,11... | collective-permute-start | bytes 393224 | tf_op jit(solution)/shard_map/ppermute | solution.py:36
  4.3 6.9 %collective-permute-start = (f32[64,128]{1,0:T(8,128)S(1)}, f32[64,128]{1,0:T(8,128)S(1)}, u32[]{:S(2)}, u32[]{:S(2)}) collective-permute-start(f32[64,128]{1,0:T(8,128)S(1)} %get-tuple-element.38), channel_id=1, source_target_pairs={{0,1},{1,0},{2,3},{3,2},{4,5},{5,4},{6,7},{7,6},{8,9},{9,8},{10,11... | collective-permute-start | bytes 98312 | tf_op jit(solution)/shard_map/ppermute | solution.py:36
  11.4 16.5 %collective-permute-start.2 = (f32[272,128]{1,0:T(8,128)S(1)}, f32[272,128]{1,0:T(8,128)S(1)}, u32[]{:S(2)}, u32[]{:S(2)}) collective-permute-start(f32[272,128]{1,0:T(8,128)S(1)} %shard_map.103.refs_4_.refs_6_), channel_id=1, source_target_pairs={{0,16},{8,24},{16,0},{24,8},{1,17},{9,25},{17,1},{25,9},{2,18},{10... | collective-permute-start | bytes 417800 | tf_op jit(solution)/shard_map/ppermute | solution.py:36
  13.4 14.5 %collective-permute-start.8 = (f32[272,128]{1,0:T(8,128)S(1)}, f32[272,128]{1,0:T(8,128)S(1)}, u32[]{:S(2)}, u32[]{:S(2)}) collective-permute-start(f32[272,128]{1,0:T(8,128)S(1)} %shard_map.104.refs_6_.refs_8_), channel_id=1, source_target_pairs={{0,8},{8,0},{16,24},{24,16},{1,9},{9,1},{17,25},{25,17},{2,10},{10... | collective-permute-start | bytes 417800 | tf_op jit(solution)/shard_map/ppermute | solution.py:36
  13.4 14.5 %collective-permute-start.6 = (f32[272,128]{1,0:T(8,128)S(1)}, f32[272,128]{1,0:T(8,128)S(1)}, u32[]{:S(2)}, u32[]{:S(2)}) collective-permute-start(f32[272,128]{1,0:T(8,128)S(1)} %shard_map.103.refs_4_.refs_6_), channel_id=1, source_target_pairs={{0,8},{8,0},{16,24},{24,16},{1,9},{9,1},{17,25},{25,17},{2,10},{10... | collective-permute-start | bytes 417800 | tf_op jit(solution)/shard_map/ppermute | solution.py:36
  13.9 16.1 %collective-permute-start.9 = (f32[272,128]{1,0:T(8,128)S(1)}, f32[272,128]{1,0:T(8,128)S(1)}, u32[]{:S(2)}, u32[]{:S(2)}) collective-permute-start(f32[272,128]{1,0:T(8,128)S(1)} %shard_map.104.refs_6_.refs_8_), channel_id=1, source_target_pairs={{0,16},{8,24},{16,0},{24,8},{1,17},{9,25},{17,1},{25,9},{2,18},{10... | collective-permute-start | bytes 417800 | tf_op jit(solution)/shard_map/ppermute | solution.py:36
  14.3 5.5 %collective-permute-start.5 = (f32[8,64]{1,0:T(8,128)S(1)}, f32[8,64]{1,0:T(8,128)S(1)}, u32[]{:S(2)}, u32[]{:S(2)}) collective-permute-start(f32[8,64]{1,0:T(8,128)S(1)} %get-tuple-element.47.refs_0_), channel_id=1, source_target_pairs={{0,6},{2,4},{4,2},{6,0},{1,7},{3,5},{5,3},{7,1},{8,14},{10,12},{12... | collective-permute-start | bytes 6152 | tf_op jit(solution)/shard_map/ppermute | solution.py:36
  19.8 4.5 %collective-permute-start.4 = (f32[8,64]{1,0:T(8,128)S(1)}, f32[8,64]{1,0:T(8,128)S(1)}, u32[]{:S(2)}, u32[]{:S(2)}) collective-permute-start(f32[8,64]{1,0:T(8,128)S(1)} %get-tuple-element.47.refs_0_), channel_id=1, source_target_pairs={{0,4},{2,6},{4,0},{6,2},{1,5},{3,7},{5,1},{7,3},{8,12},{10,14},{12... | collective-permute-start | bytes 6152 | tf_op jit(solution)/shard_map/ppermute | solution.py:36
  24.3 3.6 %collective-permute-start.3 = (f32[8,64]{1,0:T(8,128)S(1)}, f32[8,64]{1,0:T(8,128)S(1)}, u32[]{:S(2)}, u32[]{:S(2)}) collective-permute-start(f32[8,64]{1,0:T(8,128)S(1)} %get-tuple-element.47.refs_0_), channel_id=1, source_target_pairs={{0,2},{2,0},{4,6},{6,4},{1,3},{3,1},{5,7},{7,5},{8,10},{10,8},{12,... | collective-permute-start | bytes 6152 | tf_op jit(solution)/shard_map/ppermute | solution.py:36
  27.9 2.6 %collective-permute-start.10 = (f32[272,128]{1,0:T(8,128)S(1)}, f32[272,128]{1,0:T(8,128)S(1)}, u32[]{:S(2)}, u32[]{:S(2)}) collective-permute-start(f32[272,128]{1,0:T(8,128)S(1)} %collective-permute-done.2.refs_3_.refs_10_), channel_id=1, source_target_pairs={{0,8},{8,0},{16,24},{24,16},{1,9},{9,1},{17,25},{25,17},{2,10},{10... | collective-permute-start | bytes 417800 | tf_op jit(solution)/shard_map/ppermute | solution.py:36
  30.0 1.6 %collective-permute-start.11 = (f32[272,128]{1,0:T(8,128)S(1)}, f32[272,128]{1,0:T(8,128)S(1)}, u32[]{:S(2)}, u32[]{:S(2)}) collective-permute-start(f32[272,128]{1,0:T(8,128)S(1)} %collective-permute-done.9.refs_4_), channel_id=1, source_target_pairs={{0,8},{8,0},{16,24},{24,16},{1,9},{9,1},{17,25},{25,17},{2,10},{10... | collective-permute-start | bytes 417800 | tf_op jit(solution)/shard_map/ppermute | solution.py:36
  31.6 17.3 %copy-start = (f32[128]{0:T(128)S(1)}, f32[128]{0:T(128)}, u32[]{:S(2)}) copy-start(f32[128]{0:T(128)} %param.13) | copy-start | bytes 1540
  31.6 17.3 %copy-start.1 = (f32[128]{0:T(128)S(1)}, f32[128]{0:T(128)}, u32[]{:S(2)}) copy-start(f32[128]{0:T(128)} %param.14) | copy-start | bytes 1540
  31.6 17.3 %copy-start.2 = (f32[128]{0:T(128)S(1)}, f32[128]{0:T(128)}, u32[]{:S(2)}) copy-start(f32[128]{0:T(128)} %param.15) | copy-start | bytes 1540
  38.7 4.4 %collective-permute-start.12 = (f32[72,128]{1,0:T(8,128)S(1)}, f32[72,128]{1,0:T(8,128)S(1)}, u32[]{:S(2)}, u32[]{:S(2)}) collective-permute-start(f32[72,128]{1,0:T(8,128)S(1)} %get-tuple-element.64), channel_id=1, source_target_pairs={{0,2},{2,0},{4,6},{6,4},{1,3},{3,1},{5,7},{7,5},{8,10},{10,8},{12,... | collective-permute-start | bytes 110600 | tf_op jit(solution)/shard_map/ppermute | solution.py:36
  40.2 5.6 %collective-permute-start.13 = (f32[72,128]{1,0:T(8,128)S(1)}, f32[72,128]{1,0:T(8,128)S(1)}, u32[]{:S(2)}, u32[]{:S(2)}) collective-permute-start(f32[72,128]{1,0:T(8,128)S(1)} %get-tuple-element.65), channel_id=1, source_target_pairs={{0,4},{2,6},{4,0},{6,2},{1,5},{3,7},{5,1},{7,3},{8,12},{10,14},{12... | collective-permute-start | bytes 110600 | tf_op jit(solution)/shard_map/ppermute | solution.py:36
  43.1 5.8 %collective-permute-start.14 = (f32[72,128]{1,0:T(8,128)S(1)}, f32[72,128]{1,0:T(8,128)S(1)}, u32[]{:S(2)}, u32[]{:S(2)}) collective-permute-start(f32[72,128]{1,0:T(8,128)S(1)} %get-tuple-element.66), channel_id=1, source_target_pairs={{0,6},{2,4},{4,2},{6,0},{1,7},{3,5},{5,3},{7,1},{8,14},{10,12},{12... | collective-permute-start | bytes 110600 | tf_op jit(solution)/shard_map/ppermute | solution.py:36

commit v7 on v5

--- a/solution.py
+++ b/solution.py
@@ -206,9 +206,22 @@
         dst_att,
         *dst_parts,
     )
-    targets = [hop(s_dst, "col", d) for d in range(n_col - 1, 0, -1)]
-    targets = [s_dst] + targets[::-1]
-
+    rows_of = up8(heads)
+    if is_pow2(n_col) and n_col > 1:
+        targets, d = [s_dst], 1
+        while d < n_col:
+            targets = [targets[0], hop(targets[0], "col", d)]
+            d *= 2
+            if d < n_col:
+
+                def join_kernel(low_ref, high_ref, out_ref):
+                    out_ref[...] = jnp.concatenate([low_ref[...], high_ref[...]], axis=0)
+
+                shape = (d * rows_of, own_rows)
+                targets = [call(join_kernel, pltpu.VMEM(shape, F32), *targets)]
+    else:
+        targets = [s_dst] + [hop(s_dst, "col", d) for d in range(1, n_col)]
+    size = n_col // len(targets)
 
     pack_rows = part_rows + chunk_tiles * hp
 
@@ -233,7 +246,6 @@
         parts[far_first, ch] = hop(own, "row", far_first)
         parts[0, ch] = own
     last = n_chunk - 1
-    parts[0, last], tile_rows = lax.optimization_barrier((parts[0, last], tile_rows))
 
     def spread(first, ch):
         d = n_row // 4
@@ -330,19 +342,19 @@
         at = part_rows + t * hp + h
         return part_ref[at : at + 1, :TILE], part_ref[at + heads : at + heads + 1, :TILE]
 
-    def split_z(part_ref, z_cat, k):
-        z = part_ref[:part_rows, :width]
-        hi = z.astype(BF16)
-        z_cat[k * part_rows : (k + 1) * part_rows, :width] = hi
-        z_cat[k * part_rows : (k + 1) * part_rows, width:] = (z - hi.astype(F32)).astype(BF16)
-
-    def put(probs, slot, h, q, p):
-        cols = slice(q * TILE, (q + 1) * TILE)
-        hi = p.astype(BF16)
-        probs[slot, 2 * h * block : (2 * h + 1) * block, cols] = hi
-        probs[slot, (2 * h + 1) * block : (2 * h + 2) * block, cols] = (
-            p - hi.astype(F32)
-        ).astype(BF16)
+    def split(x):
+        hi = x.astype(BF16)
+        return hi, (x - hi.astype(F32)).astype(BF16)
+
+    def split_z(part_refs):
+        return jnp.concatenate(
+            [jnp.concatenate(split(p[:part_rows, :width]), axis=1) for p in part_refs], axis=0
+        )
+
+    def stack(pairs):
+        return jnp.concatenate(
+            [jnp.concatenate([p[k] for p in row], axis=1) for row in pairs for k in range(2)], axis=0
+        )
 
     def weighted(probs, z):
         both = lax.dot_general(probs, z, (((1,), (0,)), ((), ())), preferred_element_type=F32)
@@ -353,12 +365,15 @@
             num = jnp.where(lane_w() == h, hi[:, :width] + (hi[:, width:] + lo[:, :width]), num)
         return num
 
-    def attend(part_refs, w_refs, posneg, den_in, num_in, den_out, num_out, z_cat, probs):
+    def attend(part_refs, w_refs, posneg, den_in, num_in, den_out, num_out):
         base = pl.program_id(0) * group_rows
+        z_cat = split_z(part_refs)
         for b in range(unroll * blocks):
             at = pl.ds(pl.multiple_of(base + b * block, block), block)
             rt, i0 = divmod(b * block, TILE)
+            pairs = []
             for h in range(heads):
+                pairs.append([])
                 pn = posneg[at, :]
                 pos = jnp.broadcast_to(pn[:, h : h + 1], (block, TILE))
                 neg = jnp.broadcast_to(pn[:, heads + h : heads + h + 1], (block, TILE))
@@ -369,9 +384,9 @@
                         x = jnp.maximum(pos + s, neg + s_low)
                         p = w_refs[k][0, rt, t, i0 : i0 + block, :] * jnp.exp2(x)
                         den = den + p
-                        put(probs, b % 2, h, k * chunk_tiles + t, p)
+                        pairs[h].append(split(p))
                 den_out[h, at, :] = den
-            num = weighted(probs[b % 2], z_cat[...])
+            num = weighted(stack(pairs), z_cat)
             num_out[at, :] = num if num_in is None else num_in[at, :] + num
 
     shape_t, shape_w, shape_d = (all_rows, TILE), (all_rows, width), (heads, all_rows, TILE)
@@ -392,11 +407,7 @@
             + [part_spec] * (n + len(extra))
             + [unit_spec(*key) for key in (*keys, *extra)],
             out_specs=[whole(s) for s in outs],
-            scratch_shapes=[
-                pltpu.VMEM((n * part_rows, 2 * width), BF16),
-                pltpu.VMEM((2, 2 * heads * block, n * part_rows), BF16),
-                *scratch,
-            ],
+            scratch_shapes=scratch,
             cost_estimate=pl.CostEstimate(
                 flops=all_rows * n * part_rows * width * heads * 8,
                 bytes_accessed=n * part_rows * width * 4,
@@ -409,8 +420,9 @@
 
     def near_kernel(*refs):
         n = len(near_keys)
-        tgt_refs, part_refs, w_refs = refs[:n_col], refs[n_col : n_col + n], refs[n_col + n :][:n]
-        posneg, tgt_m, den_out, num_out, z_cat, probs, tgt = refs[n_col + 2 * n :]
+        n_tgt = len(targets)
+        tgt_refs, part_refs, w_refs = refs[:n_tgt], refs[n_tgt : n_tgt + n], refs[n_tgt + n :][:n]
+        posneg, tgt_m, den_out, num_out = refs[n_tgt + 2 * n :]
         col = lax.axis_index("col")
 
         @pl.when(pl.program_id(0) == 0)
@@ -433,42 +445,29 @@
                 at = pl.ds(
                     pl.multiple_of(comes_from(col, d, n_col) * own_rows, own_rows), own_rows
                 )
-                a = contract(tgt_refs[d][...], eye, ((0,), (0,)))
+                k, g = divmod(d, size)
+                a = contract(tgt_refs[k][g * rows_of : (g + 1) * rows_of], eye, ((0,), (0,)))
                 m = leaky(a + bound)
-                tgt[at, :] = a
                 tgt_m[at, :] = jnp.where(lane < heads, a, m)
                 posneg[at, :] = jnp.where(lane < heads, a, SLOPE * a) - m
-            for k, part_ref in enumerate(part_refs):
-                split_z(part_ref, z_cat, k)
-
-        attend(part_refs, w_refs, posneg, None, None, den_out, num_out, z_cat, probs)
+
+        attend(part_refs, w_refs, posneg, None, None, den_out, num_out)
 
     def middle_kernel(*refs):
         n = len(middle_keys)
         (posneg, den_in, num_in), refs = refs[:3], refs[3:]
-        part_refs, w_refs, (den_out, num_out, z_cat, probs) = refs[:n], refs[n : 2 * n], refs[2 * n :]
-
-        @pl.when(pl.program_id(0) == 0)
-        def _():
-            for k, part_ref in enumerate(part_refs):
-                split_z(part_ref, z_cat, k)
-
-        attend(part_refs, w_refs, posneg, den_in, num_in, den_out, num_out, z_cat, probs)
+        part_refs, w_refs, (den_out, num_out) = refs[:n], refs[n : 2 * n], refs[2 * n :]
+        attend(part_refs, w_refs, posneg, den_in, num_in, den_out, num_out)
 
     def last_kernel(*refs):
         n, n_all = len(last_keys), len(last_keys) + len(other_keys)
         (posneg, den_in, num_in, tgt_m), refs = refs[:4], refs[4:]
         part_refs, w_refs, refs = refs[:n_all], refs[n_all : 2 * n_all], refs[2 * n_all :]
-        out_refs, (z_cat, probs, den_s, num_s, md_s, z_one) = refs[:n_col], refs[n_col:]
+        out_refs, (den_s, num_s, md_s) = refs[:n_col], refs[n_col:]
         col = lax.axis_index("col")
         step = pl.program_id(0)
 
-        @pl.when(step == 0)
-        def _():
-            for k in range(n):
-                split_z(part_refs[k], z_cat, k)
-
-        attend(part_refs[:n], w_refs[:n], posneg, den_in, num_in, den_s, num_s, z_cat, probs)
+        attend(part_refs[:n], w_refs[:n], posneg, den_in, num_in, den_s, num_s)
         base = step * group_rows
         low = high = None
         for b in range(unroll * blocks):
@@ -505,16 +504,17 @@
                     dens.append(jnp.zeros((block, TILE), F32))
                 num_s[at, :] = jnp.zeros((block, width), F32)
                 for part_ref, w_ref in zip(part_refs, w_refs):
+                    pairs = []
                     for h in range(heads):
+                        pairs.append([])
                         pos, neg = posnegs[h]
                         for t in range(chunk_tiles):
                             s, s_low = score_rows(part_ref, t, h)
                             x = jnp.minimum(jnp.maximum(pos + s, neg + s_low), 0.0)
                             p = w_ref[0, rt, t, rows, :] * jnp.exp2(x)
                             dens[h] = dens[h] + p
-                            put(probs, 0, h, t, p)
-                    split_z(part_ref, z_one, 0)
-                    num_s[at, :] = num_s[at, :] + weighted(probs[0, :, :part_rows], z_one[...])
+                            pairs[h].append(split(p))
+                    num_s[at, :] = num_s[at, :] + weighted(stack(pairs), split_z([part_ref]))
                 for h in range(heads):
                     md = jnp.where(lane_t() == h, jnp.sum(dens[h], axis=1, keepdims=True), md)
                 md_s[at, :] = md
@@ -537,9 +537,8 @@
         near_kernel,
         near_keys,
         targets,
-        [(up8(heads), own_rows)] * n_col,
+        [(size * rows_of, own_rows)] * len(targets),
         [shape_t, shape_t, shape_d, shape_w],
-        scratch=[pltpu.VMEM(shape_t, F32)],
     )
     parts[far_first, last], den = lax.optimization_barrier((parts[far_first, last], den))
     spread(far_first, last)
@@ -565,7 +564,6 @@
             pltpu.VMEM(shape_d, F32),
             pltpu.VMEM(shape_w, F32),
             pltpu.VMEM(shape_t, F32),
-            pltpu.VMEM((part_rows, 2 * width), BF16),
         ],
     )
     gathered = [hop(chunks[d], "col", d) for d in range(n_col - 1, 0, -1)]

time: 54.6 us -> 44.8 us (0.82)
  Pallas kernels: 21.1 us -> 16.6 us
  waiting for transfers between devices: 13.6 us -> 9.85 us
  starting transfers between devices: 19 us -> 17.4 us
    pallas_call x3, Pallas kernels: 14.6 us -> 10.2 us  [stage(): pl.pallas_call(kernel, out_shape=[pltpu.VMEM(s, F32) for s in outs], grid...]
    ppermute x15 -> x14, waiting for transfers between devices: 13.6 us -> 9.85 us  [hop(): return lax.ppermute(x, axis, pairs)]
    ppermute x15 -> x14, starting transfers between devices: 19 us -> 17.4 us  [hop(): return lax.ppermute(x, axis, pairs)]
    pallas_call x7 -> x8, Pallas kernels: 6.43 us -> 6.43 us  [call(): pl.pallas_call(kernel, out_shape=out_shape, in_specs=in_specs or [VMEM] *...]
  transfers between devices with their start and end apart: 15 -> 14, of which waited for: 5 -> 4; matrix products, arithmetic and copies ran while one was open for 0% -> 0% of each run, Pallas kernels for 16% -> 16%
where the time goes in v7:
time: 44.8 us; the launch traced here: 44.6 us
  starting transfers between devices  17.4 us (39%)
  Pallas kernels  16.6 us (37%)
  waiting for transfers between devices  9.85 us (22%)
  between operations  0.79 us (2%)
    ppermute x14, starting transfers between devices, hop(): return lax.ppermute(x, axis, pairs)  17.4 us
    pallas_call x3, Pallas kernels, stage(): pl.pallas_call(kernel, out_shape=[pltpu.VMEM(s, F32) for s in outs], grid...  10.2 us
    ppermute x14, waiting for transfers between devices, hop(): return lax.ppermute(x, axis, pairs)  9.85 us
    pallas_call x8, Pallas kernels, call(): pl.pallas_call(kernel, out_shape=out_shape, in_specs=in_specs or [VMEM] *...  6.43 us
  transfers between devices with their start and end apart: 14, of which 4 were waited for; matrix products, arithmetic and copies ran while one was open for 0% of the time, Pallas kernels for 16%

profile of v7, /device:TPU:0, one launch (start us, length us, event | category | flops | bytes accessed | tf_op | source)
XLA Modules:
  0.0 44.6 jit_solution(1007909120817959850)
XLA Ops:
  0.0 1.1 %shard_map.101 = (f32[64,128]{1,0:T(8,128)S(1)}, f32[256,128]{1,0:T(8,128)S(1)}, f32[256,128]{1,0:T(8,128)S(1)}) custom-call(bf16[512,128]{1,0:T(8,128)(2,1)} %refs_0_.3, bf16[64,128]{1,0:T(8,128)(2,1)} %refs_1_.3, bf16[128,256]{1,0:T(8,128)(2,1)} %refs_2_.3), custom_call_target="tpu_custom_call" | custom-call | tf_op jit(solution)/shard_map/pallas_call | solution.py:40
  1.1 3.0 %collective-permute-start.1 = (f32[256,128]{1,0:T(8,128)S(1)}, f32[256,128]{1,0:T(8,128)S(1)}, u32[]{:S(2)}, u32[]{:S(2)}) collective-permute-start(f32[256,128]{1,0:T(8,128)S(1)} %get-tuple-element.42), channel_id=1, source_target_pairs={{0,1},{1,0},{2,3},{3,2},{4,5},{5,4},{6,7},{7,6},{8,9},{9,8},{10,11... | collective-permute-start | bytes 393224 | tf_op jit(solution)/shard_map/ppermute | solution.py:36
  4.2 0.1 collective-permute-start.6
  4.3 1.9 %collective-permute-start = (f32[64,128]{1,0:T(8,128)S(1)}, f32[64,128]{1,0:T(8,128)S(1)}, u32[]{:S(2)}, u32[]{:S(2)}) collective-permute-start(f32[64,128]{1,0:T(8,128)S(1)} %get-tuple-element.35), channel_id=1, source_target_pairs={{0,1},{1,0},{2,3},{3,2},{4,5},{5,4},{6,7},{7,6},{8,9},{9,8},{10,11... | collective-permute-start | bytes 98312 | tf_op jit(solution)/shard_map/ppermute | solution.py:36
  6.2 1.2 %shard_map.100 = (f32[64,128]{1,0:T(8,128)S(1)}, f32[8,128]{1,0:T(8,128)S(1)}, f32[8,128]{1,0:T(8,128)S(1)}, f32[256,128]{1,0:T(8,128)S(1)}, f32[256,128]{1,0:T(8,128)S(1)}) custom-call(bf16[512,128]{1,0:T(8,128)(2,1)} %refs_0_.3, bf16[64,128]{1,0:T(8,128)(2,1)} %refs_1_.3, bf16[128,256]{1,0:T(8,128)(2,1)} %refs_2_.3, f32[1,128]{1,0:T(1,128)} %bitcast.4, ...), custom_call_target="tpu_custom_call" | custom-call | tf_op jit(solution)/shard_map/pallas_call | solution.py:40
  7.4 3.8 %collective-permute-done.rest_0_ = f32[64,128]{1,0:T(8,128)S(1)} collective-permute-done((f32[64,128]{1,0:T(8,128)S(1)}, f32[64,128]{1,0:T(8,128)S(1)}, u32[]{:S(2)}, u32[]{:S(2)}) %collective-permute-start) | collective-permute-done | bytes 32800 | tf_op jit(solution)/shard_map/ppermute | solution.py:36
  11.2 0.0 collective-permute-done.1.rest_0_
  11.2 0.2 shard_map.103.refs_2_.refs_6_
  11.4 1.8 %collective-permute-start.2 = (f32[272,128]{1,0:T(8,128)S(1)}, f32[272,128]{1,0:T(8,128)S(1)}, u32[]{:S(2)}, u32[]{:S(2)}) collective-permute-start(f32[272,128]{1,0:T(8,128)S(1)} %shard_map.103.refs_2_.refs_6_), channel_id=1, source_target_pairs={{0,16},{8,24},{16,0},{24,8},{1,17},{9,25},{17,1},{25,9},{2,18},{10... | collective-permute-start | bytes 417800 | tf_op jit(solution)/shard_map/ppermute | solution.py:36
  13.2 0.0 collective-permute-done.6.rest_0_
  13.2 0.2 shard_map.105.refs_4_.refs_8_
  13.4 0.5 %collective-permute-start.5 = (f32[272,128]{1,0:T(8,128)S(1)}, f32[272,128]{1,0:T(8,128)S(1)}, u32[]{:S(2)}, u32[]{:S(2)}) collective-permute-start(f32[272,128]{1,0:T(8,128)S(1)} %shard_map.103.refs_2_.refs_6_), channel_id=1, source_target_pairs={{0,8},{8,0},{16,24},{24,16},{1,9},{9,1},{17,25},{25,17},{2,10},{10... | collective-permute-start | bytes 417800 | tf_op jit(solution)/shard_map/ppermute | solution.py:36
  13.9 0.3 collective-permute-start.8
  14.2 0.1 shard_map.102
  14.3 1.9 %collective-permute-start.3 = (f32[8,64]{1,0:T(8,128)S(1)}, f32[8,64]{1,0:T(8,128)S(1)}, u32[]{:S(2)}, u32[]{:S(2)}) collective-permute-start(f32[8,64]{1,0:T(8,128)S(1)} %get-tuple-element.43.low_ref), channel_id=1, source_target_pairs={{0,2},{2,0},{4,6},{6,4},{1,3},{3,1},{5,7},{7,5},{8,10},{10,8},{12,... | collective-permute-start | bytes 6152 | tf_op jit(solution)/shard_map/ppermute | solution.py:36
  16.2 1.8 %collective-permute-done.3.high_ref = f32[8,64]{1,0:T(8,128)S(1)} collective-permute-done((f32[8,64]{1,0:T(8,128)S(1)}, f32[8,64]{1,0:T(8,128)S(1)}, u32[]{:S(2)}, u32[]{:S(2)}) %collective-permute-start.3) | collective-permute-done | bytes 2080 | tf_op jit(solution)/shard_map/ppermute | solution.py:36
  18.0 2.8 %collective-permute-start.4 = (f32[16,64]{1,0:T(8,128)S(1)}, f32[16,64]{1,0:T(8,128)S(1)}, u32[]{:S(2)}, u32[]{:S(2)}) collective-permute-start(f32[16,64]{1,0:T(8,128)S(1)} %shard_map.104.refs_0_), channel_id=1, source_target_pairs={{0,4},{2,6},{4,0},{6,2},{1,5},{3,7},{5,1},{7,3},{8,12},{10,14},{12... | collective-permute-start | bytes 12296 | tf_op jit(solution)/shard_map/ppermute | solution.py:36
  21.5 2.5 %shard_map.106.refs_6_.refs_7_.refs_8_.refs_9_.refs_5_.refs_12_.refs_13_.refs_14_.refs_15_.refs_16_.refs_17_.refs_18_.refs_19_ = f32[8,2,2,128,128]{4,3,2,1,0:T(8,128)S(1)} custom-call(s32[1,1,128]{2,1,0:T(1,128)} %rows_hbm.1, s32[1,1,128]{2,1,0:T(1,128)} %cols_hbm.1, s32[1,1]{1,0:T(1,128)S(6)} %copy.11.count_ref, bf16[4,32,128,128]{3,2,1,0:T(8,128)(2,1)} %bitcast.9), custom_call_target="tpu_custom_call" | custom-call | flops 2097152 | bytes 4194304 | tf_op jit(solution)/shard_map/pallas_call | solution.py:40
  24.0 0.1 collective-permute-start.9
  24.1 2.0 %shard_map.107 = (f32[256,128]{1,0:T(8,128)S(1)}, f32[256,128]{1,0:T(8,128)S(1)}, f32[4,256,128]{2,1,0:T(8,128)S(1)}, f32[256,128]{1,0:T(8,128)S(1)}) custom-call(f32[16,64]{1,0:T(8,128)S(1)} %shard_map.104.refs_0_, f32[16,64]{1,0:T(8,128)S(1)} %collective-permute-done.4.refs_1_, f32[272,128]{1,0:T(8,128)S(1)} %shard_map.103.refs_2_.refs_6_, ...), custom_call_target="tpu_custom_call" | custom-call | flops 1073741824 | bytes 524288 | tf_op jit(solution)/shard_map/pallas_call | solution.py:402
  26.2 0.5 %collective-permute-start.10 = (f32[272,128]{1,0:T(8,128)S(1)}, f32[272,128]{1,0:T(8,128)S(1)}, u32[]{:S(2)}, u32[]{:S(2)}) collective-permute-start(f32[272,128]{1,0:T(8,128)S(1)} %collective-permute-done.8.refs_4_), channel_id=1, source_target_pairs={{0,8},{8,0},{16,24},{24,16},{1,9},{9,1},{17,25},{25,17},{2,10},{10... | collective-permute-start | bytes 417800 | tf_op jit(solution)/shard_map/ppermute | solution.py:36
  26.7 1.0 %shard_map.108 = (f32[4,256,128]{2,1,0:T(8,128)S(1)}, f32[256,128]{1,0:T(8,128)S(1)}) custom-call(f32[256,128]{1,0:T(8,128)S(1)} %get-tuple-element.48.refs_0_, f32[4,256,128]{2,1,0:T(8,128)S(1)} %get-tuple-element.50.refs_1_, f32[256,128]{1,0:T(8,128)S(1)} %get-tuple-element.51.refs_2_, f32[272,128]{1,0:T(8,128)S(1)} %collective-permute-done.2.refs_3_.refs_10_, ...), custom_call_target="tpu_custom_call" | custom-call | flops 536870912 | bytes 262144 | tf_op jit(solution)/shard_map/pallas_call | solution.py:402
  27.8 0.0 copy-start
  27.8 0.0 copy-start.1
  27.8 0.0 copy-start.2
  27.8 7.1 %shard_map.109 = (f32[72,128]{1,0:T(8,128)S(1)}, f32[72,128]{1,0:T(8,128)S(1)}, f32[72,128]{1,0:T(8,128)S(1)}, f32[72,128]{1,0:T(8,128)S(1)}) custom-call(f32[256,128]{1,0:T(8,128)S(1)} %get-tuple-element.48.refs_0_, f32[4,256,128]{2,1,0:T(8,128)S(1)} %get-tuple-element.53.refs_1_, f32[256,128]{1,0:T(8,128)S(1)} %get-tuple-element.54.refs_2_, ...), custom_call_target="tpu_custom_call" | custom-call | flops 536870912 | bytes 262144 | tf_op jit(solution)/shard_map/pallas_call | solution.py:402
  34.9 1.6 %collective-permute-start.11 = (f32[72,128]{1,0:T(8,128)S(1)}, f32[72,128]{1,0:T(8,128)S(1)}, u32[]{:S(2)}, u32[]{:S(2)}) collective-permute-start(f32[72,128]{1,0:T(8,128)S(1)} %get-tuple-element.58), channel_id=1, source_target_pairs={{0,2},{2,0},{4,6},{6,4},{1,3},{3,1},{5,7},{7,5},{8,10},{10,8},{12,... | collective-permute-start | bytes 110600 | tf_op jit(solution)/shard_map/ppermute | solution.py:36
  36.5 1.3 %collective-permute-start.12 = (f32[72,128]{1,0:T(8,128)S(1)}, f32[72,128]{1,0:T(8,128)S(1)}, u32[]{:S(2)}, u32[]{:S(2)}) collective-permute-start(f32[72,128]{1,0:T(8,128)S(1)} %get-tuple-element.59), channel_id=1, source_target_pairs={{0,4},{2,6},{4,0},{6,2},{1,5},{3,7},{5,1},{7,3},{8,12},{10,14},{12... | collective-permute-start | bytes 110600 | tf_op jit(solution)/shard_map/ppermute | solution.py:36
  37.8 1.5 %collective-permute-start.13 = (f32[72,128]{1,0:T(8,128)S(1)}, f32[72,128]{1,0:T(8,128)S(1)}, u32[]{:S(2)}, u32[]{:S(2)}) collective-permute-start(f32[72,128]{1,0:T(8,128)S(1)} %get-tuple-element.60), channel_id=1, source_target_pairs={{0,6},{2,4},{4,2},{6,0},{1,7},{3,5},{5,3},{7,1},{8,14},{10,12},{12... | collective-permute-start | bytes 110600 | tf_op jit(solution)/shard_map/ppermute | solution.py:36
  39.3 2.5 %collective-permute-done.12.rest_2_ = f32[72,128]{1,0:T(8,128)S(1)} collective-permute-done((f32[72,128]{1,0:T(8,128)S(1)}, f32[72,128]{1,0:T(8,128)S(1)}, u32[]{:S(2)}, u32[]{:S(2)}) %collective-permute-start.12) | collective-permute-done | bytes 36896 | tf_op jit(solution)/shard_map/ppermute | solution.py:36
  41.8 1.7 %collective-permute-done.13.rest_3_ = f32[72,128]{1,0:T(8,128)S(1)} collective-permute-done((f32[72,128]{1,0:T(8,128)S(1)}, f32[72,128]{1,0:T(8,128)S(1)}, u32[]{:S(2)}, u32[]{:S(2)}) %collective-permute-start.13) | collective-permute-done | bytes 36896 | tf_op jit(solution)/shard_map/ppermute | solution.py:36
  43.6 1.1 %shard_map.110 = bf16[64,128]{1,0:T(8,128)(2,1)} custom-call(f32[64,128]{1,0:T(8,128)S(1)} %get-tuple-element.39.zdst_ref, f32[1,128]{1,0:T(1,128)S(1)} %bitcast.5, f32[1,128]{1,0:T(1,128)S(1)} %bitcast.7, f32[1,128]{1,0:T(1,128)S(1)} %bitcast.8, f32[72,128]{1,0:T(8,128)S(1)} %get-tuple-element.57.rest_0_, f32[72,128]{1,0:T(8,128)S(1)} %collective-permute-done.11.rest_1_, ...), custom_call_target="tpu_custom_call" | custom-call | tf_op jit(solution)/shard_map/pallas_call | solution.py:40
  (13 shorter events, 0.0 us)
Async XLA Ops:
  1.1 10.0 %collective-permute-start.1 = (f32[256,128]{1,0:T(8,128)S(1)}, f32[256,128]{1,0:T(8,128)S(1)}, u32[]{:S(2)}, u32[]{:S(2)}) collective-permute-start(f32[256,128]{1,0:T(8,128)S(1)} %get-tuple-element.42), channel_id=1, source_target_pairs={{0,1},{1,0},{2,3},{3,2},{4,5},{5,4},{6,7},{7,6},{8,9},{9,8},{10,11... | collective-permute-start | bytes 393224 | tf_op jit(solution)/shard_map/ppermute | solution.py:36
  4.2 9.0 %collective-permute-start.6 = (f32[256,128]{1,0:T(8,128)S(1)}, f32[256,128]{1,0:T(8,128)S(1)}, u32[]{:S(2)}, u32[]{:S(2)}) collective-permute-start(f32[256,128]{1,0:T(8,128)S(1)} %get-tuple-element.47), channel_id=1, source_target_pairs={{0,1},{1,0},{2,3},{3,2},{4,5},{5,4},{6,7},{7,6},{8,9},{9,8},{10,11... | collective-permute-start | bytes 393224 | tf_op jit(solution)/shard_map/ppermute | solution.py:36
  4.3 6.9 %collective-permute-start = (f32[64,128]{1,0:T(8,128)S(1)}, f32[64,128]{1,0:T(8,128)S(1)}, u32[]{:S(2)}, u32[]{:S(2)}) collective-permute-start(f32[64,128]{1,0:T(8,128)S(1)} %get-tuple-element.35), channel_id=1, source_target_pairs={{0,1},{1,0},{2,3},{3,2},{4,5},{5,4},{6,7},{7,6},{8,9},{9,8},{10,11... | collective-permute-start | bytes 98312 | tf_op jit(solution)/shard_map/ppermute | solution.py:36
  11.4 12.6 %collective-permute-start.2 = (f32[272,128]{1,0:T(8,128)S(1)}, f32[272,128]{1,0:T(8,128)S(1)}, u32[]{:S(2)}, u32[]{:S(2)}) collective-permute-start(f32[272,128]{1,0:T(8,128)S(1)} %shard_map.103.refs_2_.refs_6_), channel_id=1, source_target_pairs={{0,16},{8,24},{16,0},{24,8},{1,17},{9,25},{17,1},{25,9},{2,18},{10... | collective-permute-start | bytes 417800 | tf_op jit(solution)/shard_map/ppermute | solution.py:36
  13.4 10.7 %collective-permute-start.7 = (f32[272,128]{1,0:T(8,128)S(1)}, f32[272,128]{1,0:T(8,128)S(1)}, u32[]{:S(2)}, u32[]{:S(2)}) collective-permute-start(f32[272,128]{1,0:T(8,128)S(1)} %shard_map.105.refs_4_.refs_8_), channel_id=1, source_target_pairs={{0,8},{8,0},{16,24},{24,16},{1,9},{9,1},{17,25},{25,17},{2,10},{10... | collective-permute-start | bytes 417800 | tf_op jit(solution)/shard_map/ppermute | solution.py:36
  13.4 10.7 %collective-permute-start.5 = (f32[272,128]{1,0:T(8,128)S(1)}, f32[272,128]{1,0:T(8,128)S(1)}, u32[]{:S(2)}, u32[]{:S(2)}) collective-permute-start(f32[272,128]{1,0:T(8,128)S(1)} %shard_map.103.refs_2_.refs_6_), channel_id=1, source_target_pairs={{0,8},{8,0},{16,24},{24,16},{1,9},{9,1},{17,25},{25,17},{2,10},{10... | collective-permute-start | bytes 417800 | tf_op jit(solution)/shard_map/ppermute | solution.py:36
  13.9 12.2 %collective-permute-start.8 = (f32[272,128]{1,0:T(8,128)S(1)}, f32[272,128]{1,0:T(8,128)S(1)}, u32[]{:S(2)}, u32[]{:S(2)}) collective-permute-start(f32[272,128]{1,0:T(8,128)S(1)} %shard_map.105.refs_4_.refs_8_), channel_id=1, source_target_pairs={{0,16},{8,24},{16,0},{24,8},{1,17},{9,25},{17,1},{25,9},{2,18},{10... | collective-permute-start | bytes 417800 | tf_op jit(solution)/shard_map/ppermute | solution.py:36
  14.3 3.6 %collective-permute-start.3 = (f32[8,64]{1,0:T(8,128)S(1)}, f32[8,64]{1,0:T(8,128)S(1)}, u32[]{:S(2)}, u32[]{:S(2)}) collective-permute-start(f32[8,64]{1,0:T(8,128)S(1)} %get-tuple-element.43.low_ref), channel_id=1, source_target_pairs={{0,2},{2,0},{4,6},{6,4},{1,3},{3,1},{5,7},{7,5},{8,10},{10,8},{12,... | collective-permute-start | bytes 6152 | tf_op jit(solution)/shard_map/ppermute | solution.py:36
  18.0 6.0 %collective-permute-start.4 = (f32[16,64]{1,0:T(8,128)S(1)}, f32[16,64]{1,0:T(8,128)S(1)}, u32[]{:S(2)}, u32[]{:S(2)}) collective-permute-start(f32[16,64]{1,0:T(8,128)S(1)} %shard_map.104.refs_0_), channel_id=1, source_target_pairs={{0,4},{2,6},{4,0},{6,2},{1,5},{3,7},{5,1},{7,3},{8,12},{10,14},{12... | collective-permute-start | bytes 12296 | tf_op jit(solution)/shard_map/ppermute | solution.py:36
  24.0 2.7 %collective-permute-start.9 = (f32[272,128]{1,0:T(8,128)S(1)}, f32[272,128]{1,0:T(8,128)S(1)}, u32[]{:S(2)}, u32[]{:S(2)}) collective-permute-start(f32[272,128]{1,0:T(8,128)S(1)} %collective-permute-done.2.refs_3_.refs_10_), channel_id=1, source_target_pairs={{0,8},{8,0},{16,24},{24,16},{1,9},{9,1},{17,25},{25,17},{2,10},{10... | collective-permute-start | bytes 417800 | tf_op jit(solution)/shard_map/ppermute | solution.py:36
  26.2 1.6 %collective-permute-start.10 = (f32[272,128]{1,0:T(8,128)S(1)}, f32[272,128]{1,0:T(8,128)S(1)}, u32[]{:S(2)}, u32[]{:S(2)}) collective-permute-start(f32[272,128]{1,0:T(8,128)S(1)} %collective-permute-done.8.refs_4_), channel_id=1, source_target_pairs={{0,8},{8,0},{16,24},{24,16},{1,9},{9,1},{17,25},{25,17},{2,10},{10... | collective-permute-start | bytes 417800 | tf_op jit(solution)/shard_map/ppermute | solution.py:36
  27.8 15.8 %copy-start = (f32[128]{0:T(128)S(1)}, f32[128]{0:T(128)}, u32[]{:S(2)}) copy-start(f32[128]{0:T(128)} %param.13) | copy-start | bytes 1540
  27.8 15.8 %copy-start.1 = (f32[128]{0:T(128)S(1)}, f32[128]{0:T(128)}, u32[]{:S(2)}) copy-start(f32[128]{0:T(128)} %param.14) | copy-start | bytes 1540
  27.8 15.8 %copy-start.2 = (f32[128]{0:T(128)S(1)}, f32[128]{0:T(128)}, u32[]{:S(2)}) copy-start(f32[128]{0:T(128)} %param.15) | copy-start | bytes 1540
  34.9 4.4 %collective-permute-start.11 = (f32[72,128]{1,0:T(8,128)S(1)}, f32[72,128]{1,0:T(8,128)S(1)}, u32[]{:S(2)}, u32[]{:S(2)}) collective-permute-start(f32[72,128]{1,0:T(8,128)S(1)} %get-tuple-element.58), channel_id=1, source_target_pairs={{0,2},{2,0},{4,6},{6,4},{1,3},{3,1},{5,7},{7,5},{8,10},{10,8},{12,... | collective-permute-start | bytes 110600 | tf_op jit(solution)/shard_map/ppermute | solution.py:36
  36.5 5.3 %collective-permute-start.12 = (f32[72,128]{1,0:T(8,128)S(1)}, f32[72,128]{1,0:T(8,128)S(1)}, u32[]{:S(2)}, u32[]{:S(2)}) collective-permute-start(f32[72,128]{1,0:T(8,128)S(1)} %get-tuple-element.59), channel_id=1, source_target_pairs={{0,4},{2,6},{4,0},{6,2},{1,5},{3,7},{5,1},{7,3},{8,12},{10,14},{12... | collective-permute-start | bytes 110600 | tf_op jit(solution)/shard_map/ppermute | solution.py:36
  37.8 5.8 %collective-permute-start.13 = (f32[72,128]{1,0:T(8,128)S(1)}, f32[72,128]{1,0:T(8,128)S(1)}, u32[]{:S(2)}, u32[]{:S(2)}) collective-permute-start(f32[72,128]{1,0:T(8,128)S(1)} %get-tuple-element.60), channel_id=1, source_target_pairs={{0,6},{2,4},{4,2},{6,0},{1,7},{3,5},{5,3},{7,1},{8,14},{10,12},{12... | collective-permute-start | bytes 110600 | tf_op jit(solution)/shard_map/ppermute | solution.py:36

commit v8 on v7

--- a/solution.py
+++ b/solution.py
@@ -245,7 +245,6 @@
         own = call(z_kernel, pltpu.VMEM((pack_rows, lanes), F32), src_own[ch], src_att, *src_parts[ch])
         parts[far_first, ch] = hop(own, "row", far_first)
         parts[0, ch] = own
-    last = n_chunk - 1
 
     def spread(first, ch):
         d = n_row // 4
@@ -530,9 +529,6 @@
                 out_refs[d][:own_rows, :width] = num_s[at, :]
                 out_refs[d][own_rows:, :own_rows] = md_s[at, :].T[:mdp]
 
-    if n_chunk > 1:
-        parts[far_first, 0], targets = lax.optimization_barrier((parts[far_first, 0], targets))
-        spread(far_first, 0)
     posneg, tgt_m, den, num = stage(
         near_kernel,
         near_keys,
@@ -540,9 +536,13 @@
         [(size * rows_of, own_rows)] * len(targets),
         [shape_t, shape_t, shape_d, shape_w],
     )
-    parts[far_first, last], den = lax.optimization_barrier((parts[far_first, last], den))
-    spread(far_first, last)
-    middle_keys = [(k, ch) for ch in range(last) for k in range(far_first, n_row)]
+    arrived = [parts[far_first, ch] for ch in range(n_chunk)]
+    arrived, den = lax.optimization_barrier((arrived, den))
+    for ch in range(n_chunk):
+        parts[far_first, ch] = arrived[ch]
+        spread(far_first, ch)
+    far_keys = [(k, ch) for k in range(far_first, n_row) for ch in range(n_chunk)]
+    middle_keys = far_keys[:n_chunk] if n_row > 2 else []
     if middle_keys:
         den, num = stage(
             middle_kernel,
@@ -551,7 +551,7 @@
             [shape_t, shape_d, shape_w],
             [shape_d, shape_w],
         )
-    last_keys = [(k, last) for k in range(far_first, n_row)]
+    last_keys = far_keys[len(middle_keys) :]
     other_keys = near_keys + middle_keys
     chunks = stage(
         last_kernel,

time: 44.8 us -> 44.8 us (level)
  no operation moved by 1% of the time
where the time goes in v8:
time: 44.8 us; the launch traced here: 44.7 us
  starting transfers between devices  17.3 us (39%)
  Pallas kernels  16.6 us (37%)
  waiting for transfers between devices  9.93 us (22%)
  between operations  0.8 us (2%)
    ppermute x14, starting transfers between devices, hop(): return lax.ppermute(x, axis, pairs)  17.3 us
    pallas_call x3, Pallas kernels, stage(): pl.pallas_call(kernel, out_shape=[pltpu.VMEM(s, F32) for s in outs], grid...  10.2 us
    ppermute x14, waiting for transfers between devices, hop(): return lax.ppermute(x, axis, pairs)  9.93 us
    pallas_call x8, Pallas kernels, call(): pl.pallas_call(kernel, out_shape=out_shape, in_specs=in_specs or [VMEM] *...  6.43 us
  transfers between devices with their start and end apart: 14, of which 4 were waited for; matrix products, arithmetic and copies ran while one was open for 0% of the time, Pallas kernels for 16%

profile of v8, /device:TPU:0, one launch (start us, length us, event | category | flops | bytes accessed | tf_op | source)
XLA Modules:
  0.0 44.7 jit_solution(16516999956159531922)
XLA Ops:
  0.0 1.1 %shard_map.101 = (f32[64,128]{1,0:T(8,128)S(1)}, f32[256,128]{1,0:T(8,128)S(1)}, f32[256,128]{1,0:T(8,128)S(1)}) custom-call(bf16[512,128]{1,0:T(8,128)(2,1)} %refs_0_.3, bf16[64,128]{1,0:T(8,128)(2,1)} %refs_1_.3, bf16[128,256]{1,0:T(8,128)(2,1)} %refs_2_.3), custom_call_target="tpu_custom_call" | custom-call | tf_op jit(solution)/shard_map/pallas_call | solution.py:40
  1.1 3.0 %collective-permute-start.5 = (f32[256,128]{1,0:T(8,128)S(1)}, f32[256,128]{1,0:T(8,128)S(1)}, u32[]{:S(2)}, u32[]{:S(2)}) collective-permute-start(f32[256,128]{1,0:T(8,128)S(1)} %get-tuple-element.43), channel_id=1, source_target_pairs={{0,1},{1,0},{2,3},{3,2},{4,5},{5,4},{6,7},{7,6},{8,9},{9,8},{10,11... | collective-permute-start | bytes 393224 | tf_op jit(solution)/shard_map/ppermute | solution.py:36
  4.2 0.1 collective-permute-start.3
  4.3 1.9 %collective-permute-start = (f32[64,128]{1,0:T(8,128)S(1)}, f32[64,128]{1,0:T(8,128)S(1)}, u32[]{:S(2)}, u32[]{:S(2)}) collective-permute-start(f32[64,128]{1,0:T(8,128)S(1)} %get-tuple-element.33), channel_id=1, source_target_pairs={{0,1},{1,0},{2,3},{3,2},{4,5},{5,4},{6,7},{7,6},{8,9},{9,8},{10,11... | collective-permute-start | bytes 98312 | tf_op jit(solution)/shard_map/ppermute | solution.py:36
  6.2 1.2 %shard_map.100 = (f32[64,128]{1,0:T(8,128)S(1)}, f32[8,128]{1,0:T(8,128)S(1)}, f32[8,128]{1,0:T(8,128)S(1)}, f32[256,128]{1,0:T(8,128)S(1)}, f32[256,128]{1,0:T(8,128)S(1)}) custom-call(bf16[512,128]{1,0:T(8,128)(2,1)} %refs_0_.3, bf16[64,128]{1,0:T(8,128)(2,1)} %refs_1_.3, bf16[128,256]{1,0:T(8,128)(2,1)} %refs_2_.3, f32[1,128]{1,0:T(1,128)} %bitcast.4, ...), custom_call_target="tpu_custom_call" | custom-call | tf_op jit(solution)/shard_map/pallas_call | solution.py:40
  7.4 3.8 %collective-permute-done.rest_0_ = f32[64,128]{1,0:T(8,128)S(1)} collective-permute-done((f32[64,128]{1,0:T(8,128)S(1)}, f32[64,128]{1,0:T(8,128)S(1)}, u32[]{:S(2)}, u32[]{:S(2)}) %collective-permute-start) | collective-permute-done | bytes 32800 | tf_op jit(solution)/shard_map/ppermute | solution.py:36
  11.2 0.0 collective-permute-done.5.rest_0_
  11.2 0.2 shard_map.105.refs_4_.refs_8_
  11.4 0.0 collective-permute-done.3.rest_0_
  11.4 0.2 shard_map.104.refs_2_.refs_6_
  11.6 0.5 %collective-permute-start.4 = (f32[272,128]{1,0:T(8,128)S(1)}, f32[272,128]{1,0:T(8,128)S(1)}, u32[]{:S(2)}, u32[]{:S(2)}) collective-permute-start(f32[272,128]{1,0:T(8,128)S(1)} %shard_map.104.refs_2_.refs_6_), channel_id=1, source_target_pairs={{0,8},{8,0},{16,24},{24,16},{1,9},{9,1},{17,25},{25,17},{2,10},{10... | collective-permute-start | bytes 417800 | tf_op jit(solution)/shard_map/ppermute | solution.py:36
  12.2 1.8 %collective-permute-start.8 = (f32[272,128]{1,0:T(8,128)S(1)}, f32[272,128]{1,0:T(8,128)S(1)}, u32[]{:S(2)}, u32[]{:S(2)}) collective-permute-start(f32[272,128]{1,0:T(8,128)S(1)} %shard_map.105.refs_4_.refs_8_), channel_id=1, source_target_pairs={{0,16},{8,24},{16,0},{24,8},{1,17},{9,25},{17,1},{25,9},{2,18},{10... | collective-permute-start | bytes 417800 | tf_op jit(solution)/shard_map/ppermute | solution.py:36
  13.9 0.3 collective-permute-start.7
  14.2 0.1 shard_map.102
  14.3 1.9 %collective-permute-start.1 = (f32[8,64]{1,0:T(8,128)S(1)}, f32[8,64]{1,0:T(8,128)S(1)}, u32[]{:S(2)}, u32[]{:S(2)}) collective-permute-start(f32[8,64]{1,0:T(8,128)S(1)} %get-tuple-element.38.low_ref), channel_id=1, source_target_pairs={{0,2},{2,0},{4,6},{6,4},{1,3},{3,1},{5,7},{7,5},{8,10},{10,8},{12,... | collective-permute-start | bytes 6152 | tf_op jit(solution)/shard_map/ppermute | solution.py:36
  16.2 1.8 %collective-permute-done.1.high_ref = f32[8,64]{1,0:T(8,128)S(1)} collective-permute-done((f32[8,64]{1,0:T(8,128)S(1)}, f32[8,64]{1,0:T(8,128)S(1)}, u32[]{:S(2)}, u32[]{:S(2)}) %collective-permute-start.1) | collective-permute-done | bytes 2080 | tf_op jit(solution)/shard_map/ppermute | solution.py:36
  18.0 2.8 %collective-permute-start.2 = (f32[16,64]{1,0:T(8,128)S(1)}, f32[16,64]{1,0:T(8,128)S(1)}, u32[]{:S(2)}, u32[]{:S(2)}) collective-permute-start(f32[16,64]{1,0:T(8,128)S(1)} %shard_map.103.refs_0_), channel_id=1, source_target_pairs={{0,4},{2,6},{4,0},{6,2},{1,5},{3,7},{5,1},{7,3},{8,12},{10,14},{12... | collective-permute-start | bytes 12296 | tf_op jit(solution)/shard_map/ppermute | solution.py:36
  21.5 2.5 %shard_map.106.refs_6_.refs_7_.refs_8_.refs_9_.refs_5_.refs_12_.refs_13_.refs_14_.refs_15_.refs_16_.refs_17_.refs_18_.refs_19_ = f32[8,2,2,128,128]{4,3,2,1,0:T(8,128)S(1)} custom-call(s32[1,1,128]{2,1,0:T(1,128)} %rows_hbm.1, s32[1,1,128]{2,1,0:T(1,128)} %cols_hbm.1, s32[1,1]{1,0:T(1,128)S(6)} %copy.11.count_ref, bf16[4,32,128,128]{3,2,1,0:T(8,128)(2,1)} %bitcast.9), custom_call_target="tpu_custom_call" | custom-call | flops 2097152 | bytes 4194304 | tf_op jit(solution)/shard_map/pallas_call | solution.py:40
  24.0 2.0 %shard_map.107 = (f32[256,128]{1,0:T(8,128)S(1)}, f32[256,128]{1,0:T(8,128)S(1)}, f32[4,256,128]{2,1,0:T(8,128)S(1)}, f32[256,128]{1,0:T(8,128)S(1)}) custom-call(f32[16,64]{1,0:T(8,128)S(1)} %shard_map.103.refs_0_, f32[16,64]{1,0:T(8,128)S(1)} %collective-permute-done.2.refs_1_, f32[272,128]{1,0:T(8,128)S(1)} %shard_map.104.refs_2_.refs_6_, ...), custom_call_target="tpu_custom_call" | custom-call | flops 1073741824 | bytes 524288 | tf_op jit(solution)/shard_map/pallas_call | solution.py:401
  26.1 0.1 collective-permute-start.9
  26.2 0.5 %collective-permute-start.10 = (f32[272,128]{1,0:T(8,128)S(1)}, f32[272,128]{1,0:T(8,128)S(1)}, u32[]{:S(2)}, u32[]{:S(2)}) collective-permute-start(f32[272,128]{1,0:T(8,128)S(1)} %collective-permute-done.8.refs_4_.refs_11_), channel_id=1, source_target_pairs={{0,8},{8,0},{16,24},{24,16},{1,9},{9,1},{17,25},{25,17},{2,10},{10... | collective-permute-start | bytes 417800 | tf_op jit(solution)/shard_map/ppermute | solution.py:36
  26.7 1.0 %shard_map.108 = (f32[4,256,128]{2,1,0:T(8,128)S(1)}, f32[256,128]{1,0:T(8,128)S(1)}) custom-call(f32[256,128]{1,0:T(8,128)S(1)} %get-tuple-element.44.refs_0_, f32[4,256,128]{2,1,0:T(8,128)S(1)} %get-tuple-element.46.refs_1_, f32[256,128]{1,0:T(8,128)S(1)} %get-tuple-element.47.refs_2_, f32[272,128]{1,0:T(8,128)S(1)} %collective-permute-done.7.refs_3_.refs_10_, ...), custom_call_target="tpu_custom_call" | custom-call | flops 536870912 | bytes 262144 | tf_op jit(solution)/shard_map/pallas_call | solution.py:401
  27.7 0.0 copy-start
  27.8 0.0 copy-start.1
  27.8 0.0 copy-start.2
  27.8 7.1 %shard_map.109 = (f32[72,128]{1,0:T(8,128)S(1)}, f32[72,128]{1,0:T(8,128)S(1)}, f32[72,128]{1,0:T(8,128)S(1)}, f32[72,128]{1,0:T(8,128)S(1)}) custom-call(f32[256,128]{1,0:T(8,128)S(1)} %get-tuple-element.44.refs_0_, f32[4,256,128]{2,1,0:T(8,128)S(1)} %get-tuple-element.50.refs_1_, f32[256,128]{1,0:T(8,128)S(1)} %get-tuple-element.51.refs_2_, ...), custom_call_target="tpu_custom_call" | custom-call | flops 536870912 | bytes 262144 | tf_op jit(solution)/shard_map/pallas_call | solution.py:401
  34.9 1.6 %collective-permute-start.11 = (f32[72,128]{1,0:T(8,128)S(1)}, f32[72,128]{1,0:T(8,128)S(1)}, u32[]{:S(2)}, u32[]{:S(2)}) collective-permute-start(f32[72,128]{1,0:T(8,128)S(1)} %get-tuple-element.54), channel_id=1, source_target_pairs={{0,2},{2,0},{4,6},{6,4},{1,3},{3,1},{5,7},{7,5},{8,10},{10,8},{12,... | collective-permute-start | bytes 110600 | tf_op jit(solution)/shard_map/ppermute | solution.py:36
  36.5 1.3 %collective-permute-start.12 = (f32[72,128]{1,0:T(8,128)S(1)}, f32[72,128]{1,0:T(8,128)S(1)}, u32[]{:S(2)}, u32[]{:S(2)}) collective-permute-start(f32[72,128]{1,0:T(8,128)S(1)} %get-tuple-element.55), channel_id=1, source_target_pairs={{0,4},{2,6},{4,0},{6,2},{1,5},{3,7},{5,1},{7,3},{8,12},{10,14},{12... | collective-permute-start | bytes 110600 | tf_op jit(solution)/shard_map/ppermute | solution.py:36
  37.8 1.5 %collective-permute-start.13 = (f32[72,128]{1,0:T(8,128)S(1)}, f32[72,128]{1,0:T(8,128)S(1)}, u32[]{:S(2)}, u32[]{:S(2)}) collective-permute-start(f32[72,128]{1,0:T(8,128)S(1)} %get-tuple-element.56), channel_id=1, source_target_pairs={{0,6},{2,4},{4,2},{6,0},{1,7},{3,5},{5,3},{7,1},{8,14},{10,12},{12... | collective-permute-start | bytes 110600 | tf_op jit(solution)/shard_map/ppermute | solution.py:36
  39.3 2.5 %collective-permute-done.12.rest_2_ = f32[72,128]{1,0:T(8,128)S(1)} collective-permute-done((f32[72,128]{1,0:T(8,128)S(1)}, f32[72,128]{1,0:T(8,128)S(1)}, u32[]{:S(2)}, u32[]{:S(2)}) %collective-permute-start.12) | collective-permute-done | bytes 36896 | tf_op jit(solution)/shard_map/ppermute | solution.py:36
  41.8 1.8 %collective-permute-done.13.rest_3_ = f32[72,128]{1,0:T(8,128)S(1)} collective-permute-done((f32[72,128]{1,0:T(8,128)S(1)}, f32[72,128]{1,0:T(8,128)S(1)}, u32[]{:S(2)}, u32[]{:S(2)}) %collective-permute-start.13) | collective-permute-done | bytes 36896 | tf_op jit(solution)/shard_map/ppermute | solution.py:36
  43.6 1.1 %shard_map.110 = bf16[64,128]{1,0:T(8,128)(2,1)} custom-call(f32[64,128]{1,0:T(8,128)S(1)} %get-tuple-element.37.zdst_ref, f32[1,128]{1,0:T(1,128)S(1)} %bitcast.5, f32[1,128]{1,0:T(1,128)S(1)} %bitcast.7, f32[1,128]{1,0:T(1,128)S(1)} %bitcast.8, f32[72,128]{1,0:T(8,128)S(1)} %get-tuple-element.53.rest_0_, f32[72,128]{1,0:T(8,128)S(1)} %collective-permute-done.11.rest_1_, ...), custom_call_target="tpu_custom_call" | custom-call | tf_op jit(solution)/shard_map/pallas_call | solution.py:40
  (13 shorter events, 0.0 us)
Async XLA Ops:
  1.1 10.0 %collective-permute-start.5 = (f32[256,128]{1,0:T(8,128)S(1)}, f32[256,128]{1,0:T(8,128)S(1)}, u32[]{:S(2)}, u32[]{:S(2)}) collective-permute-start(f32[256,128]{1,0:T(8,128)S(1)} %get-tuple-element.43), channel_id=1, source_target_pairs={{0,1},{1,0},{2,3},{3,2},{4,5},{5,4},{6,7},{7,6},{8,9},{9,8},{10,11... | collective-permute-start | bytes 393224 | tf_op jit(solution)/shard_map/ppermute | solution.py:36
  4.2 7.2 %collective-permute-start.3 = (f32[256,128]{1,0:T(8,128)S(1)}, f32[256,128]{1,0:T(8,128)S(1)}, u32[]{:S(2)}, u32[]{:S(2)}) collective-permute-start(f32[256,128]{1,0:T(8,128)S(1)} %get-tuple-element.41), channel_id=1, source_target_pairs={{0,1},{1,0},{2,3},{3,2},{4,5},{5,4},{6,7},{7,6},{8,9},{9,8},{10,11... | collective-permute-start | bytes 393224 | tf_op jit(solution)/shard_map/ppermute | solution.py:36
  4.3 6.9 %collective-permute-start = (f32[64,128]{1,0:T(8,128)S(1)}, f32[64,128]{1,0:T(8,128)S(1)}, u32[]{:S(2)}, u32[]{:S(2)}) collective-permute-start(f32[64,128]{1,0:T(8,128)S(1)} %get-tuple-element.33), channel_id=1, source_target_pairs={{0,1},{1,0},{2,3},{3,2},{4,5},{5,4},{6,7},{7,6},{8,9},{9,8},{10,11... | collective-permute-start | bytes 98312 | tf_op jit(solution)/shard_map/ppermute | solution.py:36
  11.4 12.6 %collective-permute-start.6 = (f32[272,128]{1,0:T(8,128)S(1)}, f32[272,128]{1,0:T(8,128)S(1)}, u32[]{:S(2)}, u32[]{:S(2)}) collective-permute-start(f32[272,128]{1,0:T(8,128)S(1)} %shard_map.105.refs_4_.refs_8_), channel_id=1, source_target_pairs={{0,8},{8,0},{16,24},{24,16},{1,9},{9,1},{17,25},{25,17},{2,10},{10... | collective-permute-start | bytes 417800 | tf_op jit(solution)/shard_map/ppermute | solution.py:36
  11.6 12.4 %collective-permute-start.4 = (f32[272,128]{1,0:T(8,128)S(1)}, f32[272,128]{1,0:T(8,128)S(1)}, u32[]{:S(2)}, u32[]{:S(2)}) collective-permute-start(f32[272,128]{1,0:T(8,128)S(1)} %shard_map.104.refs_2_.refs_6_), channel_id=1, source_target_pairs={{0,8},{8,0},{16,24},{24,16},{1,9},{9,1},{17,25},{25,17},{2,10},{10... | collective-permute-start | bytes 417800 | tf_op jit(solution)/shard_map/ppermute | solution.py:36
  12.2 13.9 %collective-permute-start.8 = (f32[272,128]{1,0:T(8,128)S(1)}, f32[272,128]{1,0:T(8,128)S(1)}, u32[]{:S(2)}, u32[]{:S(2)}) collective-permute-start(f32[272,128]{1,0:T(8,128)S(1)} %shard_map.105.refs_4_.refs_8_), channel_id=1, source_target_pairs={{0,16},{8,24},{16,0},{24,8},{1,17},{9,25},{17,1},{25,9},{2,18},{10... | collective-permute-start | bytes 417800 | tf_op jit(solution)/shard_map/ppermute | solution.py:36
  13.9 12.2 %collective-permute-start.7 = (f32[272,128]{1,0:T(8,128)S(1)}, f32[272,128]{1,0:T(8,128)S(1)}, u32[]{:S(2)}, u32[]{:S(2)}) collective-permute-start(f32[272,128]{1,0:T(8,128)S(1)} %shard_map.104.refs_2_.refs_6_), channel_id=1, source_target_pairs={{0,16},{8,24},{16,0},{24,8},{1,17},{9,25},{17,1},{25,9},{2,18},{10... | collective-permute-start | bytes 417800 | tf_op jit(solution)/shard_map/ppermute | solution.py:36
  14.3 3.6 %collective-permute-start.1 = (f32[8,64]{1,0:T(8,128)S(1)}, f32[8,64]{1,0:T(8,128)S(1)}, u32[]{:S(2)}, u32[]{:S(2)}) collective-permute-start(f32[8,64]{1,0:T(8,128)S(1)} %get-tuple-element.38.low_ref), channel_id=1, source_target_pairs={{0,2},{2,0},{4,6},{6,4},{1,3},{3,1},{5,7},{7,5},{8,10},{10,8},{12,... | collective-permute-start | bytes 6152 | tf_op jit(solution)/shard_map/ppermute | solution.py:36
  18.0 6.0 %collective-permute-start.2 = (f32[16,64]{1,0:T(8,128)S(1)}, f32[16,64]{1,0:T(8,128)S(1)}, u32[]{:S(2)}, u32[]{:S(2)}) collective-permute-start(f32[16,64]{1,0:T(8,128)S(1)} %shard_map.103.refs_0_), channel_id=1, source_target_pairs={{0,4},{2,6},{4,0},{6,2},{1,5},{3,7},{5,1},{7,3},{8,12},{10,14},{12... | collective-permute-start | bytes 12296 | tf_op jit(solution)/shard_map/ppermute | solution.py:36
  26.1 1.6 %collective-permute-start.9 = (f32[272,128]{1,0:T(8,128)S(1)}, f32[272,128]{1,0:T(8,128)S(1)}, u32[]{:S(2)}, u32[]{:S(2)}) collective-permute-start(f32[272,128]{1,0:T(8,128)S(1)} %collective-permute-done.7.refs_3_.refs_10_), channel_id=1, source_target_pairs={{0,8},{8,0},{16,24},{24,16},{1,9},{9,1},{17,25},{25,17},{2,10},{10... | collective-permute-start | bytes 417800 | tf_op jit(solution)/shard_map/ppermute | solution.py:36
  26.2 1.6 %collective-permute-start.10 = (f32[272,128]{1,0:T(8,128)S(1)}, f32[272,128]{1,0:T(8,128)S(1)}, u32[]{:S(2)}, u32[]{:S(2)}) collective-permute-start(f32[272,128]{1,0:T(8,128)S(1)} %collective-permute-done.8.refs_4_.refs_11_), channel_id=1, source_target_pairs={{0,8},{8,0},{16,24},{24,16},{1,9},{9,1},{17,25},{25,17},{2,10},{10... | collective-permute-start | bytes 417800 | tf_op jit(solution)/shard_map/ppermute | solution.py:36
  27.7 15.8 %copy-start = (f32[128]{0:T(128)S(1)}, f32[128]{0:T(128)}, u32[]{:S(2)}) copy-start(f32[128]{0:T(128)} %param.13) | copy-start | bytes 1540
  27.8 15.8 %copy-start.1 = (f32[128]{0:T(128)S(1)}, f32[128]{0:T(128)}, u32[]{:S(2)}) copy-start(f32[128]{0:T(128)} %param.14) | copy-start | bytes 1540
  27.8 15.8 %copy-start.2 = (f32[128]{0:T(128)S(1)}, f32[128]{0:T(128)}, u32[]{:S(2)}) copy-start(f32[128]{0:T(128)} %param.15) | copy-start | bytes 1540
  34.9 4.4 %collective-permute-start.11 = (f32[72,128]{1,0:T(8,128)S(1)}, f32[72,128]{1,0:T(8,128)S(1)}, u32[]{:S(2)}, u32[]{:S(2)}) collective-permute-start(f32[72,128]{1,0:T(8,128)S(1)} %get-tuple-element.54), channel_id=1, source_target_pairs={{0,2},{2,0},{4,6},{6,4},{1,3},{3,1},{5,7},{7,5},{8,10},{10,8},{12,... | collective-permute-start | bytes 110600 | tf_op jit(solution)/shard_map/ppermute | solution.py:36
  36.5 5.3 %collective-permute-start.12 = (f32[72,128]{1,0:T(8,128)S(1)}, f32[72,128]{1,0:T(8,128)S(1)}, u32[]{:S(2)}, u32[]{:S(2)}) collective-permute-start(f32[72,128]{1,0:T(8,128)S(1)} %get-tuple-element.55), channel_id=1, source_target_pairs={{0,4},{2,6},{4,0},{6,2},{1,5},{3,7},{5,1},{7,3},{8,12},{10,14},{12... | collective-permute-start | bytes 110600 | tf_op jit(solution)/shard_map/ppermute | solution.py:36
  37.8 5.8 %collective-permute-start.13 = (f32[72,128]{1,0:T(8,128)S(1)}, f32[72,128]{1,0:T(8,128)S(1)}, u32[]{:S(2)}, u32[]{:S(2)}) collective-permute-start(f32[72,128]{1,0:T(8,128)S(1)} %get-tuple-element.56), channel_id=1, source_target_pairs={{0,6},{2,4},{4,2},{6,0},{1,7},{3,5},{5,3},{7,1},{8,14},{10,12},{12... | collective-permute-start | bytes 110600 | tf_op jit(solution)/shard_map/ppermute | solution.py:36

commit v9 on v6

--- a/solution.py
+++ b/solution.py
@@ -133,19 +133,23 @@
         )
 
     def send_kernel(*refs):
-        hbm, outs, (src_ref, dst_ref, proj_ref, sems) = refs[:3], refs[3:-4], refs[-4:]
-        fetch(hbm, (src_ref, dst_ref, proj_ref), sems)
+        hbm, outs, refs = refs[:4], refs[4:-5], refs[-5:]
+        fetch(hbm, refs[:4], refs[4])
+        src_ref, dst_ref, proj_ref, att_ref = refs[:4]
         me = lax.axis_index("feat")
+        outs[0][...] = project(dst_ref[...], take_cols(proj_ref, me, width))
+        outs[1][...] = LOG2E * head_rows(att_ref[...], heads, width, up8(heads))
         for d in range(1, n_feat):
             w = take_cols(proj_ref, goes_to(me, d, n_feat), width)
-            own_outs = outs[(d - 1) * (n_chunk + 1) : d * (n_chunk + 1)]
+            own_outs = outs[2 + (d - 1) * (n_chunk + 1) : 2 + d * (n_chunk + 1)]
             own_outs[0][...] = project(dst_ref[...], w)
             for ch in range(n_chunk):
                 own_outs[ch + 1][...] = project(src_ref[ch * part_rows : (ch + 1) * part_rows], w)
 
-    sent = fetching(
+    dst_own, dst_att, *sent = fetching(
         send_kernel,
-        [
+        [pltpu.VMEM((own_rows, width), F32), pltpu.VMEM((up8(heads), width), F32)]
+        + [
             pltpu.VMEM((n, width), F32)
             for _ in range(1, n_feat)
             for n in [own_rows] + [part_rows] * n_chunk
@@ -153,29 +157,69 @@
         src_feats,
         dst_feats,
         proj,
+        att_dst2,
     )
     sent = [sent[k :: n_chunk + 1] for k in range(n_chunk + 1)]
     dst_parts = [hop(sent[0][d - 1], "feat", d) for d in range(1, n_feat)]
     src_parts = [[hop(part[d - 1], "feat", d) for d in range(1, n_feat)] for part in sent[1:]]
 
+    tiles = row_tiles * col_tiles
+    whole = lambda shape: pl.BlockSpec(shape, lambda s: (0,) * len(shape))
+
+    def dst_kernel(own_ref, att_ref, *rest):
+        got, (z_ref, s_ref) = rest[: n_feat - 1], rest[n_feat - 1 :]
+        z = own_ref[...]
+        for part in got:
+            z = z + part[...]
+        z_ref[...] = z
+        s_ref[...] = contract(att_ref[...], z, ((1,), (1,)))
+
+    zdst, s_dst = call(
+        dst_kernel,
+        [
+            jax.ShapeDtypeStruct((own_rows, width), F32),
+            jax.ShapeDtypeStruct((up8(heads), own_rows), F32),
+        ],
+        dst_own,
+        dst_att,
+        *dst_parts,
+    )
+    rows_of = up8(heads)
+    if is_pow2(n_col) and n_col > 1:
+        bits = n_col.bit_length() - 1
+        place = lambda d: sum(((d >> k) & 1) << (bits - 1 - k) for k in range(bits))
+        targets, d = [s_dst], n_col // 2
+        while d:
+            targets = [targets[0], hop(targets[0], "col", d)]
+            d //= 2
+            if d:
+
+                def join_kernel(low_ref, high_ref, out_ref):
+                    out_ref[...] = jnp.concatenate([low_ref[...], high_ref[...]], axis=0)
+
+                shape = (2 * targets[0].shape[0], own_rows)
+                targets = [call(join_kernel, pltpu.VMEM(shape, F32), *targets)]
+    else:
+        place = lambda d: d
+        targets = [s_dst] + [hop(s_dst, "col", d) for d in range(1, n_col)]
+    size = n_col // len(targets)
+
     units = n_row * n_chunk
-    tiles = row_tiles * col_tiles
     period = min(slots, tiles) if slots % min(slots, tiles) == 0 else slots
     reps = slots // period
     group = 8
     groups = period // group
 
     def local_kernel(*refs):
-        hbm, count_ref, refs = refs[:8], refs[8], refs[9:]
-        outs, panel_ref, refs = refs[: 3 + n_chunk], refs[3 + n_chunk], refs[4 + n_chunk :]
-        src_ref, dst_ref, proj_ref, att_src_ref, att_dst_ref, rows_ref, cols_ref, w_ref = refs[:8]
-        sems, w_sems = refs[8:]
+        hbm, count_ref, refs = refs[:6], refs[6], refs[7:]
+        outs, panel_ref, refs = refs[: 1 + n_chunk], refs[1 + n_chunk], refs[2 + n_chunk :]
+        src_ref, proj_ref, att_ref, rows_ref, cols_ref, w_ref, sems, w_sems = refs
         small = [
-            pltpu.make_async_copy(h, v, sems.at[k]) for k, (h, v) in enumerate(zip(hbm[:7], refs[:7]))
+            pltpu.make_async_copy(h, v, sems.at[k]) for k, (h, v) in enumerate(zip(hbm[:5], refs[:5]))
         ]
         large = [
             pltpu.make_async_copy(
-                hbm[7].at[k, pl.ds(g * group, group)],
+                hbm[5].at[k, pl.ds(g * group, group)],
                 w_ref.at[k, pl.ds(g * group, group)],
                 w_sems.at[g, k],
             )
@@ -193,12 +237,10 @@
 
         for copy in small:
             copy.wait()
+        outs[0][...] = LOG2E * head_rows(att_ref[...], heads, width, hp)
         w = take_cols(proj_ref, lax.axis_index("feat"), width)
-        outs[0][...] = project(dst_ref[...], w)
-        outs[1][...] = LOG2E * head_rows(att_dst_ref[...], heads, width, up8(heads))
-        outs[2][...] = LOG2E * head_rows(att_src_ref[...], heads, width, hp)
         for ch in range(n_chunk):
-            outs[3 + ch][...] = project(src_ref[ch * part_rows : (ch + 1) * part_rows], w)
+            outs[1 + ch][...] = project(src_ref[ch * part_rows : (ch + 1) * part_rows], w)
 
         row = lax.axis_index("row")
         count = count_ref[0, 0]
@@ -219,14 +261,10 @@
                 panel_ref[unit, r, t] = panel_ref[unit, r, t] + total
 
     slot_weights = edge_weight.reshape(reps, period, TILE, TILE)
-    inputs = (src_feats, dst_feats, proj, att_src2, att_dst2, tile_rows, tile_cols, slot_weights)
-    dst_own, dst_att, src_att, *src_own, panel = call(
+    inputs = (src_feats, proj, att_src2, tile_rows, tile_cols, slot_weights)
+    src_att, *src_own, panel = call(
         local_kernel,
-        [
-            pltpu.VMEM((own_rows, width), F32),
-            pltpu.VMEM((up8(heads), width), F32),
-            pltpu.VMEM((hp, width), F32),
-        ]
+        [pltpu.VMEM((hp, width), F32)]
         + [pltpu.VMEM((part_rows, width), F32)] * n_chunk
         + [pltpu.VMEM((units, row_tiles, chunk_tiles, TILE, TILE), F32)],
         *map(in_hbm, inputs),
@@ -237,36 +275,11 @@
                 (pltpu.SMEM if v.dtype == jnp.int32 else pltpu.VMEM)(v.shape, v.dtype)
                 for v in inputs
             ),
-            pltpu.SemaphoreType.DMA((7,)),
+            pltpu.SemaphoreType.DMA((5,)),
             pltpu.SemaphoreType.DMA((groups, reps)),
         ],
         grant=12 << 20,
     )
-    dst_parts, src_own = lax.optimization_barrier((dst_parts, src_own))
-
-    whole = lambda shape: pl.BlockSpec(shape, lambda s: (0,) * len(shape))
-
-    def dst_kernel(own_ref, att_ref, *rest):
-        got, (z_ref, s_ref) = rest[: n_feat - 1], rest[n_feat - 1 :]
-        z = own_ref[...]
-        for part in got:
-            z = z + part[...]
-        z_ref[...] = z
-        s_ref[...] = contract(att_ref[...], z, ((1,), (1,)))
-
-    zdst, s_dst = call(
-        dst_kernel,
-        [
-            jax.ShapeDtypeStruct((own_rows, width), F32),
-            jax.ShapeDtypeStruct((up8(heads), own_rows), F32),
-        ],
-        dst_own,
-        dst_att,
-        *dst_parts,
-    )
-    targets = [hop(s_dst, "col", d) for d in range(n_col - 1, 0, -1)]
-    targets = [s_dst] + targets[::-1]
-
 
     pack_rows = part_rows + chunk_tiles * hp
 
@@ -290,7 +303,6 @@
         own = call(z_kernel, pltpu.VMEM((pack_rows, lanes), F32), src_own[ch], src_att, *src_parts[ch])
         parts[far_first, ch] = hop(own, "row", far_first)
         parts[0, ch] = own
-    last = n_chunk - 1
 
     def spread(first, ch):
         d = n_row // 4
@@ -395,8 +407,9 @@
 
     def near_kernel(*refs):
         n = len(near_keys)
-        tgt_refs, part_refs, w_refs = refs[:n_col], refs[n_col : n_col + n], refs[n_col + n :][:n]
-        posneg, tgt_m, den_out, num_out = refs[n_col + 2 * n :]
+        n_tgt = len(targets)
+        tgt_refs, part_refs, w_refs = refs[:n_tgt], refs[n_tgt : n_tgt + n], refs[n_tgt + n :][:n]
+        posneg, tgt_m, den_out, num_out = refs[n_tgt + 2 * n :]
         col = lax.axis_index("col")
 
         @pl.when(pl.program_id(0) == 0)
@@ -419,7 +432,8 @@
                 at = pl.ds(
                     pl.multiple_of(comes_from(col, d, n_col) * own_rows, own_rows), own_rows
                 )
-                a = contract(tgt_refs[d][...], eye, ((0,), (0,)))
+                k, g = divmod(place(d), size)
+                a = contract(tgt_refs[k][g * rows_of : (g + 1) * rows_of], eye, ((0,), (0,)))
                 m = leaky(a + bound)
                 tgt_m[at, :] = jnp.where(lane < heads, a, m)
                 posneg[at, :] = jnp.where(lane < heads, a, SLOPE * a) - m
@@ -503,19 +517,20 @@
                 out_refs[d][:own_rows, :width] = num_s[at, :]
                 out_refs[d][own_rows:, :own_rows] = md_s[at, :].T[:mdp]
 
-    if n_chunk > 1:
-        parts[far_first, 0], targets = lax.optimization_barrier((parts[far_first, 0], targets))
-        spread(far_first, 0)
     posneg, tgt_m, den, num = stage(
         near_kernel,
         near_keys,
         targets,
-        [(up8(heads), own_rows)] * n_col,
+        [(size * rows_of, own_rows)] * len(targets),
         [shape_t, shape_t, shape_d, shape_w],
     )
-    parts[far_first, last], den = lax.optimization_barrier((parts[far_first, last], den))
-    spread(far_first, last)
-    middle_keys = [(k, ch) for ch in range(last) for k in range(far_first, n_row)]
+    arrived = [parts[far_first, ch] for ch in range(n_chunk)]
+    arrived, den = lax.optimization_barrier((arrived, den))
+    for ch in range(n_chunk):
+        parts[far_first, ch] = arrived[ch]
+        spread(far_first, ch)
+    far_keys = [(k, ch) for k in range(far_first, n_row) for ch in range(n_chunk)]
+    middle_keys = far_keys[:n_chunk] if n_row > 2 else []
     if middle_keys:
         den, num = stage(
             middle_kernel,
@@ -524,7 +539,7 @@
             [shape_t, shape_d, shape_w],
             [shape_d, shape_w],
         )
-    last_keys = [(k, last) for k in range(far_first, n_row)]
+    last_keys = far_keys[len(middle_keys) :]
     other_keys = near_keys + middle_keys
     chunks = stage(
         last_kernel,

time: 50.1 us -> 45.3 us (0.904)
  waiting for transfers between devices: 14.2 us -> 11.6 us
  starting transfers between devices: 19 us -> 16.6 us
    ppermute x15 -> x14, waiting for transfers between devices: 14.2 us -> 11.6 us  [hop(): return lax.ppermute(x, axis, pairs)]
    ppermute x15 -> x14, starting transfers between devices: 19 us -> 16.6 us  [hop(): return lax.ppermute(x, axis, pairs)]
    pallas_call x6 -> x7, Pallas kernels: 5.89 us -> 5.97 us  [call(): pl.pallas_call(kernel, out_shape=out_shape, in_specs=in_specs or [VMEM] *...]
  transfers between devices with their start and end apart: 15 -> 14, of which waited for: 6 -> 7; matrix products, arithmetic and copies ran while one was open for 0% -> 0% of each run, Pallas kernels for 13% -> 15%
where the time goes in v9:
time: 45.3 us; the launch traced here: 45.2 us
  starting transfers between devices  16.6 us (37%)
  Pallas kernels  16.2 us (36%)
  waiting for transfers between devices  11.6 us (26%)
  between operations  0.76 us (2%)
    ppermute x14, starting transfers between devices, hop(): return lax.ppermute(x, axis, pairs)  16.6 us
    ppermute x14, waiting for transfers between devices, hop(): return lax.ppermute(x, axis, pairs)  11.6 us
    pallas_call x3, Pallas kernels, stage(): pl.pallas_call(kernel, out_shape=[pltpu.VMEM(s, F32) for s in outs], grid...  10.2 us
    pallas_call x7, Pallas kernels, call(): pl.pallas_call(kernel, out_shape=out_shape, in_specs=in_specs or [VMEM] *...  5.97 us
  transfers between devices with their start and end apart: 14, of which 7 were waited for; matrix products, arithmetic and copies ran while one was open for 0% of the time, Pallas kernels for 15%

profile of v9, /device:TPU:0, one launch (start us, length us, event | category | flops | bytes accessed | tf_op | source)
XLA Modules:
  0.0 45.2 jit_solution(15392055616632481675)
XLA Ops:
  0.0 1.2 %shard_map.100 = (f32[64,128]{1,0:T(8,128)S(1)}, f32[8,128]{1,0:T(8,128)S(1)}, f32[64,128]{1,0:T(8,128)S(1)}, f32[256,128]{1,0:T(8,128)S(1)}, f32[256,128]{1,0:T(8,128)S(1)}) custom-call(bf16[512,128]{1,0:T(8,128)(2,1)} %refs_0_.3, bf16[64,128]{1,0:T(8,128)(2,1)} %refs_1_.2, bf16[128,256]{1,0:T(8,128)(2,1)} %refs_1_.3, f32[1,128]{1,0:T(1,128)} %bitcast.4), custom_call_target="tpu_custom_call" | custom-call | tf_op jit(solution)/shard_map/pallas_call | solution.py:40
  1.2 3.0 %collective-permute-start.5 = (f32[256,128]{1,0:T(8,128)S(1)}, f32[256,128]{1,0:T(8,128)S(1)}, u32[]{:S(2)}, u32[]{:S(2)}) collective-permute-start(f32[256,128]{1,0:T(8,128)S(1)} %get-tuple-element.38), channel_id=1, source_target_pairs={{0,1},{1,0},{2,3},{3,2},{4,5},{5,4},{6,7},{7,6},{8,9},{9,8},{10,11... | collective-permute-start | bytes 393224 | tf_op jit(solution)/shard_map/ppermute | solution.py:36
  4.2 0.1 collective-permute-start.3
  4.9 3.2 %shard_map.103 = (f32[8,128]{1,0:T(8,128)S(1)}, f32[256,128]{1,0:T(8,128)S(1)}, f32[256,128]{1,0:T(8,128)S(1)}, f32[8,2,2,128,128]{4,3,2,1,0:T(8,128)S(1)}) custom-call(bf16[512,128]{1,0:T(8,128)(2,1)} %refs_0_.3, bf16[128,256]{1,0:T(8,128)(2,1)} %refs_1_.3, f32[1,128]{1,0:T(1,128)} %bitcast.6, s32[1,1,128]{2,1,0:T(1,128)} %refs_3_.1, s32[1,1,128]{2,1,0:T(1,128)} %refs_4_.1, ...), custom_call_target="tpu_custom_call" | custom-call | tf_op jit(solution)/shard_map/pallas_call | solution.py:40
  8.1 0.4 collective-permute-done.5.rest_0_
  8.6 0.2 shard_map.105.refs_4_.refs_8_
  8.8 0.0 collective-permute-start.6
  8.8 1.8 %collective-permute-done.3.rest_0_ = f32[256,128]{1,0:T(8,128)S(1)} collective-permute-done((f32[256,128]{1,0:T(8,128)S(1)}, f32[256,128]{1,0:T(8,128)S(1)}, u32[]{:S(2)}, u32[]{:S(2)}) %collective-permute-start.3) | collective-permute-done | bytes 131104 | tf_op jit(solution)/shard_map/ppermute | solution.py:36
  10.5 0.2 shard_map.104.refs_2_.refs_6_
  10.7 1.8 %collective-permute-start = (f32[64,128]{1,0:T(8,128)S(1)}, f32[64,128]{1,0:T(8,128)S(1)}, u32[]{:S(2)}, u32[]{:S(2)}) collective-permute-start(f32[64,128]{1,0:T(8,128)S(1)} %get-tuple-element.31), channel_id=1, source_target_pairs={{0,1},{1,0},{2,3},{3,2},{4,5},{5,4},{6,7},{7,6},{8,9},{9,8},{10,11... | collective-permute-start | bytes 98312 | tf_op jit(solution)/shard_map/ppermute | solution.py:36
  12.5 1.5 %collective-permute-start.8 = (f32[272,128]{1,0:T(8,128)S(1)}, f32[272,128]{1,0:T(8,128)S(1)}, u32[]{:S(2)}, u32[]{:S(2)}) collective-permute-start(f32[272,128]{1,0:T(8,128)S(1)} %shard_map.105.refs_4_.refs_8_), channel_id=1, source_target_pairs={{0,16},{8,24},{16,0},{24,8},{1,17},{9,25},{17,1},{25,9},{2,18},{10... | collective-permute-start | bytes 417800 | tf_op jit(solution)/shard_map/ppermute | solution.py:36
  14.0 0.5 %collective-permute-start.7 = (f32[272,128]{1,0:T(8,128)S(1)}, f32[272,128]{1,0:T(8,128)S(1)}, u32[]{:S(2)}, u32[]{:S(2)}) collective-permute-start(f32[272,128]{1,0:T(8,128)S(1)} %shard_map.104.refs_2_.refs_6_), channel_id=1, source_target_pairs={{0,16},{8,24},{16,0},{24,8},{1,17},{9,25},{17,1},{25,9},{2,18},{10... | collective-permute-start | bytes 417800 | tf_op jit(solution)/shard_map/ppermute | solution.py:36
  14.5 0.1 collective-permute-done.rest_0_
  14.7 0.1 shard_map.101
  14.8 2.9 %collective-permute-start.1 = (f32[8,64]{1,0:T(8,128)S(1)}, f32[8,64]{1,0:T(8,128)S(1)}, u32[]{:S(2)}, u32[]{:S(2)}) collective-permute-start(f32[8,64]{1,0:T(8,128)S(1)} %get-tuple-element.33.low_ref), channel_id=1, source_target_pairs={{0,4},{2,6},{4,0},{6,2},{1,5},{3,7},{5,1},{7,3},{8,12},{10,14},{12... | collective-permute-start | bytes 6152 | tf_op jit(solution)/shard_map/ppermute | solution.py:36
  17.7 1.7 %collective-permute-done.1.high_ref = f32[8,64]{1,0:T(8,128)S(1)} collective-permute-done((f32[8,64]{1,0:T(8,128)S(1)}, f32[8,64]{1,0:T(8,128)S(1)}, u32[]{:S(2)}, u32[]{:S(2)}) %collective-permute-start.1) | collective-permute-done | bytes 2080 | tf_op jit(solution)/shard_map/ppermute | solution.py:36
  19.4 1.8 %collective-permute-start.2 = (f32[16,64]{1,0:T(8,128)S(1)}, f32[16,64]{1,0:T(8,128)S(1)}, u32[]{:S(2)}, u32[]{:S(2)}) collective-permute-start(f32[16,64]{1,0:T(8,128)S(1)} %shard_map.102.refs_0_), channel_id=1, source_target_pairs={{0,2},{2,0},{4,6},{6,4},{1,3},{3,1},{5,7},{7,5},{8,10},{10,8},{12,... | collective-permute-start | bytes 12296 | tf_op jit(solution)/shard_map/ppermute | solution.py:36
  21.2 1.8 %collective-permute-done.2.refs_1_ = f32[16,64]{1,0:T(8,128)S(1)} collective-permute-done((f32[16,64]{1,0:T(8,128)S(1)}, f32[16,64]{1,0:T(8,128)S(1)}, u32[]{:S(2)}, u32[]{:S(2)}) %collective-permute-start.2) | collective-permute-done | bytes 4128 | tf_op jit(solution)/shard_map/ppermute | solution.py:36
  23.0 0.0 collective-permute-done.6.refs_5_.refs_9_
  23.0 2.0 %shard_map.106 = (f32[256,128]{1,0:T(8,128)S(1)}, f32[256,128]{1,0:T(8,128)S(1)}, f32[4,256,128]{2,1,0:T(8,128)S(1)}, f32[256,128]{1,0:T(8,128)S(1)}) custom-call(f32[16,64]{1,0:T(8,128)S(1)} %shard_map.102.refs_0_, f32[16,64]{1,0:T(8,128)S(1)} %collective-permute-done.2.refs_1_, f32[272,128]{1,0:T(8,128)S(1)} %shard_map.104.refs_2_.refs_6_, ...), custom_call_target="tpu_custom_call" | custom-call | flops 1073741824 | bytes 524288 | tf_op jit(solution)/shard_map/pallas_call | solution.py:389
  25.1 0.1 collective-permute-start.9
  25.2 0.5 %collective-permute-start.10 = (f32[272,128]{1,0:T(8,128)S(1)}, f32[272,128]{1,0:T(8,128)S(1)}, u32[]{:S(2)}, u32[]{:S(2)}) collective-permute-start(f32[272,128]{1,0:T(8,128)S(1)} %collective-permute-done.8.refs_4_.refs_11_), channel_id=1, source_target_pairs={{0,8},{8,0},{16,24},{24,16},{1,9},{9,1},{17,25},{25,17},{2,10},{10... | collective-permute-start | bytes 417800 | tf_op jit(solution)/shard_map/ppermute | solution.py:36
  25.7 1.0 %shard_map.107 = (f32[4,256,128]{2,1,0:T(8,128)S(1)}, f32[256,128]{1,0:T(8,128)S(1)}) custom-call(f32[256,128]{1,0:T(8,128)S(1)} %get-tuple-element.40.refs_0_, f32[4,256,128]{2,1,0:T(8,128)S(1)} %get-tuple-element.42.refs_1_, f32[256,128]{1,0:T(8,128)S(1)} %get-tuple-element.43.refs_2_, f32[272,128]{1,0:T(8,128)S(1)} %collective-permute-done.7.refs_3_.refs_10_, ...), custom_call_target="tpu_custom_call" | custom-call | flops 536870912 | bytes 262144 | tf_op jit(solution)/shard_map/pallas_call | solution.py:389
  26.7 0.0 copy-start
  26.7 0.0 copy-start.1
  26.8 0.0 copy-start.2
  26.8 7.1 %shard_map.108 = (f32[72,128]{1,0:T(8,128)S(1)}, f32[72,128]{1,0:T(8,128)S(1)}, f32[72,128]{1,0:T(8,128)S(1)}, f32[72,128]{1,0:T(8,128)S(1)}) custom-call(f32[256,128]{1,0:T(8,128)S(1)} %get-tuple-element.40.refs_0_, f32[4,256,128]{2,1,0:T(8,128)S(1)} %get-tuple-element.46.refs_1_, f32[256,128]{1,0:T(8,128)S(1)} %get-tuple-element.47.refs_2_, ...), custom_call_target="tpu_custom_call" | custom-call | flops 536870912 | bytes 262144 | tf_op jit(solution)/shard_map/pallas_call | solution.py:389
  33.9 1.8 %collective-permute-start.11 = (f32[72,128]{1,0:T(8,128)S(1)}, f32[72,128]{1,0:T(8,128)S(1)}, u32[]{:S(2)}, u32[]{:S(2)}) collective-permute-start(f32[72,128]{1,0:T(8,128)S(1)} %get-tuple-element.50), channel_id=1, source_target_pairs={{0,2},{2,0},{4,6},{6,4},{1,3},{3,1},{5,7},{7,5},{8,10},{10,8},{12,... | collective-permute-start | bytes 110600 | tf_op jit(solution)/shard_map/ppermute | solution.py:36
  35.7 2.6 %collective-permute-start.12 = (f32[72,128]{1,0:T(8,128)S(1)}, f32[72,128]{1,0:T(8,128)S(1)}, u32[]{:S(2)}, u32[]{:S(2)}) collective-permute-start(f32[72,128]{1,0:T(8,128)S(1)} %get-tuple-element.51), channel_id=1, source_target_pairs={{0,4},{2,6},{4,0},{6,2},{1,5},{3,7},{5,1},{7,3},{8,12},{10,14},{12... | collective-permute-start | bytes 110600 | tf_op jit(solution)/shard_map/ppermute | solution.py:36
  38.3 3.0 %collective-permute-done.12.rest_2_ = f32[72,128]{1,0:T(8,128)S(1)} collective-permute-done((f32[72,128]{1,0:T(8,128)S(1)}, f32[72,128]{1,0:T(8,128)S(1)}, u32[]{:S(2)}, u32[]{:S(2)}) %collective-permute-start.12) | collective-permute-done | bytes 36896 | tf_op jit(solution)/shard_map/ppermute | solution.py:36
  41.3 2.7 %collective-permute-done.13.rest_3_ = f32[72,128]{1,0:T(8,128)S(1)} collective-permute-done((f32[72,128]{1,0:T(8,128)S(1)}, f32[72,128]{1,0:T(8,128)S(1)}, u32[]{:S(2)}, u32[]{:S(2)}) %collective-permute-start.13) | collective-permute-done | bytes 36896 | tf_op jit(solution)/shard_map/ppermute | solution.py:36
  44.1 1.1 %shard_map.109 = bf16[64,128]{1,0:T(8,128)(2,1)} custom-call(f32[64,128]{1,0:T(8,128)S(1)} %get-tuple-element.32.zdst_ref, f32[1,128]{1,0:T(1,128)S(1)} %bitcast.7, f32[1,128]{1,0:T(1,128)S(1)} %bitcast.5, f32[1,128]{1,0:T(1,128)S(1)} %bitcast.8, f32[72,128]{1,0:T(8,128)S(1)} %get-tuple-element.49.rest_0_, f32[72,128]{1,0:T(8,128)S(1)} %collective-permute-done.11.rest_1_, ...), custom_call_target="tpu_custom_call" | custom-call | tf_op jit(solution)/shard_map/pallas_call | solution.py:40
  (12 shorter events, 0.0 us)
Async XLA Ops:
  1.2 7.4 %collective-permute-start.5 = (f32[256,128]{1,0:T(8,128)S(1)}, f32[256,128]{1,0:T(8,128)S(1)}, u32[]{:S(2)}, u32[]{:S(2)}) collective-permute-start(f32[256,128]{1,0:T(8,128)S(1)} %get-tuple-element.38), channel_id=1, source_target_pairs={{0,1},{1,0},{2,3},{3,2},{4,5},{5,4},{6,7},{7,6},{8,9},{9,8},{10,11... | collective-permute-start | bytes 393224 | tf_op jit(solution)/shard_map/ppermute | solution.py:36
  4.2 6.3 %collective-permute-start.3 = (f32[256,128]{1,0:T(8,128)S(1)}, f32[256,128]{1,0:T(8,128)S(1)}, u32[]{:S(2)}, u32[]{:S(2)}) collective-permute-start(f32[256,128]{1,0:T(8,128)S(1)} %get-tuple-element.36), channel_id=1, source_target_pairs={{0,1},{1,0},{2,3},{3,2},{4,5},{5,4},{6,7},{7,6},{8,9},{9,8},{10,11... | collective-permute-start | bytes 393224 | tf_op jit(solution)/shard_map/ppermute | solution.py:36
  8.8 14.3 %collective-permute-start.6 = (f32[272,128]{1,0:T(8,128)S(1)}, f32[272,128]{1,0:T(8,128)S(1)}, u32[]{:S(2)}, u32[]{:S(2)}) collective-permute-start(f32[272,128]{1,0:T(8,128)S(1)} %shard_map.105.refs_4_.refs_8_), channel_id=1, source_target_pairs={{0,8},{8,0},{16,24},{24,16},{1,9},{9,1},{17,25},{25,17},{2,10},{10... | collective-permute-start | bytes 417800 | tf_op jit(solution)/shard_map/ppermute | solution.py:36
  10.7 12.3 %collective-permute-start.4 = (f32[272,128]{1,0:T(8,128)S(1)}, f32[272,128]{1,0:T(8,128)S(1)}, u32[]{:S(2)}, u32[]{:S(2)}) collective-permute-start(f32[272,128]{1,0:T(8,128)S(1)} %shard_map.104.refs_2_.refs_6_), channel_id=1, source_target_pairs={{0,8},{8,0},{16,24},{24,16},{1,9},{9,1},{17,25},{25,17},{2,10},{10... | collective-permute-start | bytes 417800 | tf_op jit(solution)/shard_map/ppermute | solution.py:36
  10.7 4.0 %collective-permute-start = (f32[64,128]{1,0:T(8,128)S(1)}, f32[64,128]{1,0:T(8,128)S(1)}, u32[]{:S(2)}, u32[]{:S(2)}) collective-permute-start(f32[64,128]{1,0:T(8,128)S(1)} %get-tuple-element.31), channel_id=1, source_target_pairs={{0,1},{1,0},{2,3},{3,2},{4,5},{5,4},{6,7},{7,6},{8,9},{9,8},{10,11... | collective-permute-start | bytes 98312 | tf_op jit(solution)/shard_map/ppermute | solution.py:36
  12.5 12.6 %collective-permute-start.8 = (f32[272,128]{1,0:T(8,128)S(1)}, f32[272,128]{1,0:T(8,128)S(1)}, u32[]{:S(2)}, u32[]{:S(2)}) collective-permute-start(f32[272,128]{1,0:T(8,128)S(1)} %shard_map.105.refs_4_.refs_8_), channel_id=1, source_target_pairs={{0,16},{8,24},{16,0},{24,8},{1,17},{9,25},{17,1},{25,9},{2,18},{10... | collective-permute-start | bytes 417800 | tf_op jit(solution)/shard_map/ppermute | solution.py:36
  14.0 11.1 %collective-permute-start.7 = (f32[272,128]{1,0:T(8,128)S(1)}, f32[272,128]{1,0:T(8,128)S(1)}, u32[]{:S(2)}, u32[]{:S(2)}) collective-permute-start(f32[272,128]{1,0:T(8,128)S(1)} %shard_map.104.refs_2_.refs_6_), channel_id=1, source_target_pairs={{0,16},{8,24},{16,0},{24,8},{1,17},{9,25},{17,1},{25,9},{2,18},{10... | collective-permute-start | bytes 417800 | tf_op jit(solution)/shard_map/ppermute | solution.py:36
  14.8 4.5 %collective-permute-start.1 = (f32[8,64]{1,0:T(8,128)S(1)}, f32[8,64]{1,0:T(8,128)S(1)}, u32[]{:S(2)}, u32[]{:S(2)}) collective-permute-start(f32[8,64]{1,0:T(8,128)S(1)} %get-tuple-element.33.low_ref), channel_id=1, source_target_pairs={{0,4},{2,6},{4,0},{6,2},{1,5},{3,7},{5,1},{7,3},{8,12},{10,14},{12... | collective-permute-start | bytes 6152 | tf_op jit(solution)/shard_map/ppermute | solution.py:36
  19.4 3.7 %collective-permute-start.2 = (f32[16,64]{1,0:T(8,128)S(1)}, f32[16,64]{1,0:T(8,128)S(1)}, u32[]{:S(2)}, u32[]{:S(2)}) collective-permute-start(f32[16,64]{1,0:T(8,128)S(1)} %shard_map.102.refs_0_), channel_id=1, source_target_pairs={{0,2},{2,0},{4,6},{6,4},{1,3},{3,1},{5,7},{7,5},{8,10},{10,8},{12,... | collective-permute-start | bytes 12296 | tf_op jit(solution)/shard_map/ppermute | solution.py:36
  25.1 1.6 %collective-permute-start.9 = (f32[272,128]{1,0:T(8,128)S(1)}, f32[272,128]{1,0:T(8,128)S(1)}, u32[]{:S(2)}, u32[]{:S(2)}) collective-permute-start(f32[272,128]{1,0:T(8,128)S(1)} %collective-permute-done.7.refs_3_.refs_10_), channel_id=1, source_target_pairs={{0,8},{8,0},{16,24},{24,16},{1,9},{9,1},{17,25},{25,17},{2,10},{10... | collective-permute-start | bytes 417800 | tf_op jit(solution)/shard_map/ppermute | solution.py:36
  25.2 1.6 %collective-permute-start.10 = (f32[272,128]{1,0:T(8,128)S(1)}, f32[272,128]{1,0:T(8,128)S(1)}, u32[]{:S(2)}, u32[]{:S(2)}) collective-permute-start(f32[272,128]{1,0:T(8,128)S(1)} %collective-permute-done.8.refs_4_.refs_11_), channel_id=1, source_target_pairs={{0,8},{8,0},{16,24},{24,16},{1,9},{9,1},{17,25},{25,17},{2,10},{10... | collective-permute-start | bytes 417800 | tf_op jit(solution)/shard_map/ppermute | solution.py:36
  26.7 17.3 %copy-start = (f32[128]{0:T(128)S(1)}, f32[128]{0:T(128)}, u32[]{:S(2)}) copy-start(f32[128]{0:T(128)} %param.14) | copy-start | bytes 1540
  26.7 17.3 %copy-start.1 = (f32[128]{0:T(128)S(1)}, f32[128]{0:T(128)}, u32[]{:S(2)}) copy-start(f32[128]{0:T(128)} %param.13) | copy-start | bytes 1540
  26.8 17.3 %copy-start.2 = (f32[128]{0:T(128)S(1)}, f32[128]{0:T(128)}, u32[]{:S(2)}) copy-start(f32[128]{0:T(128)} %param.15) | copy-start | bytes 1540
  33.9 4.4 %collective-permute-start.11 = (f32[72,128]{1,0:T(8,128)S(1)}, f32[72,128]{1,0:T(8,128)S(1)}, u32[]{:S(2)}, u32[]{:S(2)}) collective-permute-start(f32[72,128]{1,0:T(8,128)S(1)} %get-tuple-element.50), channel_id=1, source_target_pairs={{0,2},{2,0},{4,6},{6,4},{1,3},{3,1},{5,7},{7,5},{8,10},{10,8},{12,... | collective-permute-start | bytes 110600 | tf_op jit(solution)/shard_map/ppermute | solution.py:36
  35.7 5.6 %collective-permute-start.12 = (f32[72,128]{1,0:T(8,128)S(1)}, f32[72,128]{1,0:T(8,128)S(1)}, u32[]{:S(2)}, u32[]{:S(2)}) collective-permute-start(f32[72,128]{1,0:T(8,128)S(1)} %get-tuple-element.51), channel_id=1, source_target_pairs={{0,4},{2,6},{4,0},{6,2},{1,5},{3,7},{5,1},{7,3},{8,12},{10,14},{12... | collective-permute-start | bytes 110600 | tf_op jit(solution)/shard_map/ppermute | solution.py:36
  38.3 5.8 %collective-permute-start.13 = (f32[72,128]{1,0:T(8,128)S(1)}, f32[72,128]{1,0:T(8,128)S(1)}, u32[]{:S(2)}, u32[]{:S(2)}) collective-permute-start(f32[72,128]{1,0:T(8,128)S(1)} %get-tuple-element.52), channel_id=1, source_target_pairs={{0,6},{2,4},{4,2},{6,0},{1,7},{3,5},{5,3},{7,1},{8,14},{10,12},{12... | collective-permute-start | bytes 110600 | tf_op jit(solution)/shard_map/ppermute | solution.py:36
